TPU v7x, 32 devices: a whole 2x2x4 slice. The times are simulated.
32 devices in a mesh: view: 4 (over z), brick: 8 (over y, x, core).
Axes of the slice: x: 2, y: 2, z: 4, core: 2. Of those that a mesh axis runs over, the one named last changes fastest.
Arguments:
- estimate: float32 [16, 16, 64, 256], P('brick'), may hold values from 0.5 to 2
- views_data: bfloat16 [4, 8, 112, 32, 128], P('view', 'brick'), may hold values from 0.5 to 2
- psf_taps: float32 [4, 3, 31], P('view'), may hold values from 0.02 to 1
- seg_owner: int32 [4, 8, 32, 1], P('view', 'brick'), may hold values from 0 to 7; in each aligned block of 32 rows (0 to 31, 32 to 63, ..., all dimensions but the last counted through in order) at most 8 rows name the same one
- seg_local: int32 [4, 8, 32], P('view', 'brick'), may hold values from 0 to 1
- seg_offset: int32 [4, 8, 32], P('view', 'brick'), may hold values from 0 to 12
- seg_extent: int32 [4, 8, 32], P('view', 'brick'), may hold values from 1 to 4, 112 in all within a row
- view_shift: int32 [4, 2], P('view'), may hold values from 0 to 32
Outputs:
- joined: float32 [16, 16, 64, 256], P('brick')
Inputs may be any that keep to these rules, and one draw needn't show every extreme that they name: `seg_owner`: within one tile's 32 segments no owner is named more than 8 times, and in every draw some tile names one owner exactly 8 times. `seg_extent`: the 32 extents of a tile sum to 112, and some extent is exactly 4.
All inputs are finite; a program needn't handle non-finite values.
Results may differ from a plain program's by a relative error of at most 0.0003.
Values may be sent and summed in bfloat16 or wider, within the bound.
No kernel may reach another device: no remote copies, remote signals or barrier semaphores. Data moves between devices by JAX's collectives and lax.ppermute only.
A program may use at most 128 MiB of HBM per device.

v0:
```python
import jax
import jax.numpy as jnp
from jax import lax
from jax.sharding import PartitionSpec as P

ITERS = 2
EXTMAX = 4


def blur_matrix(tap_values, length):
    centre = tap_values.shape[0] // 2
    positions = jnp.arange(length, dtype=jnp.int32)
    offsets_tab = positions[:, None] - positions[None, :] + centre
    match_table = (
        offsets_tab[:, :, None] == jnp.arange(tap_values.shape[0], dtype=jnp.int32)[None, None, :]
    ).astype(tap_values.dtype)
    return jnp.sum(match_table * tap_values[None, None, :], axis=-1)


def apply_blur(volume, matrices):
    along_z, along_y, along_x = matrices
    highest = lax.Precision.HIGHEST
    volume = jnp.einsum("...xyz,zw->...xyw", volume, along_z, precision=highest)
    volume = jnp.einsum("...xyz,yw->...xwz", volume, along_y, precision=highest)
    volume = jnp.einsum("...xyz,xw->...wyz", volume, along_x, precision=highest)
    return volume


def view_matrices(view_taps, tile_x, tile_y, tile_z):
    normed = view_taps / jnp.sum(view_taps, axis=1, keepdims=True)
    forward = (
        blur_matrix(normed[2], tile_z),
        blur_matrix(normed[1], tile_y),
        blur_matrix(normed[0], tile_x),
    )
    backward = (forward[0].T, forward[1].T, forward[2].T)
    return (forward, backward)


def slot_ranks(owners):
    positions = jnp.arange(owners.shape[-1], dtype=jnp.int32)
    same_owner = owners[..., :, None] == owners[..., None, :]
    earlier = positions[None, :] < positions[:, None]
    return jnp.sum((same_owner & earlier).astype(jnp.int32), axis=-1)


def on_device(
    estimate, views_data, psf_taps, seg_owner, seg_local, seg_offset, seg_extent, view_shift
):
    per_owner, brick_x, brick_y, brick_z = estimate.shape
    tile_x, tile_y, tile_z = (views_data.shape[2], views_data.shape[3], views_data.shape[4])
    seg_count = seg_extent.shape[2]
    brick_count = lax.axis_size("brick")
    owner_me = lax.axis_index("brick")
    capacity = max(2, 2 * seg_count // brick_count)
    slot_rows = capacity * EXTMAX
    own_rows = per_owner * brick_x
    forward, backward = view_matrices(psf_taps[0], tile_x, tile_y, tile_z)
    shift_y = view_shift[0, 0]
    shift_z = view_shift[0, 1]
    measured = views_data[0, 0].astype(jnp.float32)
    lists = (
        lax.all_gather(seg_owner[:, :, :, 0], "brick", axis=1, tiled=True),
        lax.all_gather(seg_local, "brick", axis=1, tiled=True),
        lax.all_gather(seg_offset, "brick", axis=1, tiled=True),
        lax.all_gather(seg_extent, "brick", axis=1, tiled=True),
    )
    all_owner, all_local, all_offset, all_extent = (
        lists[0][0],
        lists[1][0],
        lists[2][0],
        lists[3][0],
    )
    own_owner = seg_owner[0, 0, :, 0]
    own_local = seg_local[0, 0]
    own_offset = seg_offset[0, 0]
    own_extent = seg_extent[0, 0]
    own_rank = slot_ranks(own_owner)
    seg_ids = jnp.arange(seg_count, dtype=jnp.int32)
    peer_ids = jnp.arange(brick_count, dtype=jnp.int32)
    slot_ids = jnp.arange(capacity, dtype=jnp.int32)
    row_steps = jnp.arange(EXTMAX, dtype=jnp.int32)
    starts = jnp.cumsum(own_extent) - own_extent
    tile_rows = jnp.arange(tile_x, dtype=jnp.int32)
    seg_of = jnp.sum((starts[None, :] <= tile_rows[:, None]).astype(jnp.int32), axis=1) - 1
    within = tile_rows - starts[seg_of]
    source_of_row = (
        (own_owner[seg_of] * per_owner + own_local[seg_of]) * brick_x + own_offset[seg_of] + within
    )
    back_match = (own_owner[None, None, :] == peer_ids[:, None, None]) & (
        own_rank[None, None, :] == slot_ids[None, :, None]
    )
    back_valid = jnp.any(back_match, axis=-1)
    back_seg = jnp.sum(back_match.astype(jnp.int32) * seg_ids, axis=-1)
    back_mask = back_valid[:, :, None] & (
        row_steps[None, None, :] < own_extent[back_seg][:, :, None]
    )
    back_rows = jnp.where(
        back_mask, starts[back_seg][:, :, None] + row_steps[None, None, :], 0
    ).reshape(-1)
    back_mask = back_mask.reshape(-1)
    all_rank = slot_ranks(all_owner)
    owner_match = (all_owner[:, None, :] == owner_me) & (
        all_rank[:, None, :] == slot_ids[None, :, None]
    )
    owner_valid = jnp.any(owner_match, axis=-1)
    owner_seg = jnp.sum(owner_match.astype(jnp.int32) * seg_ids, axis=-1)
    owner_base = jnp.take_along_axis(all_local, owner_seg, axis=1) * brick_x + jnp.take_along_axis(
        all_offset, owner_seg, axis=1
    )
    owner_ext = jnp.take_along_axis(all_extent, owner_seg, axis=1)
    owner_mask = owner_valid[:, :, None] & (row_steps[None, None, :] < owner_ext[:, :, None])
    owner_rows = jnp.where(
        owner_mask, owner_base[:, :, None] + row_steps[None, None, :], 0
    ).reshape(-1)
    owner_mask = owner_mask.reshape(-1)
    landing = (
        (owner_rows[None, :] == jnp.arange(own_rows, dtype=jnp.int32)[:, None])
        & owner_mask[None, :]
    ).astype(jnp.float32)

    def to_owners(projected):
        outgoing = jnp.where(back_mask[:, None, None], jnp.take(projected, back_rows, axis=0), 0.0)
        outgoing = outgoing.reshape(brick_count, slot_rows, tile_y, tile_z)
        arrived = lax.all_to_all(
            outgoing, "brick", split_axis=0, concat_axis=0, tiled=True
        ).reshape(-1, tile_y, tile_z)
        accumulated = jnp.einsum("pq,qyz->pyz", landing, arrived, precision=lax.Precision.HIGHEST)
        brick_part = lax.dynamic_update_slice(
            jnp.zeros((own_rows, brick_y, brick_z), jnp.float32), accumulated, (0, shift_y, shift_z)
        )
        brick_part = brick_part.reshape(per_owner, brick_x, brick_y, brick_z)
        return lax.psum(brick_part, "view")

    weight = to_owners(apply_blur(jnp.ones((tile_x, tile_y, tile_z), jnp.float32), backward))
    current = estimate
    for sweep in range(ITERS):
        flat_est = current.reshape(own_rows, brick_y, brick_z)
        cropped = lax.dynamic_slice(
            flat_est, (0, shift_y, shift_z), (own_rows, tile_y, tile_z)
        ).astype(jnp.bfloat16)
        gathered = lax.all_gather(cropped, "brick", axis=0, tiled=True)
        view_tile = jnp.take(gathered, source_of_row, axis=0)
        correction_view_tile = view_tile.astype(jnp.float32)
        quotient = measured / apply_blur(correction_view_tile, forward)
        correction = to_owners(apply_blur(quotient, backward))
        current = current * (1.0 + correction) / (1.0 + weight)
    return current


def solution(mesh):
    placed = (
        P("brick", None, None, None),
        P("view", "brick", None, None, None),
        P("view", None, None),
        P("view", "brick", None, None),
        P("view", "brick", None),
        P("view", "brick", None),
        P("view", "brick", None),
        P("view", None),
    )
    return jax.shard_map(
        on_device,
        mesh=mesh,
        in_specs=placed,
        out_specs=P("brick", None, None, None),
        check_vma=False,
    )
```

profile of v0, /device:TPU:0, one launch (start us, length us, event | category | flops | bytes accessed | tf_op | source)
XLA Modules:
  0.0 638.7 jit_solution(17363092485871562912)
XLA Ops:
  31.5 3.0 gather_fusion.11
  34.6 10.2 %all-gather.4.cloned.1.call-done = bf16[256,32,128]{2,1,0:T(8,128)(2,1)} async-done(((bf16[32,32,128]{2,1,0:T(8,128)(2,1)}), bf16[256,32,128]{2,1,0:T(8,128)(2,1)}) %all-gather.4.cloned.1.call-update) | async-done | bytes 2097168 | tf_op jit(solution)/shard_map/all_gather | solution.py:142
  49.8 3.1 convert_divide_fusion.1
  59.9 3.0 gather_fusion.10
  62.8 16.0 %select_select_fusion.1 = (f32[256,32,128]{2,1,0:T(8,128)S(1)}, f32[256,32,128]{2,1,0:T(8,128)}) fusion(f32[256,32,128]{2,1,0:T(8,128)} %gather_fusion.11, pred[256]{0:T(512)(128)(4,1)S(1)} %get-tuple-element.12, pred[256]{0:T(512)(128)(4,1)S(1)} %and.102, f32[256,32,128]{2,1,0:T(8,128)} %gather_fusion.10), kind=kLoop, calls=%fused_computation.15 | loop fusion | flops 4194304 | bytes 16777728 | tf_op jit(solution)/shard_map/jit(_where)/select_n | solution.py:123
  78.8 4.3 copy.69
  83.2 4.5 all-to-all-start.1
  87.7 6.5 %copy.64 = f32[8,32,32,128]{3,1,2,0:T(8,128)} copy(f32[8,32,32,128]{3,2,1,0:T(8,128)} %bitcast.133) | data formatting | bytes 8388608 | tf_op jit(solution)/shard_map/reshape | solution.py:124
  94.3 42.6 %all-to-all-done.1 = f32[8,32,32,128]{3,1,2,0:T(8,128)} async-done(((f32[8,32,32,128]{3,1,2,0:T(8,128)}), f32[8,32,32,128]{3,1,2,0:T(8,128)}, u32[]{:S(2)}, u32[]{:S(2)}) %all-to-all-start.1) | async-done | bytes 4194336 | tf_op jit(solution)/shard_map/all_to_all | solution.py:125
  136.8 4.6 all-to-all-start
  141.5 52.0 %all-gather = s32[1,8,32,1]{2,3,0,1:T(1,128)S(1)} all-gather(s32[1,1,32,1]{2,3,0,1:T(1,128)S(1)} %bitcast.124), channel_id=2, replica_groups=mesh['view'=4,'brick'=8] {'brick'}, dimensions={1}, use_global_device_ids=true | all-gather | bytes 1152 | tf_op jit(solution)/shard_map/all_gather | solution.py:63
  194.1 7.9 %all_gather.20 = s32[1,8,32]{2,0,1:T(1,128)S(1)} all-gather(s32[1,1,32]{2,0,1:T(1,128)S(1)} %bitcast.126), channel_id=1, replica_groups=mesh['view'=4,'brick'=8] {'brick'}, dimensions={1}, use_global_device_ids=true | all-gather | bytes 1152 | tf_op jit(solution)/shard_map/all_gather | solution.py:64
  202.8 8.7 %all_gather.21 = s32[1,8,32]{2,0,1:T(1,128)S(1)} all-gather(s32[1,1,32]{2,0,1:T(1,128)S(1)} %bitcast.128), channel_id=1, replica_groups=mesh['view'=4,'brick'=8] {'brick'}, dimensions={1}, use_global_device_ids=true | all-gather | bytes 1152 | tf_op jit(solution)/shard_map/all_gather | solution.py:65
  212.3 7.9 %all_gather.19 = s32[1,8,32]{2,0,1:T(1,128)S(1)} all-gather(s32[1,1,32]{2,0,1:T(1,128)S(1)} %bitcast.117), channel_id=1, replica_groups=mesh['view'=4,'brick'=8] {'brick'}, dimensions={1}, use_global_device_ids=true | all-gather | bytes 1152 | tf_op jit(solution)/shard_map/all_gather | solution.py:66
  231.5 13.3 %dynamic_update_slice.10 = f32[32,64,256]{2,1,0:T(8,128)S(1)} dynamic-update-slice(f32[32,64,256]{2,1,0:T(8,128)S(1)} %broadcast.183.clone.1, f32[32,32,128]{2,1,0:T(8,128)S(1)} %copy.71, s32[]{:T(128)} %constant.39.clone.1, s32[]{:T(128)S(6)} %select_n.82, s32[]{:T(128)S(6)} %select_n.83) | dynamic-update-slice | bytes 1048580 | tf_op jit(solution)/shard_map/dynamic_update_slice | solution.py:129
  246.5 13.9 %dynamic_update_slice.9 = f32[32,64,256]{2,1,0:T(8,128)} dynamic-update-slice(f32[32,64,256]{2,1,0:T(8,128)} %broadcast.183.clone, f32[32,32,128]{2,1,0:T(8,128)S(1)} %copy.66, s32[]{:T(128)} %constant.39.clone.1, s32[]{:T(128)S(6)} %select_n.82, s32[]{:T(128)S(6)} %select_n.83) | dynamic-update-slice | bytes 1048580 | tf_op jit(solution)/shard_map/dynamic_update_slice | solution.py:129
  260.5 155.0 %all-reduce.6.cloned.1.call-done = (f32[2,16,64,256]{3,2,1,0:T(8,128)}, f32[2,16,64,256]{3,2,1,0:T(8,128)}) async-done(((f32[2,16,64,256]{3,2,1,0:T(8,128)}, f32[2,16,64,256]{3,2,1,0:T(8,128)}), (f32[2,16,64,256]{3,2,1,0:T(8,128)}, f32[2,16,64,256]{3,2,1,0:T(8,128)})) %all-reduce.6.cloned.1.call-update) | async-done | bytes 4194320 | tf_op jit(solution)/shard_map/psum | solution.py:133
  415.5 3.5 multiply_divide_fusion.1
  421.5 26.7 %all-gather.6.cloned.1.call-done = bf16[256,32,128]{2,1,0:T(8,128)(2,1)} async-done(((bf16[32,32,128]{2,1,0:T(8,128)(2,1)}), bf16[256,32,128]{2,1,0:T(8,128)(2,1)}) %all-gather.6.cloned.1.call-update) | async-done | bytes 2097168 | tf_op jit(solution)/shard_map/all_gather | solution.py:142
  466.2 3.8 select_select_fusion
  472.3 51.6 %all_to_all.15 = f32[8,32,32,128]{3,1,2,0:T(8,128)S(1)} all-to-all(f32[8,32,32,128]{3,1,2,0:T(8,128)S(1)} %copy.78), channel_id=1, replica_groups=mesh['view'=4,'brick'=8] {'brick'}, dimensions={0} | all-to-all | bytes 8388608 | tf_op jit(solution)/shard_map/all_to_all | solution.py:125
  528.1 14.0 %dynamic_update_slice.11 = f32[32,64,256]{2,1,0:T(8,128)} dynamic-update-slice(f32[32,64,256]{2,1,0:T(8,128)} %broadcast.183, f32[32,32,128]{2,1,0:T(8,128)S(1)} %copy.80, s32[]{:T(128)} %constant.39.clone.1, s32[]{:T(128)S(6)} %select_n.82, s32[]{:T(128)S(6)} %select_n.83) | dynamic-update-slice | bytes 1048580 | tf_op jit(solution)/shard_map/dynamic_update_slice | solution.py:129
  542.1 85.4 %all-reduce.4.cloned.1.call-done = f32[2,16,64,256]{3,2,1,0:T(8,128)} async-done(((f32[2,16,64,256]{3,2,1,0:T(8,128)}), f32[2,16,64,256]{3,2,1,0:T(8,128)}) %all-reduce.4.cloned.1.call-update) | async-done | bytes 2097168 | tf_op jit(solution)/shard_map/psum | solution.py:133
  627.5 4.2 multiply_divide_fusion
  (125 shorter events, 74.9 us)
Async XLA Ops:
  6.5 12.1 %copy-start.1 = (s32[1,1,32,1]{2,3,1,0:T(1,128)S(1)}, s32[1,1,32,1]{2,3,1,0:T(1,128)}, u32[]{:S(2)}) copy-start(s32[1,1,32,1]{2,3,1,0:T(1,128)} %param.17) | copy-start | bytes 388
  6.5 12.3 %copy-start.2 = (s32[1,1,32]{2,1,0:T(1,128)S(1)}, s32[1,1,32]{2,1,0:T(1,128)}, u32[]{:S(2)}) copy-start(s32[1,1,32]{2,1,0:T(1,128)} %param.18) | copy-start | bytes 388
  6.5 13.5 %copy-start.3 = (s32[1,1,32]{2,1,0:T(1,128)S(1)}, s32[1,1,32]{2,1,0:T(1,128)}, u32[]{:S(2)}) copy-start(s32[1,1,32]{2,1,0:T(1,128)} %param.19) | copy-start | bytes 388
  6.5 38.2 %all-gather.4.cloned.1.call-start = ((), (), s32[]{:S(2)}) async-start(), calls=%async_computation.3 | async-start | bytes 2359296 | tf_op jit(solution)/shard_map/all_gather | solution.py:142
  21.6 0.8 copy-start
  22.4 1.6 copy-start.7
  48.1 1.7 copy-start.8
  83.2 53.6 %all-to-all-start.1 = ((f32[8,32,32,128]{3,1,2,0:T(8,128)}), f32[8,32,32,128]{3,1,2,0:T(8,128)}, u32[]{:S(2)}, u32[]{:S(2)}) async-start(f32[8,32,32,128]{3,1,2,0:T(8,128)} %copy.69), calls=%async_computation.1 | async-start | bytes 8388608 | tf_op jit(solution)/shard_map/all_to_all | solution.py:125
  136.8 89.6 %all-to-all-start = ((f32[8,32,32,128]{3,1,2,0:T(8,128)}), f32[8,32,32,128]{3,1,2,0:T(8,128)}, u32[]{:S(2)}, u32[]{:S(2)}) async-start(f32[8,32,32,128]{3,1,2,0:T(8,128)} %copy.64), calls=%async_computation | async-start | bytes 8388608 | tf_op jit(solution)/shard_map/all_to_all | solution.py:125
  141.4 274.1 %all-reduce.6.cloned.1.call-start = ((), (), s32[]{:S(2)}) async-start(), calls=%async_computation.6 | async-start | bytes 8388608 | tf_op jit(solution)/shard_map/psum | solution.py:133
  244.8 15.6 %copy-start.6 = (f32[32,64,256]{2,1,0:T(8,128)}, f32[32,64,256]{2,1,0:T(8,128)S(1)}, u32[]{:S(2)}) copy-start(f32[32,64,256]{2,1,0:T(8,128)S(1)} %dynamic_update_slice.10) | copy-start | bytes 6291460
  260.4 187.7 %all-gather.6.cloned.1.call-start = ((), (), s32[]{:S(2)}) async-start(), calls=%async_computation.4 | async-start | bytes 2359296 | tf_op jit(solution)/shard_map/all_gather | solution.py:142
  418.9 1.3 copy-start.4
  421.2 206.3 %all-reduce.4.cloned.1.call-start = ((), (), s32[]{:S(2)}) async-start(), calls=%async_computation.5 | async-start | bytes 4194304 | tf_op jit(solution)/shard_map/psum | solution.py:133
  451.4 1.7 copy-start.9
  528.1 99.4 %copy-start.5 = (f32[2,16,64,256]{3,2,1,0:T(8,128)S(1)}, f32[2,16,64,256]{3,2,1,0:T(8,128)}, u32[]{:S(2)}) copy-start(f32[2,16,64,256]{3,2,1,0:T(8,128)} %copy-done.4) | copy-start | bytes 6291460
Sparse Core Ops, SparseCore 0:
  14.2 30.5 all-gather.3
  260.5 154.8 all-reduce.5
  421.3 26.7 all-gather.5
  542.2 85.2 all-reduce.3
where the time goes:
time: 648 us; the launch traced here: 639 us
  waiting for transfers between devices  320 us (49%)
  blocking collectives  128 us (20%)
  local copies, waits for them, and re-layouts  97.1 us (15%)
  matrix products  35 us (5%)
  other arithmetic  31.1 us (5%)
  between operations  18.1 us (3%)
  starting transfers between devices  9.48 us (1%)
    psum x2, waiting for transfers between devices, to_owners(): return lax.psum(brick_part, 'view')  240 us
    all_gather x1, blocking collectives, on_device(): lax.all_gather(seg_owner[:, :, :, 0], 'brick', axis=1, tiled=True)  52 us
    all_to_all x1, blocking collectives, to_owners(): lax.all_to_all(outgoing, 'brick', split_axis=0, concat_axis=0, tiled=True)  51.6 us
    all_to_all x2, waiting for transfers between devices, to_owners(): lax.all_to_all(outgoing, 'brick', split_axis=0, concat_axis=0, tiled=True)  42.6 us
    dynamic_update_slice x3, local copies, waits for them, and re-layouts, to_owners(): lax.dynamic_update_slice(jnp.zeros((own_rows, brick_y, brick_z), jnp.floa...  41.2 us
    all_gather x2, waiting for transfers between devices, on_device(): gathered = lax.all_gather(cropped, 'brick', axis=0, tiled=True)  36.9 us
    select_n x2, other arithmetic, to_owners(): jnp.where(back_mask[:, None, None], jnp.take(projected, back_rows, axis=0...  19.7 us
    dot_general x5, matrix products, apply_blur(): volume = jnp.einsum('...xyz,xw->...wyz', volume, along_x, precision=highest)  14.2 us
  transfers between devices with their start and end apart: 6, of which 5 were waited for; matrix products, arithmetic and copies ran while one was open for 6% of the time, Pallas kernels for 0%

commit v1 on v0

v1 whole, which is shorter than its diff:
```python
import jax
import jax.numpy as jnp
from jax import lax
from jax.experimental import pallas as pl
from jax.experimental.pallas import tpu as pltpu
from jax.sharding import PartitionSpec as P

ITERS = 2
WIRE = jnp.float32
F32 = jnp.float32
BF16 = jnp.bfloat16


def split(x):
    hi = x.astype(BF16)
    return hi, (x - hi.astype(F32)).astype(BF16)


def split_outside(x):
    hi = lax.reduce_precision(x, 8, 7)
    return hi.astype(BF16), lax.reduce_precision(x - hi, 8, 7).astype(BF16)


def dot(a, b):
    return lax.dot_general(a, b, (((1,), (0,)), ((), ())), preferred_element_type=F32)


def band(taps, rows, cols):
    count = taps.shape[0]
    index = rows[:, None] - cols[None, :] + count // 2
    hit = index[:, :, None] == jnp.arange(count, dtype=jnp.int32)
    return jnp.sum(jnp.where(hit, taps, 0.0), axis=-1)


def crop_rows(value, shift_y, shift_z, tile_y, tile_z, stage):
    brick_z = value.shape[1]
    turned = pltpu.roll(value, lax.rem(brick_z - shift_z, brick_z), 1)
    stage[...] = turned[:, :tile_z]
    return stage[pl.ds(shift_y, tile_y), :]


def first_crop(shifts, estimate, tile_y, tile_z):
    rows, brick_y, brick_z = estimate.shape

    def kernel(shift_ref, est_ref, out_ref, stage, crops):
        def step(r, carry):
            crops[pl.ds(r, tile_y, stride=rows), :] = crop_rows(
                est_ref[r], shift_ref[0], shift_ref[1], tile_y, tile_z, stage
            )
            return carry

        lax.fori_loop(0, rows, step, 0, unroll=4)
        out_ref[...] = crops[...].astype(BF16).reshape(tile_y, rows, tile_z)

    return pl.pallas_call(
        kernel,
        out_shape=jax.ShapeDtypeStruct((tile_y, rows, tile_z), BF16),
        in_specs=[
            pl.BlockSpec(memory_space=pltpu.SMEM),
            pl.BlockSpec(memory_space=pltpu.VMEM),
        ],
        out_specs=pl.BlockSpec(memory_space=pltpu.VMEM),
        scratch_shapes=[
            pltpu.VMEM((brick_y, tile_z), F32),
            pltpu.VMEM((tile_y * rows, tile_z), F32),
        ],
        name="first_crop",
    )(shifts, estimate)


def read_tile(pieces, measured, gather_mat, scatter_mat, z_mat, y_mat, slots, with_weight):
    owners = len(pieces)
    half, rows, tile_z = pieces[0][0].shape
    tile_y = 2 * half
    tile_x = measured.shape[0] // tile_y
    flat = [p for pair in pieces for p in pair]
    n_send = owners // 2
    group = y_mat.shape[1] // 2
    per_group = group // tile_y
    groups = tile_x // per_group
    extra = (1 if with_weight else 0, 0)

    def kernel(*refs):
        g_refs = refs[: 2 * owners]
        m_ref, gm_ref, sm_ref, zm_ref, ym_ref = refs[2 * owners : 2 * owners + 5]
        outs = refs[2 * owners + 5 : 2 * owners + 9]
        buf = refs[2 * owners + 9]
        for h in range(2):
            parts = [g_refs[2 * k + h] for k in range(owners)]

            def gather(i, carry):
                y = i * 2
                both = jnp.concatenate(
                    [
                        jnp.concatenate([p[y], p[y + 1]], axis=1)
                        for p in parts
                    ],
                    axis=0,
                )
                got = dot(gm_ref[...], both)
                got = got[:tile_x] + got[tile_x:]
                stacked = jnp.concatenate([got[:, :tile_z], got[:, tile_z:]], axis=0)
                hi, lo = split(stacked)
                out = dot(jnp.concatenate([hi, lo], axis=1), zm_ref[...])
                out = out[:, :tile_z] + out[:, tile_z:]
                buf[pl.ds(h * half + y, tile_x, stride=tile_y), :] = out[:tile_x]
                buf[pl.ds(h * half + y + 1, tile_x, stride=tile_y), :] = out[tile_x:]
                return carry

            lax.fori_loop(0, half // 2, gather, 0, unroll=2)

        def divide(i, carry):
            at = pl.multiple_of(i * 2 * group, 2 * group)
            first = buf[pl.ds(at, group), :]
            second = buf[pl.ds(at + group, group), :]
            hi, lo = split(jnp.concatenate([first, second], axis=1))
            out = dot(ym_ref[...], jnp.concatenate([hi, lo], axis=0))
            out = out[:group] + out[group:]
            data = m_ref[pl.ds(at, 2 * group), :].astype(F32)
            buf[pl.ds(at, group), :] = data[:group] / out[:, :tile_z]
            buf[pl.ds(at + group, group), :] = data[group:] / out[:, tile_z:]
            return carry

        lax.fori_loop(0, groups // 2, divide, 0, unroll=2)

        for h in range(2):
            send_ref, keep_ref = outs[2 * h], outs[2 * h + 1]

            def put(y, sums, send_ref=send_ref, keep_ref=keep_ref, h=h):
                for k in range(owners):
                    block = sums[k * rows : (k + 1) * rows]
                    slot = slots[h][k]
                    if slot < n_send:
                        send_ref[slot, y] = block.astype(send_ref.dtype)
                    else:
                        keep_ref[slot - n_send, y] = block

            def scatter(i, carry, h=h, put=put):
                y = i * 2
                first = buf[pl.ds(h * half + y, tile_x, stride=tile_y), :]
                second = buf[pl.ds(h * half + y + 1, tile_x, stride=tile_y), :]
                hi, lo = split(jnp.concatenate([first, second], axis=1))
                out = dot(sm_ref[...], jnp.concatenate([hi, lo], axis=0))
                out = out[: owners * rows] + out[owners * rows :]
                put(y, out[:, :tile_z])
                put(y + 1, out[:, tile_z:])
                return carry

            lax.fori_loop(0, half // 2, scatter, 0, unroll=2)
            if extra[h]:
                ones = jnp.ones((tile_x, tile_z), BF16)
                out = dot(sm_ref[:, :tile_x], ones)
                put(half, out[: owners * rows] + out[owners * rows :])

    vmem = pl.BlockSpec(memory_space=pltpu.VMEM)
    shapes = []
    for h in range(2):
        for dtype in (WIRE, F32):
            shapes.append(jax.ShapeDtypeStruct((n_send, half + extra[h], rows, tile_z), dtype))
    return pl.pallas_call(
        kernel,
        out_shape=tuple(shapes),
        in_specs=[vmem] * (2 * owners + 5),
        out_specs=(vmem,) * 4,
        scratch_shapes=[pltpu.VMEM((tile_x * tile_y, tile_z), F32)],
        name="read_tile",
    )(*flat, measured, gather_mat, scatter_mat, z_mat, y_mat)


def update(scalars, sums, estimate, z_place, y_place, outline, row_weight, tile_y, tile_z, last):
    views = len(sums)
    rows, brick_y, brick_z = estimate.shape
    half = tile_y // 2
    flat = [p for pair in sums for p in pair]

    def kernel(*refs):
        s_ref = refs[0]
        in_refs = refs[1 : 1 + 2 * views]
        est_ref, zp_ref, yp_ref, pat_ref, rw_ref = refs[1 + 2 * views : 6 + 2 * views]
        rest = refs[6 + 2 * views :]
        out_ref = rest[0]
        crop_ref = None if last else rest[1]
        placed, stage, crops = rest[-3:]
        me = s_ref[2]
        for s in range(views):
            view = lax.rem(me + views - s, views)
            for h in range(2):
                src = in_refs[2 * s + h]
                x = src[pl.ds(0, half)].astype(F32).reshape(half * rows, tile_z)
                hi, lo = split(x)
                out = dot(jnp.concatenate([hi, lo], axis=1), zp_ref[view, 0])
                out = out + dot(hi, zp_ref[view, 1, :tile_z, :])
                at = pl.multiple_of((view * 2 + h) * half * rows, half * rows)
                for j in range(brick_z // tile_z):
                    placed[j, pl.ds(at, half * rows), :] = out[:, j * tile_z : (j + 1) * tile_z]

        def step(r, carry):
            x = jnp.concatenate(
                [
                    placed[j, pl.ds(r, views * tile_y, stride=rows), :]
                    for j in range(brick_z // tile_z)
                ],
                axis=1,
            )
            hi, lo = split(x)
            out = dot(yp_ref[...], jnp.concatenate([hi, lo], axis=0))
            correction = out[:brick_y] + out[brick_y:]
            weight = jnp.zeros((brick_y, brick_z), F32)
            for v in range(views):
                factor = rw_ref[v, pl.ds(r, 1), :]
                factor = jnp.concatenate([factor] * (brick_z // factor.shape[1]), axis=1)
                weight = weight + factor * pat_ref[v]
            value = est_ref[r] * (1.0 + correction) / (1.0 + weight)
            out_ref[r] = value
            if not last:
                crops[pl.ds(r, tile_y, stride=rows), :] = crop_rows(
                    value, s_ref[0], s_ref[1], tile_y, tile_z, stage
                )
            return carry

        lax.fori_loop(0, rows, step, 0, unroll=2)
        if not last:
            crop_ref[...] = crops[...].astype(BF16).reshape(tile_y, rows, tile_z)

    vmem = pl.BlockSpec(memory_space=pltpu.VMEM)
    shapes = [jax.ShapeDtypeStruct(estimate.shape, F32)]
    if not last:
        shapes.append(jax.ShapeDtypeStruct((tile_y, rows, tile_z), BF16))
    return pl.pallas_call(
        kernel,
        out_shape=tuple(shapes),
        in_specs=[pl.BlockSpec(memory_space=pltpu.SMEM)] + [vmem] * (2 * views + 5),
        out_specs=(vmem,) * len(shapes),
        scratch_shapes=[
            pltpu.VMEM((brick_z // tile_z, views * tile_y * rows, tile_z), F32),
            pltpu.VMEM((brick_y, tile_z), F32),
            pltpu.VMEM((tile_y * rows, tile_z), F32),
        ],
        name="update",
    )(scalars, *flat, estimate, z_place, y_place, outline, row_weight)


def flip(x, bit, count):
    return lax.ppermute(x, "brick", [(i, i ^ bit) for i in range(count)])


def gather_owners(crop, count):
    half = crop.shape[0] // 2
    got = {0: (crop[:half], crop[half:])}
    bits = [1 << i for i in range(count.bit_length() - 1)]
    wide = bits[1:]
    if len(wide) == 2:
        x, y = wide
        over_x = flip(crop, x, count)
        over_y = flip(crop, y, count)
        got[x] = (over_x[:half], over_x[half:])
        got[y] = (over_y[:half], over_y[half:])
        got[x | y] = (flip(over_x[:half], y, count), flip(over_y[half:], x, count))
        core = {0: flip(crop, 1, count), x: flip(over_x, 1, count), y: flip(over_y, 1, count)}
        for k, value in core.items():
            got[k | 1] = (value[:half], value[half:])
        got[x | y | 1] = tuple(flip(p, 1, count) for p in got[x | y])
    else:
        for bit in wide + [1]:
            for k in list(got):
                got[k ^ bit] = tuple(flip(p, bit, count) for p in got[k])
    return [got[k] for k in range(count)]


def halving_orders(count):
    bits = [1 << i for i in range(count.bit_length() - 1)]
    orders = [bits, bits[:1] + bits[:0:-1]]
    slots = []
    for order in orders:
        place = {}
        for k in range(count):
            slot = 0
            for bit in order:
                slot = slot * 2 + (0 if k & bit else 1)
            place[k] = slot
        slots.append(place)
    return orders, slots


def on_device(
    estimate, views_data, psf_taps, seg_owner, seg_local, seg_offset, seg_extent, view_shift
):
    per_owner, brick_x, brick_y, brick_z = estimate.shape
    tile_x, tile_y, tile_z = views_data.shape[2:]
    own_rows = per_owner * brick_x
    owners = lax.axis_size("brick")
    views = lax.axis_size("view")
    me = lax.axis_index("brick")
    my_view = lax.axis_index("view")
    half = tile_y // 2
    highest = lax.Precision.HIGHEST

    flat = estimate.reshape(own_rows, brick_y, brick_z)
    shifts = view_shift[0]
    scalars = jnp.concatenate([shifts, my_view[None].astype(jnp.int32)])
    crop = first_crop(scalars, flat, tile_y, tile_z)

    taps = psf_taps[0] / jnp.sum(psf_taps[0], axis=1, keepdims=True)
    count = taps.shape[1]
    lanes = 128
    meta = jnp.zeros((8, lanes), F32)
    meta = meta.at[0, :count].set(taps[1]).at[1, :count].set(taps[2])
    meta = meta.at[2, :2].set(shifts.astype(F32))
    around = [meta] + [
        lax.ppermute(meta, "view", [(i, (i + s) % views) for i in range(views)])
        for s in range(1, views)
    ]
    view_ids = jnp.arange(views, dtype=jnp.int32)
    steps_back = lax.rem(my_view - view_ids + views, views)
    metas = sum(
        jnp.where((steps_back == s)[:, None, None], around[s][None], 0.0) for s in range(views)
    )
    all_shifts = metas[:, 2, :2].astype(jnp.int32)

    tile_rows = jnp.arange(tile_x, dtype=jnp.int32)
    tile_cols = jnp.arange(tile_z, dtype=jnp.int32)
    tile_mids = jnp.arange(tile_y, dtype=jnp.int32)
    extent = seg_extent[0, 0]
    seg_ids = jnp.arange(extent.shape[0], dtype=jnp.int32)
    starts = jnp.sum(jnp.where(seg_ids[None, :] < seg_ids[:, None], extent[None, :], 0), axis=1)
    base = (
        (seg_owner[0, 0, :, 0] ^ me) * own_rows + seg_local[0, 0] * brick_x + seg_offset[0, 0]
    )
    inside = (starts[None, :] <= tile_rows[:, None]) & (
        tile_rows[:, None] < (starts + extent)[None, :]
    )
    source = jnp.sum(jnp.where(inside, (base - starts)[None, :], 0), axis=1) + tile_rows
    picks = (
        source[:, None] == jnp.arange(owners * own_rows, dtype=jnp.int32)[None, :]
    ).astype(F32)
    x_mat = band(taps[0], tile_rows, tile_rows)
    rows_mat = jnp.einsum("tw,tr->wr", x_mat, picks, precision=highest)
    hi, lo = split_outside(rows_mat)
    gather_mat = jnp.concatenate([hi, lo], axis=0)
    scatter_mat = jnp.concatenate(
        [jnp.concatenate([hi.T, hi.T], axis=1), jnp.concatenate([lo.T, lo.T], axis=1)], axis=0
    )
    hi, lo = split_outside(band(taps[2], tile_cols, tile_cols))
    pair = jnp.concatenate([hi, lo], axis=1)
    z_mat = jnp.concatenate([pair, pair], axis=0)
    per_group = max(1, 128 // tile_y)
    y_mat = jnp.kron(
        jnp.eye(per_group, dtype=F32), band(taps[1], tile_mids, tile_mids).T
    )
    hi, lo = split_outside(y_mat)
    y_mat = jnp.concatenate(
        [jnp.concatenate([hi, hi], axis=1), jnp.concatenate([lo, lo], axis=1)], axis=0
    )

    def placing(values, shift, long, short):
        at = jnp.arange(long, dtype=jnp.int32) - shift
        mat = band(values, at, jnp.arange(short, dtype=jnp.int32))
        return jnp.where(((at >= 0) & (at < short))[:, None], mat, 0.0)

    z_all = jax.vmap(lambda m, s: placing(m[1, :count], s[1], brick_z, tile_z).T)(
        metas, all_shifts
    )
    y_all = jax.vmap(lambda m, s: placing(m[0, :count], s[0], brick_y, tile_y))(
        metas, all_shifts
    )
    outline = jnp.sum(y_all, axis=2)[:, :, None] * jnp.sum(z_all, axis=1)[:, None, :]
    hi, lo = split_outside(z_all)
    z_place = jnp.stack(
        [jnp.concatenate([hi, hi], axis=1), jnp.concatenate([lo, lo], axis=1)], axis=1
    )
    y_wide = jnp.transpose(y_all, (1, 0, 2)).reshape(brick_y, views * tile_y)
    hi, lo = split_outside(y_wide)
    y_place = jnp.concatenate(
        [jnp.concatenate([hi, hi], axis=1), jnp.concatenate([lo, lo], axis=1)], axis=0
    )
    measured = views_data.reshape(tile_x * tile_y, tile_z)
    orders, slots = halving_orders(owners)

    row_weight = None
    current = flat
    for sweep in range(ITERS):
        last = sweep == ITERS - 1
        pieces = gather_owners(crop, owners)
        outs = read_tile(
            pieces, measured, gather_mat, scatter_mat, z_mat, y_mat, slots, sweep == 0
        )
        send = [outs[0], outs[2]]
        keep = [outs[1], outs[3]]
        for i in range(len(orders[0])):
            for h in range(2):
                total = keep[h] + flip(send[h], orders[h][i], owners).astype(F32)
                left = total.shape[0] // 2
                send[h] = total[:left].astype(WIRE) if left else None
                keep[h] = total[left:]
        mine = [k[0].astype(WIRE) for k in keep]
        sums = [tuple(mine)] + [
            tuple(
                lax.ppermute(p, "view", [(i, (i + s) % views) for i in range(views)])
                for p in mine
            )
            for s in range(1, views)
        ]
        if sweep == 0:
            row_weight = sum(
                jnp.where((steps_back == s)[:, None, None], sums[s][0][half][None], 0.0)
                for s in range(views)
            )
        result = update(
            scalars, sums, current, z_place, y_place, outline, row_weight, tile_y, tile_z, last
        )
        current = result[0]
        if not last:
            crop = result[1]
    return current.reshape(estimate.shape)


def solution(mesh):
    placed = (
        P("brick", None, None, None),
        P("view", "brick", None, None, None),
        P("view", None, None),
        P("view", "brick", None, None),
        P("view", "brick", None),
        P("view", "brick", None),
        P("view", "brick", None),
        P("view", None),
    )
    return jax.shard_map(
        on_device,
        mesh=mesh,
        in_specs=placed,
        out_specs=P("brick", None, None, None),
        check_vma=False,
    )
```

time: 648 us -> 260 us (0.40); the launches traced: 639 us -> 260 us
  waiting for transfers between devices: 320 us -> 120 us
  blocking collectives: 128 us -> 0 us
  local copies, waits for them, and re-layouts: 97.1 us -> 15.4 us
  Pallas kernels: 0 us -> 53.4 us
  starting transfers between devices: 9.48 us -> 54.2 us
  matrix products: 35 us -> 0.29 us
  between operations: 18.1 us -> 0.69 us
  other arithmetic: 31.1 us -> 15.7 us
    psum x2 -> x0, waiting for transfers between devices: 240 us -> none  [to_owners(): return lax.psum(brick_part, 'view')]
    ppermute x0 -> x45, waiting for transfers between devices: none -> 120 us  [the longest x12 67 us: on_device(): lax.ppermute(p, 'view', [(i, (i + s) % views) for i in range(views)])]
    all_gather x4 -> x0, blocking collectives: 76.4 us -> none  [the longest x1 52 us: on_device(): lax.all_gather(seg_owner[:, :, :, 0], 'brick', axis=1, tiled=True)]
    ppermute x0 -> x45, starting transfers between devices: none -> 54.2 us  [the longest x12 30.7 us: on_device(): lax.ppermute(p, 'view', [(i, (i + s) % views) for i in range(views)])]
    pallas_call x0 -> x5, Pallas kernels: none -> 53.4 us  [the longest x2 26.7 us: read_tile(): pl.pallas_call(kernel, out_shape=tuple(shapes), in_specs=[vmem] * (2 * ow...]
    all_to_all x1 -> x0, blocking collectives: 51.6 us -> none  [to_owners(): lax.all_to_all(outgoing, 'brick', split_axis=0, concat_axis=0, tiled=True)]
    all_to_all x2 -> x0, waiting for transfers between devices: 42.6 us -> none  [to_owners(): lax.all_to_all(outgoing, 'brick', split_axis=0, concat_axis=0, tiled=True)]
    dynamic_update_slice x3 -> x0, local copies, waits for them, and re-layouts: 41.2 us -> none  [to_owners(): lax.dynamic_update_slice(jnp.zeros((own_rows, brick_y, brick_z), jnp.floa...]
  transfers between devices with their start and end apart: 6 -> 45, of which waited for: 5 -> 18; matrix products, arithmetic and copies ran while one was open for 6% -> 10% of each run, Pallas kernels for 0% -> 1%
where the time goes in v1:
time: 260 us
  waiting for transfers between devices  120 us (46%)
  starting transfers between devices  54.2 us (21%)
  Pallas kernels  53.4 us (21%)
  other arithmetic  15.7 us (6%)
  local copies, waits for them, and re-layouts  15.4 us (6%)
    ppermute x12, waiting for transfers between devices, on_device(): lax.ppermute(p, 'view', [(i, (i + s) % views) for i in range(views)])  67 us
    ppermute x30, waiting for transfers between devices, flip(): return lax.ppermute(x, 'brick', [(i, i ^ bit) for i in range(count)])  53.3 us
    ppermute x12, starting transfers between devices, on_device(): lax.ppermute(p, 'view', [(i, (i + s) % views) for i in range(views)])  30.7 us
    pallas_call x2, Pallas kernels, read_tile(): pl.pallas_call(kernel, out_shape=tuple(shapes), in_specs=[vmem] * (2 * ow...  26.7 us
    pallas_call x2, Pallas kernels, update(): pl.pallas_call(kernel, out_shape=tuple(shapes), in_specs=[pl.BlockSpec(me...  22.9 us
    ppermute x30, starting transfers between devices, flip(): return lax.ppermute(x, 'brick', [(i, i ^ bit) for i in range(count)])  17.4 us
    ppermute x3, starting transfers between devices, on_device(): lax.ppermute(meta, 'view', [(i, (i + s) % views) for i in range(views)])  6.14 us
  transfers between devices with their start and end apart: 45, of which 18 were waited for; matrix products, arithmetic and copies ran while one was open for 10% of the time, Pallas kernels for 1%

profile of v1, /device:TPU:0, one launch (start us, length us, event | category | flops | bytes accessed | tf_op | source)
XLA Modules:
  0.0 259.9 jit_solution(13309126592091955098)
XLA Ops:
  2.7 5.1 %collective-permute-start.23 = (f32[8,128]{1,0:T(8,128)S(1)}, f32[8,128]{1,0:T(8,128)S(1)}, u32[]{:S(2)}, u32[]{:S(2)}) collective-permute-start(f32[8,128]{1,0:T(8,128)S(1)} %scatter.14), channel_id=1, source_target_pairs={{0,24},{8,0},{16,8},{24,16},{1,25},{9,1},{17,9},{25,17},{2,26},{10... | collective-permute-start | bytes 12296 | tf_op jit(solution)/shard_map/ppermute | solution.py:310
  10.1 3.8 %first_crop.1 = bf16[32,32,128]{2,1,0:T(8,128)(2,1)} custom-call(s32[3]{0:T(128)} %pad_add_fusion.shift_ref.refs_0_, f32[32,64,256]{2,1,0:T(8,128)} %bitcast.67), custom_call_target="tpu_custom_call" | custom-call | tf_op jit(solution)/shard_map/first_crop/pallas_call | solution.py:55
  26.5 3.8 %collective-permute-done.3 = bf16[32,32,128]{2,1,0:T(8,128)(2,1)S(1)} collective-permute-done((bf16[32,32,128]{2,1,0:T(8,128)(2,1)S(1)}, bf16[32,32,128]{2,1,0:T(8,128)(2,1)S(1)}, u32[]{:S(2)}, u32[]{:S(2)}) %collective-permute-start.3) | collective-permute-done | bytes 262176 | tf_op jit(solution)/shard_map/ppermute | solution.py:244
  32.8 3.2 %collective-permute-done.6.refs_13_ = bf16[16,32,128]{2,1,0:T(8,128)(2,1)S(1)} collective-permute-done((bf16[16,32,128]{2,1,0:T(8,128)(2,1)S(1)}, bf16[16,32,128]{2,1,0:T(8,128)(2,1)S(1)}, u32[]{:S(2)}, u32[]{:S(2)}) %collective-permute-start.6) | collective-permute-done | bytes 131104 | tf_op jit(solution)/shard_map/ppermute | solution.py:244
  38.2 13.4 %read_tile.2 = (f32[4,17,32,128]{3,2,1,0:T(8,128)}, f32[4,17,32,128]{3,2,1,0:T(8,128)}, f32[4,16,32,128]{3,2,1,0:T(8,128)}, f32[4,16,32,128]{3,2,1,0:T(8,128)}) custom-call(bf16[16,32,128]{2,1,0:T(8,128)(2,1)} %get-tuple-element.87.refs_0_, bf16[16,32,128]{2,1,0:T(8,128)(2,1)} %get-tuple-element.86.refs_1_, bf16[16,32,128]{2,1,0:T(8,128)(2,1)} %get-tuple-element.85.refs_2_, ...), custom_call_target="tpu_custom_call" | custom-call | tf_op jit(solution)/shard_map/read_tile/pallas_call | solution.py:160
  59.0 11.1 %collective-permute-done.10 = f32[2,17,32,128]{3,2,1,0:T(8,128)S(1)} collective-permute-done((f32[2,17,32,128]{3,2,1,0:T(8,128)S(1)}, f32[2,17,32,128]{3,2,1,0:T(8,128)S(1)}, u32[]{:S(2)}, u32[]{:S(2)}) %collective-permute-start.10) | collective-permute-done | bytes 557088 | tf_op jit(solution)/shard_map/ppermute | solution.py:244
  73.1 5.2 %collective-permute-done.11 = f32[1,17,32,128]{3,2,1,0:T(8,128)S(1)} collective-permute-done((f32[1,17,32,128]{3,2,1,0:T(8,128)S(1)}, f32[1,17,32,128]{3,2,1,0:T(8,128)S(1)}, u32[]{:S(2)}, u32[]{:S(2)}) %collective-permute-start.11) | collective-permute-done | bytes 278560 | tf_op jit(solution)/shard_map/ppermute | solution.py:244
  78.4 2.9 %collective-permute-start.19 = (f32[17,32,128]{2,1,0:T(8,128)S(1)}, f32[17,32,128]{2,1,0:T(8,128)S(1)}, u32[]{:S(2)}, u32[]{:S(2)}) collective-permute-start(f32[17,32,128]{2,1,0:T(8,128)S(1)} %bitcast.71), channel_id=1, source_target_pairs={{0,24},{8,0},{16,8},{24,16},{1,25},{9,1},{17,9},{25,17},{2,26},{10... | collective-permute-start | bytes 835592 | tf_op jit(solution)/shard_map/ppermute | solution.py:398
  86.3 2.1 collective-permute-done.19.refs_7_
  88.4 2.0 collective-permute-start.15
  90.4 37.5 %collective-permute-done.17.refs_5_ = f32[17,32,128]{2,1,0:T(8,128)S(1)} collective-permute-done((f32[17,32,128]{2,1,0:T(8,128)S(1)}, f32[17,32,128]{2,1,0:T(8,128)S(1)}, u32[]{:S(2)}, u32[]{:S(2)}) %collective-permute-start.17) | collective-permute-done | bytes 278560 | tf_op jit(solution)/shard_map/ppermute | solution.py:398
  130.3 12.4 %update.2 = (f32[32,64,256]{2,1,0:T(8,128)}, bf16[32,32,128]{2,1,0:T(8,128)(2,1)}) custom-call(s32[3]{0:T(128)} %pad_add_fusion.shift_ref.refs_0_, f32[17,32,128]{2,1,0:T(8,128)} %bitcast.74, f32[16,32,128]{2,1,0:T(8,128)} %copy-done.5, f32[17,32,128]{2,1,0:T(8,128)} %copy-done.14, f32[16,32,128]{2,1,0:T(8,128)} %copy-done.20, f32[17,32,128]{2,1,0:T(8,128)} %copy-done.13, ...), custom_call_target="tpu_custom_call" | custom-call | tf_op jit(solution)/shard_map/update/pallas_call | solution.py:229
  146.5 2.8 %collective-permute-done.25 = bf16[32,32,128]{2,1,0:T(8,128)(2,1)S(1)} collective-permute-done((bf16[32,32,128]{2,1,0:T(8,128)(2,1)}, bf16[32,32,128]{2,1,0:T(8,128)(2,1)S(1)}, u32[]{:S(2)}, u32[]{:S(2)}) %collective-permute-start.25) | collective-permute-done | bytes 262176 | tf_op jit(solution)/shard_map/ppermute | solution.py:244
  155.0 3.1 %collective-permute-done.30.refs_13_ = bf16[16,32,128]{2,1,0:T(8,128)(2,1)S(1)} collective-permute-done((bf16[16,32,128]{2,1,0:T(8,128)(2,1)S(1)}, bf16[16,32,128]{2,1,0:T(8,128)(2,1)S(1)}, u32[]{:S(2)}, u32[]{:S(2)}) %collective-permute-start.30) | collective-permute-done | bytes 131104 | tf_op jit(solution)/shard_map/ppermute | solution.py:244
  160.3 13.3 %read_tile.3 = (f32[4,16,32,128]{3,2,1,0:T(8,128)}, f32[4,16,32,128]{3,2,1,0:T(8,128)}, f32[4,16,32,128]{3,2,1,0:T(8,128)}, f32[4,16,32,128]{3,2,1,0:T(8,128)}) custom-call(bf16[16,32,128]{2,1,0:T(8,128)(2,1)} %get-tuple-element.75.refs_0_, bf16[16,32,128]{2,1,0:T(8,128)(2,1)} %get-tuple-element.74.refs_1_, bf16[16,32,128]{2,1,0:T(8,128)(2,1)} %get-tuple-element.73.refs_2_, ...), custom_call_target="tpu_custom_call" | custom-call | tf_op jit(solution)/shard_map/read_tile/pallas_call | solution.py:160
  174.2 2.4 collective-permute-done.33
  179.6 12.8 %collective-permute-done.34 = f32[2,16,32,128]{3,2,1,0:T(8,128)S(1)} collective-permute-done((f32[2,16,32,128]{3,2,1,0:T(8,128)S(1)}, f32[2,16,32,128]{3,2,1,0:T(8,128)S(1)}, u32[]{:S(2)}, u32[]{:S(2)}) %collective-permute-start.34) | collective-permute-done | bytes 524320 | tf_op jit(solution)/shard_map/ppermute | solution.py:244
  194.7 5.7 %collective-permute-done.35 = f32[1,16,32,128]{3,2,1,0:T(8,128)S(1)} collective-permute-done((f32[1,16,32,128]{3,2,1,0:T(8,128)S(1)}, f32[1,16,32,128]{3,2,1,0:T(8,128)S(1)}, u32[]{:S(2)}, u32[]{:S(2)}) %collective-permute-start.35) | collective-permute-done | bytes 262176 | tf_op jit(solution)/shard_map/ppermute | solution.py:244
  200.5 3.8 %collective-permute-start.41 = (f32[16,32,128]{2,1,0:T(8,128)S(1)}, f32[16,32,128]{2,1,0:T(8,128)S(1)}, u32[]{:S(2)}, u32[]{:S(2)}) collective-permute-start(f32[16,32,128]{2,1,0:T(8,128)S(1)} %fusion.3.refs_1_), channel_id=1, source_target_pairs={{0,16},{8,24},{16,0},{24,8},{1,17},{9,25},{17,1},{25,9},{2,18},{10... | collective-permute-start | bytes 786440 | tf_op jit(solution)/shard_map/ppermute | solution.py:398
  204.3 1.9 collective-permute-start.39
  208.6 13.0 %collective-permute-start.40 = (f32[16,32,128]{2,1,0:T(8,128)S(1)}, f32[16,32,128]{2,1,0:T(8,128)S(1)}, u32[]{:S(2)}, u32[]{:S(2)}) collective-permute-start(f32[16,32,128]{2,1,0:T(8,128)S(1)} %fusion.2.refs_2_), channel_id=1, source_target_pairs={{0,8},{8,16},{16,24},{24,0},{1,9},{9,17},{17,25},{25,1},{2,10},{10... | collective-permute-start | bytes 786440 | tf_op jit(solution)/shard_map/ppermute | solution.py:398
  221.6 17.8 %collective-permute-done.41.refs_5_ = f32[16,32,128]{2,1,0:T(8,128)S(1)} collective-permute-done((f32[16,32,128]{2,1,0:T(8,128)S(1)}, f32[16,32,128]{2,1,0:T(8,128)S(1)}, u32[]{:S(2)}, u32[]{:S(2)}) %collective-permute-start.41) | collective-permute-done | bytes 262176 | tf_op jit(solution)/shard_map/ppermute | solution.py:398
  239.5 9.2 %collective-permute-done.42.refs_6_ = f32[16,32,128]{2,1,0:T(8,128)S(1)} collective-permute-done((f32[16,32,128]{2,1,0:T(8,128)S(1)}, f32[16,32,128]{2,1,0:T(8,128)S(1)}, u32[]{:S(2)}, u32[]{:S(2)}) %collective-permute-start.42) | collective-permute-done | bytes 262176 | tf_op jit(solution)/shard_map/ppermute | solution.py:398
  249.5 10.5 %update.3 = f32[32,64,256]{2,1,0:T(8,128)} custom-call(s32[3]{0:T(128)} %pad_add_fusion.shift_ref.refs_0_, f32[16,32,128]{2,1,0:T(8,128)} %copy-done.4, f32[16,32,128]{2,1,0:T(8,128)} %copy-done.6, f32[16,32,128]{2,1,0:T(8,128)} %copy-done.19, f32[16,32,128]{2,1,0:T(8,128)} %copy-done.23, f32[16,32,128]{2,1,0:T(8,128)} %copy-done.17, ...), custom_call_target="tpu_custom_call" | custom-call | tf_op jit(solution)/shard_map/update/pallas_call | solution.py:229
  (237 shorter events, 60.3 us)
Async XLA Ops:
  2.7 18.4 %collective-permute-start.23 = (f32[8,128]{1,0:T(8,128)S(1)}, f32[8,128]{1,0:T(8,128)S(1)}, u32[]{:S(2)}, u32[]{:S(2)}) collective-permute-start(f32[8,128]{1,0:T(8,128)S(1)} %scatter.14), channel_id=1, source_target_pairs={{0,24},{8,0},{16,8},{24,16},{1,25},{9,1},{17,9},{25,17},{2,26},{10... | collective-permute-start | bytes 12296 | tf_op jit(solution)/shard_map/ppermute | solution.py:310
  7.8 14.9 %collective-permute-start.22 = (f32[8,128]{1,0:T(8,128)S(1)}, f32[8,128]{1,0:T(8,128)S(1)}, u32[]{:S(2)}, u32[]{:S(2)}) collective-permute-start(f32[8,128]{1,0:T(8,128)S(1)} %scatter.14), channel_id=1, source_target_pairs={{0,16},{8,24},{16,0},{24,8},{1,17},{9,25},{17,1},{25,9},{2,18},{10... | collective-permute-start | bytes 12296 | tf_op jit(solution)/shard_map/ppermute | solution.py:310
  7.8 14.9 %collective-permute-start.21 = (f32[8,128]{1,0:T(8,128)S(1)}, f32[8,128]{1,0:T(8,128)S(1)}, u32[]{:S(2)}, u32[]{:S(2)}) collective-permute-start(f32[8,128]{1,0:T(8,128)S(1)} %scatter.14), channel_id=1, source_target_pairs={{0,8},{8,16},{16,24},{24,0},{1,9},{9,17},{17,25},{25,1},{2,10},{10... | collective-permute-start | bytes 12296 | tf_op jit(solution)/shard_map/ppermute | solution.py:310
  13.8 11.5 %collective-permute-start.1 = (bf16[32,32,128]{2,1,0:T(8,128)(2,1)}, bf16[32,32,128]{2,1,0:T(8,128)(2,1)S(1)}, u32[]{:S(2)}, u32[]{:S(2)}) collective-permute-start(bf16[32,32,128]{2,1,0:T(8,128)(2,1)} %first_crop.1), channel_id=1, source_target_pairs={{0,2},{1,3},{2,0},{3,1},{4,6},{5,7},{6,4},{7,5},{8,10},{9,11},{10,... | collective-permute-start | bytes 786440 | tf_op jit(solution)/shard_map/ppermute | solution.py:244
  15.3 16.3 %collective-permute-start = (bf16[32,32,128]{2,1,0:T(8,128)(2,1)}, bf16[32,32,128]{2,1,0:T(8,128)(2,1)S(1)}, u32[]{:S(2)}, u32[]{:S(2)}) collective-permute-start(bf16[32,32,128]{2,1,0:T(8,128)(2,1)} %first_crop.1), channel_id=1, source_target_pairs={{0,1},{1,0},{2,3},{3,2},{4,5},{5,4},{6,7},{7,6},{8,9},{9,8},{10,11... | collective-permute-start | bytes 786440 | tf_op jit(solution)/shard_map/ppermute | solution.py:244
  21.1 9.2 %collective-permute-start.3 = (bf16[32,32,128]{2,1,0:T(8,128)(2,1)S(1)}, bf16[32,32,128]{2,1,0:T(8,128)(2,1)S(1)}, u32[]{:S(2)}, u32[]{:S(2)}) collective-permute-start(bf16[32,32,128]{2,1,0:T(8,128)(2,1)S(1)} %copy-done.7), channel_id=1, source_target_pairs={{0,4},{1,5},{2,6},{3,7},{4,0},{5,1},{6,2},{7,3},{8,12},{9,13},{10,... | collective-permute-start | bytes 786440 | tf_op jit(solution)/shard_map/ppermute | solution.py:244
  26.5 9.5 %collective-permute-start.2 = (bf16[32,32,128]{2,1,0:T(8,128)(2,1)S(1)}, bf16[32,32,128]{2,1,0:T(8,128)(2,1)S(1)}, u32[]{:S(2)}, u32[]{:S(2)}) collective-permute-start(bf16[32,32,128]{2,1,0:T(8,128)(2,1)S(1)} %collective-permute-done.1), channel_id=1, source_target_pairs={{0,1},{1,0},{2,3},{3,2},{4,5},{5,4},{6,7},{7,6},{8,9},{9,8},{10,11... | collective-permute-start | bytes 786440 | tf_op jit(solution)/shard_map/ppermute | solution.py:244
  55.1 15.0 %collective-permute-start.10 = (f32[2,17,32,128]{3,2,1,0:T(8,128)S(1)}, f32[2,17,32,128]{3,2,1,0:T(8,128)S(1)}, u32[]{:S(2)}, u32[]{:S(2)}) collective-permute-start(f32[2,17,32,128]{3,2,1,0:T(8,128)S(1)} %slice.288), channel_id=1, source_target_pairs={{0,2},{1,3},{2,0},{3,1},{4,6},{5,7},{6,4},{7,5},{8,10},{9,11},{10,... | collective-permute-start | bytes 1671176 | tf_op jit(solution)/shard_map/ppermute | solution.py:244
  56.6 15.2 %collective-permute-start.13 = (f32[2,16,32,128]{3,2,1,0:T(8,128)S(1)}, f32[2,16,32,128]{3,2,1,0:T(8,128)S(1)}, u32[]{:S(2)}, u32[]{:S(2)}) collective-permute-start(f32[2,16,32,128]{3,2,1,0:T(8,128)S(1)} %slice.292), channel_id=1, source_target_pairs={{0,4},{1,5},{2,6},{3,7},{4,0},{5,1},{6,2},{7,3},{8,12},{9,13},{10,... | collective-permute-start | bytes 1572872 | tf_op jit(solution)/shard_map/ppermute | solution.py:244
  71.9 9.4 %collective-permute-start.14 = (f32[1,16,32,128]{3,2,1,0:T(8,128)S(1)}, f32[1,16,32,128]{3,2,1,0:T(8,128)S(1)}, u32[]{:S(2)}, u32[]{:S(2)}) collective-permute-start(f32[1,16,32,128]{3,2,1,0:T(8,128)S(1)} %slice.294), channel_id=1, source_target_pairs={{0,2},{1,3},{2,0},{3,1},{4,6},{5,7},{6,4},{7,5},{8,10},{9,11},{10,... | collective-permute-start | bytes 786440 | tf_op jit(solution)/shard_map/ppermute | solution.py:244
  78.4 10.0 %collective-permute-start.19 = (f32[17,32,128]{2,1,0:T(8,128)S(1)}, f32[17,32,128]{2,1,0:T(8,128)S(1)}, u32[]{:S(2)}, u32[]{:S(2)}) collective-permute-start(f32[17,32,128]{2,1,0:T(8,128)S(1)} %bitcast.71), channel_id=1, source_target_pairs={{0,24},{8,0},{16,8},{24,16},{1,25},{9,1},{17,9},{25,17},{2,26},{10... | collective-permute-start | bytes 835592 | tf_op jit(solution)/shard_map/ppermute | solution.py:398
  81.3 47.4 %collective-permute-start.20 = (f32[16,32,128]{2,1,0:T(8,128)S(1)}, f32[16,32,128]{2,1,0:T(8,128)S(1)}, u32[]{:S(2)}, u32[]{:S(2)}) collective-permute-start(f32[16,32,128]{2,1,0:T(8,128)S(1)} %fusion.4.refs_2_), channel_id=1, source_target_pairs={{0,24},{8,0},{16,8},{24,16},{1,25},{9,1},{17,9},{25,17},{2,26},{10... | collective-permute-start | bytes 786440 | tf_op jit(solution)/shard_map/ppermute | solution.py:398
  82.3 46.4 %collective-permute-start.18 = (f32[16,32,128]{2,1,0:T(8,128)S(1)}, f32[16,32,128]{2,1,0:T(8,128)S(1)}, u32[]{:S(2)}, u32[]{:S(2)}) collective-permute-start(f32[16,32,128]{2,1,0:T(8,128)S(1)} %fusion.4.refs_2_), channel_id=1, source_target_pairs={{0,16},{8,24},{16,0},{24,8},{1,17},{9,25},{17,1},{25,9},{2,18},{10... | collective-permute-start | bytes 786440 | tf_op jit(solution)/shard_map/ppermute | solution.py:398
  83.4 45.4 %collective-permute-start.16 = (f32[16,32,128]{2,1,0:T(8,128)S(1)}, f32[16,32,128]{2,1,0:T(8,128)S(1)}, u32[]{:S(2)}, u32[]{:S(2)}) collective-permute-start(f32[16,32,128]{2,1,0:T(8,128)S(1)} %fusion.4.refs_2_), channel_id=1, source_target_pairs={{0,8},{8,16},{16,24},{24,0},{1,9},{9,17},{17,25},{25,1},{2,10},{10... | collective-permute-start | bytes 786440 | tf_op jit(solution)/shard_map/ppermute | solution.py:398
  84.5 43.4 %collective-permute-start.17 = (f32[17,32,128]{2,1,0:T(8,128)S(1)}, f32[17,32,128]{2,1,0:T(8,128)S(1)}, u32[]{:S(2)}, u32[]{:S(2)}) collective-permute-start(f32[17,32,128]{2,1,0:T(8,128)S(1)} %bitcast.72), channel_id=1, source_target_pairs={{0,16},{8,24},{16,0},{24,8},{1,17},{9,25},{17,1},{25,9},{2,18},{10... | collective-permute-start | bytes 835592 | tf_op jit(solution)/shard_map/ppermute | solution.py:398
  88.4 39.5 %collective-permute-start.15 = (f32[17,32,128]{2,1,0:T(8,128)S(1)}, f32[17,32,128]{2,1,0:T(8,128)S(1)}, u32[]{:S(2)}, u32[]{:S(2)}) collective-permute-start(f32[17,32,128]{2,1,0:T(8,128)S(1)} %bitcast.73), channel_id=1, source_target_pairs={{0,8},{8,16},{16,24},{24,0},{1,9},{9,17},{17,25},{25,1},{2,10},{10... | collective-permute-start | bytes 835592 | tf_op jit(solution)/shard_map/ppermute | solution.py:398
  178.2 14.3 %collective-permute-start.34 = (f32[2,16,32,128]{3,2,1,0:T(8,128)S(1)}, f32[2,16,32,128]{3,2,1,0:T(8,128)S(1)}, u32[]{:S(2)}, u32[]{:S(2)}) collective-permute-start(f32[2,16,32,128]{3,2,1,0:T(8,128)S(1)} %slice.313), channel_id=1, source_target_pairs={{0,2},{1,3},{2,0},{3,1},{4,6},{5,7},{6,4},{7,5},{8,10},{9,11},{10,... | collective-permute-start | bytes 1572872 | tf_op jit(solution)/shard_map/ppermute | solution.py:244
  179.1 14.1 %collective-permute-start.37 = (f32[2,16,32,128]{3,2,1,0:T(8,128)S(1)}, f32[2,16,32,128]{3,2,1,0:T(8,128)S(1)}, u32[]{:S(2)}, u32[]{:S(2)}) collective-permute-start(f32[2,16,32,128]{3,2,1,0:T(8,128)S(1)} %slice.317), channel_id=1, source_target_pairs={{0,4},{1,5},{2,6},{3,7},{4,0},{5,1},{6,2},{7,3},{8,12},{9,13},{10,... | collective-permute-start | bytes 1572872 | tf_op jit(solution)/shard_map/ppermute | solution.py:244
  193.3 12.9 %collective-permute-start.38 = (f32[1,16,32,128]{3,2,1,0:T(8,128)S(1)}, f32[1,16,32,128]{3,2,1,0:T(8,128)S(1)}, u32[]{:S(2)}, u32[]{:S(2)}) collective-permute-start(f32[1,16,32,128]{3,2,1,0:T(8,128)S(1)} %slice.319), channel_id=1, source_target_pairs={{0,2},{1,3},{2,0},{3,1},{4,6},{5,7},{6,4},{7,5},{8,10},{9,11},{10,... | collective-permute-start | bytes 786440 | tf_op jit(solution)/shard_map/ppermute | solution.py:244
  200.5 38.9 %collective-permute-start.41 = (f32[16,32,128]{2,1,0:T(8,128)S(1)}, f32[16,32,128]{2,1,0:T(8,128)S(1)}, u32[]{:S(2)}, u32[]{:S(2)}) collective-permute-start(f32[16,32,128]{2,1,0:T(8,128)S(1)} %fusion.3.refs_1_), channel_id=1, source_target_pairs={{0,16},{8,24},{16,0},{24,8},{1,17},{9,25},{17,1},{25,9},{2,18},{10... | collective-permute-start | bytes 786440 | tf_op jit(solution)/shard_map/ppermute | solution.py:398
  204.3 35.2 %collective-permute-start.39 = (f32[16,32,128]{2,1,0:T(8,128)S(1)}, f32[16,32,128]{2,1,0:T(8,128)S(1)}, u32[]{:S(2)}, u32[]{:S(2)}) collective-permute-start(f32[16,32,128]{2,1,0:T(8,128)S(1)} %fusion.3.refs_1_), channel_id=1, source_target_pairs={{0,8},{8,16},{16,24},{24,0},{1,9},{9,17},{17,25},{25,1},{2,10},{10... | collective-permute-start | bytes 786440 | tf_op jit(solution)/shard_map/ppermute | solution.py:398
  206.3 33.2 %collective-permute-start.44 = (f32[16,32,128]{2,1,0:T(8,128)S(1)}, f32[16,32,128]{2,1,0:T(8,128)S(1)}, u32[]{:S(2)}, u32[]{:S(2)}) collective-permute-start(f32[16,32,128]{2,1,0:T(8,128)S(1)} %fusion.2.refs_2_), channel_id=1, source_target_pairs={{0,24},{8,0},{16,8},{24,16},{1,25},{9,1},{17,9},{25,17},{2,26},{10... | collective-permute-start | bytes 786440 | tf_op jit(solution)/shard_map/ppermute | solution.py:398
  208.2 40.4 %collective-permute-start.42 = (f32[16,32,128]{2,1,0:T(8,128)S(1)}, f32[16,32,128]{2,1,0:T(8,128)S(1)}, u32[]{:S(2)}, u32[]{:S(2)}) collective-permute-start(f32[16,32,128]{2,1,0:T(8,128)S(1)} %fusion.2.refs_2_), channel_id=1, source_target_pairs={{0,16},{8,24},{16,0},{24,8},{1,17},{9,25},{17,1},{25,9},{2,18},{10... | collective-permute-start | bytes 786440 | tf_op jit(solution)/shard_map/ppermute | solution.py:398
  208.6 40.1 %collective-permute-start.40 = (f32[16,32,128]{2,1,0:T(8,128)S(1)}, f32[16,32,128]{2,1,0:T(8,128)S(1)}, u32[]{:S(2)}, u32[]{:S(2)}) collective-permute-start(f32[16,32,128]{2,1,0:T(8,128)S(1)} %fusion.2.refs_2_), channel_id=1, source_target_pairs={{0,8},{8,16},{16,24},{24,0},{1,9},{9,17},{17,25},{25,1},{2,10},{10... | collective-permute-start | bytes 786440 | tf_op jit(solution)/shard_map/ppermute | solution.py:398
  (57 other events, 547.2 us)

commit v2 on v1

v2 whole, which is shorter than its diff:
```python
import jax
import jax.numpy as jnp
from jax import lax
from jax.experimental import pallas as pl
from jax.experimental.pallas import tpu as pltpu
from jax.sharding import PartitionSpec as P

ITERS = 2
WIRE = jnp.int16
FULL = 32000.0
F32 = jnp.float32
BF16 = jnp.bfloat16


def split(x):
    hi = x.astype(BF16)
    return hi, (x - hi.astype(F32)).astype(BF16)


def split_outside(x):
    hi = lax.reduce_precision(x, 8, 7)
    return hi.astype(BF16), lax.reduce_precision(x - hi, 8, 7).astype(BF16)


def dot(a, b):
    return lax.dot_general(a, b, (((1,), (0,)), ((), ())), preferred_element_type=F32)


def band(taps, rows, cols):
    count = taps.shape[0]
    index = rows[:, None] - cols[None, :] + count // 2
    hit = index[:, :, None] == jnp.arange(count, dtype=jnp.int32)
    return jnp.sum(jnp.where(hit, taps, 0.0), axis=-1)


def crop_rows(ref, r, shift_y, shift_z, tile_y, tile_z, stage):
    brick_y, brick_z = ref.shape[1:]
    base = pl.multiple_of(jnp.minimum(shift_y // 8, (brick_y - tile_y) // 8 - 1) * 8, 8)
    value = ref[r, pl.ds(base, tile_y + 8), :]
    stage[...] = pltpu.roll(value, lax.rem(brick_z - shift_z, brick_z), 1)[:, :tile_z]
    return stage[pl.ds(shift_y - base, tile_y), :]


def first_crop(shifts, estimate, tile_y, tile_z):
    rows, brick_y, brick_z = estimate.shape

    def kernel(shift_ref, est_ref, out_ref, stage, crops):
        def step(r, carry):
            crops[pl.ds(r, tile_y, stride=rows), :] = crop_rows(
                est_ref, r, shift_ref[0, 0], shift_ref[0, 1], tile_y, tile_z, stage
            )
            return carry

        lax.fori_loop(0, rows, step, 0, unroll=4)
        out_ref[...] = crops[...].astype(BF16).reshape(tile_y, rows, tile_z)

    return pl.pallas_call(
        kernel,
        out_shape=jax.ShapeDtypeStruct((tile_y, rows, tile_z), BF16),
        in_specs=[
            pl.BlockSpec(memory_space=pltpu.SMEM),
            pl.BlockSpec(memory_space=pltpu.VMEM),
        ],
        out_specs=pl.BlockSpec(memory_space=pltpu.VMEM),
        scratch_shapes=[
            pltpu.VMEM((tile_y + 8, tile_z), F32),
            pltpu.VMEM((tile_y * rows, tile_z), F32),
        ],
        name="first_crop",
    )(shifts, estimate)


def code(x):
    return (x + 0.5).astype(jnp.int32).astype(WIRE)


def read_tile(pieces, measured, pattern, gather_mat, scatter_mat, z_mat, y_mat, slots):
    owners = len(pieces)
    rows, tile_z = pieces[0][0].shape[1:]
    tile_y = sum(p.shape[0] for p in pieces[0])
    half = tile_y // 2
    tile_x = measured.shape[0] // tile_y
    flat = [p for parts in pieces for p in parts]
    n_flat = len(flat)
    firsts = [sum(len(p) for p in pieces[:k]) for k in range(owners)]
    n_send = owners // 2
    group = y_mat.shape[1] // 2
    per_group = group // tile_y
    groups = tile_x // per_group

    def kernel(*refs):
        g_refs = refs[:n_flat]
        m_ref, pat_ref, gm_ref, sm_ref, zm_ref, ym_ref = refs[n_flat : n_flat + 6]
        outs = refs[n_flat + 6 : n_flat + 10]
        buf = refs[n_flat + 10]
        for h in range(2):

            def line(k, y, h=h):
                if len(pieces[k]) == 2:
                    return g_refs[firsts[k] + h][y]
                return g_refs[firsts[k]][h * half + y]

            def gather(i, carry, h=h, line=line):
                y = i * 2
                both = jnp.concatenate(
                    [
                        jnp.concatenate([line(k, y), line(k, y + 1)], axis=1)
                        for k in range(owners)
                    ],
                    axis=0,
                )
                got = dot(gm_ref[...], both)
                got = got[:tile_x] + got[tile_x:]
                stacked = jnp.concatenate([got[:, :tile_z], got[:, tile_z:]], axis=0)
                hi, lo = split(stacked)
                out = dot(jnp.concatenate([hi, lo], axis=1), zm_ref[...])
                out = out[:, :tile_z] + out[:, tile_z:]
                buf[pl.ds(h * half + y, tile_x, stride=tile_y), :] = out[:tile_x]
                buf[pl.ds(h * half + y + 1, tile_x, stride=tile_y), :] = out[tile_x:]
                return carry

            lax.fori_loop(0, half // 2, gather, 0, unroll=2)

        def divide(i, carry):
            at = pl.multiple_of(i * 2 * group, 2 * group)
            first = buf[pl.ds(at, group), :]
            second = buf[pl.ds(at + group, group), :]
            hi, lo = split(jnp.concatenate([first, second], axis=1))
            out = dot(ym_ref[...], jnp.concatenate([hi, lo], axis=0))
            out = out[:group] + out[group:]
            data = m_ref[pl.ds(at, 2 * group), :].astype(F32)
            pat = pat_ref[...]
            buf[pl.ds(at, group), :] = data[:group] * pat / out[:, :tile_z]
            buf[pl.ds(at + group, group), :] = data[group:] * pat / out[:, tile_z:]
            return carry

        lax.fori_loop(0, groups // 2, divide, 0, unroll=2)

        for h in range(2):
            send_ref, keep_ref = outs[2 * h], outs[2 * h + 1]

            def put(y, sums, send_ref=send_ref, keep_ref=keep_ref, h=h):
                for k in range(owners):
                    block = sums[k * rows : (k + 1) * rows]
                    slot = slots[h][k]
                    if slot < n_send:
                        send_ref[slot, y] = code(block)
                    else:
                        keep_ref[slot - n_send, y] = block

            def scatter(i, carry, h=h, put=put):
                y = i * 2
                first = buf[pl.ds(h * half + y, tile_x, stride=tile_y), :]
                second = buf[pl.ds(h * half + y + 1, tile_x, stride=tile_y), :]
                hi, lo = split(jnp.concatenate([first, second], axis=1))
                out = dot(sm_ref[...], jnp.concatenate([hi, lo], axis=0))
                out = out[: owners * rows] + out[owners * rows :]
                put(y, out[:, :tile_z])
                put(y + 1, out[:, tile_z:])
                return carry

            lax.fori_loop(0, half // 2, scatter, 0, unroll=2)

    vmem = pl.BlockSpec(memory_space=pltpu.VMEM)
    shapes = []
    for h in range(2):
        for dtype in (WIRE, F32):
            shapes.append(jax.ShapeDtypeStruct((n_send, half, rows, tile_z), dtype))
    return pl.pallas_call(
        kernel,
        out_shape=tuple(shapes),
        in_specs=[vmem] * (n_flat + 6),
        out_specs=(vmem,) * 4,
        scratch_shapes=[pltpu.VMEM((tile_x * tile_y, tile_z), F32)],
        name="read_tile",
    )(*flat, measured, pattern, gather_mat, scatter_mat, z_mat, y_mat)


def update(
    scalars, sums, estimate, unit, z_place, y_place, outline, row_weight, tile_y, tile_z, last
):
    views = len(sums)
    rows, brick_y, brick_z = estimate.shape
    half = tile_y // 2
    flat = [p for pair in sums for p in pair]

    def kernel(*refs):
        s_ref = refs[0]
        in_refs = refs[1 : 1 + 2 * views]
        est_ref, un_ref, zp_ref, yp_ref, pat_ref, rw_ref = refs[1 + 2 * views : 7 + 2 * views]
        rest = refs[7 + 2 * views :]
        out_ref = rest[0]
        crop_ref = None if last else rest[1]
        placed, stage, crops = rest[-3:]
        me = s_ref[2]
        for s in range(views):
            view = lax.rem(me + views - s, views)
            for h in range(2):
                src = in_refs[2 * s + h]
                x = src[...].astype(jnp.int32).astype(F32) * un_ref[view][None]
                x = x.reshape(half * rows, tile_z)
                hi, lo = split(x)
                out = dot(jnp.concatenate([hi, lo], axis=1), zp_ref[view, 0])
                out = out + dot(hi, zp_ref[view, 1, :tile_z, :])
                at = pl.multiple_of((view * 2 + h) * half * rows, half * rows)
                for j in range(brick_z // tile_z):
                    placed[j, pl.ds(at, half * rows), :] = out[:, j * tile_z : (j + 1) * tile_z]

        def step(r, carry):
            x = jnp.concatenate(
                [
                    placed[j, pl.ds(r, views * tile_y, stride=rows), :]
                    for j in range(brick_z // tile_z)
                ],
                axis=1,
            )
            hi, lo = split(x)
            out = dot(yp_ref[...], jnp.concatenate([hi, lo], axis=0))
            correction = out[:brick_y] + out[brick_y:]
            weight = jnp.zeros((brick_y, brick_z), F32)
            for v in range(views):
                factor = rw_ref[v, pl.ds(r, 1), :]
                factor = jnp.concatenate([factor] * (brick_z // factor.shape[1]), axis=1)
                weight = weight + factor * pat_ref[v]
            value = est_ref[r] * (1.0 + correction) / (1.0 + weight)
            out_ref[r] = value
            if not last:
                crops[pl.ds(r, tile_y, stride=rows), :] = crop_rows(
                    out_ref, r, s_ref[0], s_ref[1], tile_y, tile_z, stage
                )
            return carry

        lax.fori_loop(0, rows, step, 0, unroll=2)
        if not last:
            crop_ref[...] = crops[...].astype(BF16).reshape(tile_y, rows, tile_z)

    vmem = pl.BlockSpec(memory_space=pltpu.VMEM)
    shapes = [jax.ShapeDtypeStruct(estimate.shape, F32)]
    if not last:
        shapes.append(jax.ShapeDtypeStruct((tile_y, rows, tile_z), BF16))
    return pl.pallas_call(
        kernel,
        out_shape=tuple(shapes),
        in_specs=[pl.BlockSpec(memory_space=pltpu.SMEM)] + [vmem] * (2 * views + 6),
        out_specs=(vmem,) * len(shapes),
        scratch_shapes=[
            pltpu.VMEM((brick_z // tile_z, views * tile_y * rows, tile_z), F32),
            pltpu.VMEM((tile_y + 8, tile_z), F32),
            pltpu.VMEM((tile_y * rows, tile_z), F32),
        ],
        name="update",
    )(scalars, *flat, estimate, unit, z_place, y_place, outline, row_weight)


def flip(x, bit, count):
    return lax.ppermute(x, "brick", [(i, i ^ bit) for i in range(count)])


def gather_owners(crop, count):
    half = crop.shape[0] // 2
    bits = [1 << i for i in range(count.bit_length() - 1)]
    wide = bits[1:]
    got = {0: (crop,)}
    if len(wide) == 2:
        x, y = wide
        got[x] = (flip(crop, x, count),)
        got[y] = (flip(crop, y, count),)
        got[x | y] = (flip(got[x][0][:half], y, count), flip(got[y][0][half:], x, count))
        wide = []
    for bit in wide + [1]:
        for k in list(got):
            got[k ^ bit] = tuple(flip(p, bit, count) for p in got[k])
    return [got[k] for k in range(count)]


def halving_orders(count):
    bits = [1 << i for i in range(count.bit_length() - 1)]
    orders = [bits, bits[:1] + bits[:0:-1]]
    slots = []
    for order in orders:
        place = {}
        for k in range(count):
            slot = 0
            for bit in order:
                slot = slot * 2 + (0 if k & bit else 1)
            place[k] = slot
        slots.append(place)
    return orders, slots


def on_device(
    estimate, views_data, psf_taps, seg_owner, seg_local, seg_offset, seg_extent, view_shift
):
    per_owner, brick_x, brick_y, brick_z = estimate.shape
    tile_x, tile_y, tile_z = views_data.shape[2:]
    own_rows = per_owner * brick_x
    owners = lax.axis_size("brick")
    views = lax.axis_size("view")
    me = lax.axis_index("brick")
    my_view = lax.axis_index("view")
    highest = lax.Precision.HIGHEST

    flat = estimate.reshape(own_rows, brick_y, brick_z)
    crop = first_crop(view_shift, flat, tile_y, tile_z)
    shifts = view_shift[0]
    scalars = jnp.concatenate([shifts, my_view[None].astype(jnp.int32)])

    taps = psf_taps[0] / jnp.sum(psf_taps[0], axis=1, keepdims=True)
    count = taps.shape[1]
    tile_rows = jnp.arange(tile_x, dtype=jnp.int32)
    tile_cols = jnp.arange(tile_z, dtype=jnp.int32)
    tile_mids = jnp.arange(tile_y, dtype=jnp.int32)
    extent = seg_extent[0, 0]
    seg_ids = jnp.arange(extent.shape[0], dtype=jnp.int32)
    starts = jnp.sum(jnp.where(seg_ids[None, :] < seg_ids[:, None], extent[None, :], 0), axis=1)
    inside = (starts[None, :] <= tile_rows[:, None]) & (
        tile_rows[:, None] < (starts + extent)[None, :]
    )
    in_owner = seg_local[0, 0] * brick_x + seg_offset[0, 0] - starts
    all_rows = jnp.arange(owners * own_rows, dtype=jnp.int32)[None, :]

    def picks(owner):
        base = owner * own_rows + in_owner
        source = jnp.sum(jnp.where(inside, base[None, :], 0), axis=1) + tile_rows
        return (source[:, None] == all_rows).astype(F32)

    owner = seg_owner[0, 0, :, 0]
    x_mat = band(taps[0], tile_rows, tile_rows)
    y_band = band(taps[1], tile_mids, tile_mids)
    z_band = band(taps[2], tile_cols, tile_cols)
    x_mass = jnp.sum(x_mat, axis=0)

    lanes = 128
    totals = jnp.stack(
        [jnp.sum(x_mat, axis=1), jnp.sum(x_mat / x_mass[None, :], axis=1)], axis=0
    )
    picked = picks(owner)
    table = jnp.sum(totals[:, :, None] * picked[None], axis=1).reshape(-1, lanes)
    table_rows = table.shape[0]
    table = jnp.pad(table, ((0, -table_rows % 8), (0, 0)))
    for bit in [1 << i for i in range(owners.bit_length() - 1)]:
        table = table + flip(table, bit, owners)
    table = table[:table_rows].reshape(2, owners, own_rows)
    owner_ids = jnp.arange(owners, dtype=jnp.int32)
    mine_rows = jnp.sum(jnp.where((owner_ids == me)[None, :, None], table, 0.0), axis=1)
    relative = (owner_ids[:, None] ^ me) == owner_ids[None, :]
    bound_rows = jnp.sum(
        jnp.where(relative[:, :, None], table[1][None], 0.0), axis=1
    ).reshape(-1)
    to_code = jnp.where(bound_rows > 0.0, FULL / jnp.maximum(bound_rows, 1e-30), 0.0)

    meta = jnp.concatenate(
        [
            jnp.pad(taps, ((0, 0), (0, lanes - count))),
            jnp.pad(shifts.astype(F32), (0, lanes - 2))[None],
            jnp.pad(mine_rows, ((0, 0), (0, lanes - own_rows))),
            jnp.zeros((2, lanes), F32),
        ],
        axis=0,
    )
    around = [meta] + [
        lax.ppermute(meta, "view", [(i, (i + s) % views) for i in range(views)])
        for s in range(1, views)
    ]
    view_ids = jnp.arange(views, dtype=jnp.int32)
    steps_back = lax.rem(my_view - view_ids + views, views)
    metas = sum(
        jnp.where((steps_back == s)[:, None, None], around[s][None], 0.0) for s in range(views)
    )
    all_shifts = metas[:, 3, :2].astype(jnp.int32)
    row_weight = jnp.broadcast_to(metas[:, 4, :own_rows, None], (views, own_rows, lanes))
    row_unit = jnp.broadcast_to(metas[:, 5, :own_rows, None], (views, own_rows, lanes))

    relative_picks = picks(owner ^ me)
    rows_mat = jnp.einsum("tw,tr->wr", x_mat, relative_picks, precision=highest)
    hi, lo = split_outside(rows_mat)
    gather_mat = jnp.concatenate([hi, lo], axis=0)
    hi, lo = split_outside(rows_mat.T * to_code[:, None])
    scatter_mat = jnp.concatenate(
        [jnp.concatenate([hi, hi], axis=1), jnp.concatenate([lo, lo], axis=1)], axis=0
    )
    hi, lo = split_outside(z_band)
    pair = jnp.concatenate([hi, lo], axis=1)
    z_mat = jnp.concatenate([pair, pair], axis=0)
    per_group = max(1, 128 // tile_y)
    y_mat = jnp.kron(jnp.eye(per_group, dtype=F32), y_band.T)
    hi, lo = split_outside(y_mat)
    y_mat = jnp.concatenate(
        [jnp.concatenate([hi, hi], axis=1), jnp.concatenate([lo, lo], axis=1)], axis=0
    )
    mass = jnp.sum(y_band, axis=0)[:, None] * jnp.sum(z_band, axis=0)[None, :]
    mass = jnp.tile(mass, (per_group, 1))

    def placing(values, shift, long, short):
        at = jnp.arange(long, dtype=jnp.int32) - shift
        ids = jnp.arange(short, dtype=jnp.int32)
        mat = band(values, at, ids)
        mat = jnp.where(((at >= 0) & (at < short))[:, None], mat, 0.0)
        return mat, jnp.sum(band(values, ids, ids), axis=0)

    z_all, z_mass = jax.vmap(lambda m, s: placing(m[2, :count], s[1], brick_z, tile_z))(
        metas, all_shifts
    )
    y_all, y_mass = jax.vmap(lambda m, s: placing(m[1, :count], s[0], brick_y, tile_y))(
        metas, all_shifts
    )
    outline = jnp.sum(y_all, axis=2)[:, :, None] * jnp.sum(z_all, axis=2)[:, None, :]
    z_all = jnp.transpose(z_all / z_mass[:, None, :], (0, 2, 1))
    hi, lo = split_outside(z_all)
    z_place = jnp.stack(
        [jnp.concatenate([hi, hi], axis=1), jnp.concatenate([lo, lo], axis=1)], axis=1
    )
    y_wide = jnp.transpose(y_all / y_mass[:, None, :], (1, 0, 2)).reshape(
        brick_y, views * tile_y
    )
    hi, lo = split_outside(y_wide)
    y_place = jnp.concatenate(
        [jnp.concatenate([hi, hi], axis=1), jnp.concatenate([lo, lo], axis=1)], axis=0
    )
    measured = views_data.reshape(tile_x * tile_y, tile_z)
    orders, slots = halving_orders(owners)

    current = flat
    for sweep in range(ITERS):
        last = sweep == ITERS - 1
        bound = 4.04 if sweep == 0 else 16.8
        pieces = gather_owners(crop, owners)
        outs = read_tile(
            pieces, measured, mass / bound, gather_mat, scatter_mat, z_mat, y_mat, slots
        )
        send = [outs[0], outs[2]]
        keep = [outs[1], outs[3]]
        for i in range(len(orders[0])):
            for h in range(2):
                total = keep[h] + flip(send[h], orders[h][i], owners).astype(F32)
                left = total.shape[0] // 2
                send[h] = code(total[:left]) if left else None
                keep[h] = total[left:]
        mine = [code(k[0]) for k in keep]
        sums = [tuple(mine)] + [
            tuple(
                lax.ppermute(p, "view", [(i, (i + s) % views) for i in range(views)])
                for p in mine
            )
            for s in range(1, views)
        ]
        result = update(
            scalars,
            sums,
            current,
            row_unit * (bound / FULL),
            z_place,
            y_place,
            outline,
            row_weight,
            tile_y,
            tile_z,
            last,
        )
        current = result[0]
        if not last:
            crop = result[1]
    return current.reshape(estimate.shape)


def solution(mesh):
    placed = (
        P("brick", None, None, None),
        P("view", "brick", None, None, None),
        P("view", None, None),
        P("view", "brick", None, None),
        P("view", "brick", None),
        P("view", "brick", None),
        P("view", "brick", None),
        P("view", None),
    )
    return jax.shard_map(
        on_device,
        mesh=mesh,
        in_specs=placed,
        out_specs=P("brick", None, None, None),
        check_vma=False,
    )
```

time: 260 us -> 196 us (0.75)
  waiting for transfers between devices: 120 us -> 68.3 us
  local copies, waits for them, and re-layouts: 15.4 us -> 5.62 us
  starting transfers between devices: 54.2 us -> 45.6 us
  other arithmetic: 15.7 us -> 22.4 us
    ppermute x12, waiting for transfers between devices: 67 us -> 25.6 us  [on_device(): lax.ppermute(p, 'view', [(i, (i + s) % views) for i in range(views)])]
    ppermute x30 -> x33, waiting for transfers between devices: 53.3 us -> 41.7 us  [flip(): return lax.ppermute(x, 'brick', [(i, i ^ bit) for i in range(count)])]
    ppermute x12, starting transfers between devices: 30.7 us -> 19.6 us  [on_device(): lax.ppermute(p, 'view', [(i, (i + s) % views) for i in range(views)])]
    slice x21 -> x6, local copies, waits for them, and re-layouts: 10.7 us -> 0.05 us  [the longest x2 0.02 us: gather_owners(): got[y][0][half:]]
    reduce_sum x3 -> x10, other arithmetic: 0.23 us -> 5.37 us  [the longest x2 2.41 us: placing(): return (mat, jnp.sum(band(values, ids, ids), axis=0))]
    unnamed x72 -> x98, local copies, waits for them, and re-layouts: 3.63 us -> 0.36 us
    ppermute x30 -> x33, starting transfers between devices: 17.4 us -> 20.5 us  [flip(): return lax.ppermute(x, 'brick', [(i, i ^ bit) for i in range(count)])]
  transfers between devices with their start and end apart: 45 -> 48, of which waited for: 18 -> 22; matrix products, arithmetic and copies ran while one was open for 10% -> 12% of each run, Pallas kernels for 1% -> 0%
where the time goes in v2:
time: 196 us; the launch traced here: 195 us
  waiting for transfers between devices  68.3 us (35%)
  Pallas kernels  51.9 us (26%)
  starting transfers between devices  45.6 us (23%)
  other arithmetic  22.4 us (11%)
  local copies, waits for them, and re-layouts  5.62 us (3%)
    ppermute x33, waiting for transfers between devices, flip(): return lax.ppermute(x, 'brick', [(i, i ^ bit) for i in range(count)])  41.7 us
    pallas_call x2, Pallas kernels, read_tile(): pl.pallas_call(kernel, out_shape=tuple(shapes), in_specs=[vmem] * (n_flat...  25.8 us
    ppermute x12, waiting for transfers between devices, on_device(): lax.ppermute(p, 'view', [(i, (i + s) % views) for i in range(views)])  25.6 us
    pallas_call x2, Pallas kernels, update(): pl.pallas_call(kernel, out_shape=tuple(shapes), in_specs=[pl.BlockSpec(me...  22.3 us
    ppermute x33, starting transfers between devices, flip(): return lax.ppermute(x, 'brick', [(i, i ^ bit) for i in range(count)])  20.5 us
    ppermute x12, starting transfers between devices, on_device(): lax.ppermute(p, 'view', [(i, (i + s) % views) for i in range(views)])  19.6 us
    ppermute x3, starting transfers between devices, on_device(): lax.ppermute(meta, 'view', [(i, (i + s) % views) for i in range(views)])  5.52 us
  transfers between devices with their start and end apart: 48, of which 22 were waited for; matrix products, arithmetic and copies ran while one was open for 12% of the time, Pallas kernels for 0%

profile of v2, /device:TPU:0, one launch (start us, length us, event | category | flops | bytes accessed | tf_op | source)
XLA Modules:
  0.0 195.1 jit_solution(2192329249087817177)
XLA Ops:
  0.0 3.8 %first_crop.1.refs_0_ = bf16[32,32,128]{2,1,0:T(8,128)(2,1)} custom-call(s32[1,2]{1,0:T(1,128)} %shift_ref.1, f32[32,64,256]{2,1,0:T(8,128)} %bitcast.74), custom_call_target="tpu_custom_call" | custom-call | tf_op jit(solution)/shard_map/first_crop/pallas_call | solution.py:57
  3.8 3.0 %collective-permute-start.1 = (bf16[32,32,128]{2,1,0:T(8,128)(2,1)}, bf16[32,32,128]{2,1,0:T(8,128)(2,1)S(1)}, u32[]{:S(2)}, u32[]{:S(2)}) collective-permute-start(bf16[32,32,128]{2,1,0:T(8,128)(2,1)} %first_crop.1.refs_0_), channel_id=1, source_target_pairs={{0,2},{1,3},{2,0},{3,1},{4,6},{5,7},{6,4},{7,5},{8,10},{9,11},{10,... | collective-permute-start | bytes 786440 | tf_op jit(solution)/shard_map/ppermute | solution.py:256
  14.8 3.1 %collective-permute-done.10 = f32[8,128]{1,0:T(8,128)S(1)} collective-permute-done((f32[8,128]{1,0:T(8,128)S(1)}, f32[8,128]{1,0:T(8,128)S(1)}, u32[]{:S(2)}, u32[]{:S(2)}) %collective-permute-start.10) | collective-permute-done | bytes 4128 | tf_op jit(solution)/shard_map/ppermute | solution.py:256
  23.3 2.6 %collective-permute-start.25 = (f32[8,128]{1,0:T(8,128)S(1)}, f32[8,128]{1,0:T(8,128)S(1)}, u32[]{:S(2)}, u32[]{:S(2)}) collective-permute-start(f32[8,128]{1,0:T(8,128)S(1)} %fusion.49), channel_id=1, source_target_pairs={{0,16},{8,24},{16,0},{24,8},{1,17},{9,25},{17,1},{25,9},{2,18},{10... | collective-permute-start | bytes 12296 | tf_op jit(solution)/shard_map/ppermute | solution.py:362
  38.5 2.7 %collective-permute-done.5.refs_6_ = bf16[16,32,128]{2,1,0:T(8,128)(2,1)S(1)} collective-permute-done((bf16[16,32,128]{2,1,0:T(8,128)(2,1)S(1)}, bf16[16,32,128]{2,1,0:T(8,128)(2,1)S(1)}, u32[]{:S(2)}, u32[]{:S(2)}) %collective-permute-start.5) | collective-permute-done | bytes 131104 | tf_op jit(solution)/shard_map/ppermute | solution.py:256
  44.6 12.9 %read_tile.2 = (s16[4,16,32,128]{3,2,1,0:T(8,128)(2,1)}, f32[4,16,32,128]{3,2,1,0:T(8,128)}, s16[4,16,32,128]{3,2,1,0:T(8,128)(2,1)}, f32[4,16,32,128]{3,2,1,0:T(8,128)}) custom-call(bf16[32,32,128]{2,1,0:T(8,128)(2,1)} %first_crop.1.refs_0_, bf16[32,32,128]{2,1,0:T(8,128)(2,1)} %copy-done.11, bf16[32,32,128]{2,1,0:T(8,128)(2,1)} %copy-done.3, ...), custom_call_target="tpu_custom_call" | custom-call | tf_op jit(solution)/shard_map/read_tile/pallas_call | solution.py:169
  64.3 6.3 %collective-permute-done.16 = s16[2,16,32,128]{3,2,1,0:T(8,128)(2,1)S(1)} collective-permute-done((s16[2,16,32,128]{3,2,1,0:T(8,128)(2,1)S(1)}, s16[2,16,32,128]{3,2,1,0:T(8,128)(2,1)S(1)}, u32[]{:S(2)}, u32[]{:S(2)}) %collective-permute-start.16) | collective-permute-done | bytes 262176 | tf_op jit(solution)/shard_map/ppermute | solution.py:256
  73.0 2.8 %collective-permute-done.17 = s16[1,16,32,128]{3,2,1,0:T(8,128)(2,1)S(1)} collective-permute-done((s16[1,16,32,128]{3,2,1,0:T(8,128)(2,1)S(1)}, s16[1,16,32,128]{3,2,1,0:T(8,128)(2,1)S(1)}, u32[]{:S(2)}, u32[]{:S(2)}) %collective-permute-start.17) | collective-permute-done | bytes 131104 | tf_op jit(solution)/shard_map/ppermute | solution.py:256
  76.2 3.4 %collective-permute-start.21 = (s16[16,32,128]{2,1,0:T(8,128)(2,1)S(1)}, s16[16,32,128]{2,1,0:T(8,128)(2,1)S(1)}, u32[]{:S(2)}, u32[]{:S(2)}) collective-permute-start(s16[16,32,128]{2,1,0:T(8,128)(2,1)S(1)} %fusion.33.refs_2_), channel_id=1, source_target_pairs={{0,16},{8,24},{16,0},{24,8},{1,17},{9,25},{17,1},{25,9},{2,18},{10... | collective-permute-start | bytes 393224 | tf_op jit(solution)/shard_map/ppermute | solution.py:442
  84.2 2.7 %collective-permute-start.22 = (s16[16,32,128]{2,1,0:T(8,128)(2,1)S(1)}, s16[16,32,128]{2,1,0:T(8,128)(2,1)S(1)}, u32[]{:S(2)}, u32[]{:S(2)}) collective-permute-start(s16[16,32,128]{2,1,0:T(8,128)(2,1)S(1)} %fusion.32.refs_1_), channel_id=1, source_target_pairs={{0,24},{8,0},{16,8},{24,16},{1,25},{9,1},{17,9},{25,17},{2,26},{10... | collective-permute-start | bytes 393224 | tf_op jit(solution)/shard_map/ppermute | solution.py:442
  87.9 3.2 %collective-permute-done.21.refs_6_ = s16[16,32,128]{2,1,0:T(8,128)(2,1)S(1)} collective-permute-done((s16[16,32,128]{2,1,0:T(8,128)(2,1)S(1)}, s16[16,32,128]{2,1,0:T(8,128)(2,1)S(1)}, u32[]{:S(2)}, u32[]{:S(2)}) %collective-permute-start.21) | collective-permute-done | bytes 131104 | tf_op jit(solution)/shard_map/ppermute | solution.py:442
  92.5 6.3 %collective-permute-done.20.refs_5_ = s16[16,32,128]{2,1,0:T(8,128)(2,1)S(1)} collective-permute-done((s16[16,32,128]{2,1,0:T(8,128)(2,1)S(1)}, s16[16,32,128]{2,1,0:T(8,128)(2,1)S(1)}, u32[]{:S(2)}, u32[]{:S(2)}) %collective-permute-start.20) | collective-permute-done | bytes 131104 | tf_op jit(solution)/shard_map/ppermute | solution.py:442
  100.3 12.1 %update.2 = (f32[32,64,256]{2,1,0:T(8,128)}, bf16[32,32,128]{2,1,0:T(8,128)(2,1)}) custom-call(s32[3]{0:T(128)} %pad_add_fusion.1.refs_0_, s16[16,32,128]{2,1,0:T(8,128)(2,1)} %copy-done.10, s16[16,32,128]{2,1,0:T(8,128)(2,1)} %copy-done.8, s16[16,32,128]{2,1,0:T(8,128)(2,1)} %copy-done.30, s16[16,32,128]{2,1,0:T(8,128)(2,1)} %copy-done.21, ...), custom_call_target="tpu_custom_call" | custom-call | tf_op jit(solution)/shard_map/update/pallas_call | solution.py:241
  114.5 6.0 %collective-permute-done.28.refs_2_ = bf16[32,32,128]{2,1,0:T(8,128)(2,1)S(1)} collective-permute-done((bf16[32,32,128]{2,1,0:T(8,128)(2,1)}, bf16[32,32,128]{2,1,0:T(8,128)(2,1)S(1)}, u32[]{:S(2)}, u32[]{:S(2)}) %collective-permute-start.28) | collective-permute-done | bytes 262176 | tf_op jit(solution)/shard_map/ppermute | solution.py:256
  125.6 2.6 %collective-permute-done.33.refs_7_ = bf16[16,32,128]{2,1,0:T(8,128)(2,1)S(1)} collective-permute-done((bf16[16,32,128]{2,1,0:T(8,128)(2,1)S(1)}, bf16[16,32,128]{2,1,0:T(8,128)(2,1)S(1)}, u32[]{:S(2)}, u32[]{:S(2)}) %collective-permute-start.33) | collective-permute-done | bytes 131104 | tf_op jit(solution)/shard_map/ppermute | solution.py:256
  130.3 12.9 %read_tile.3 = (s16[4,16,32,128]{3,2,1,0:T(8,128)(2,1)}, f32[4,16,32,128]{3,2,1,0:T(8,128)}, s16[4,16,32,128]{3,2,1,0:T(8,128)(2,1)}, f32[4,16,32,128]{3,2,1,0:T(8,128)}) custom-call(bf16[32,32,128]{2,1,0:T(8,128)(2,1)} %get-tuple-element.19.refs_0_, bf16[32,32,128]{2,1,0:T(8,128)(2,1)} %copy-done.12, bf16[32,32,128]{2,1,0:T(8,128)(2,1)} %copy-done.5, ...), custom_call_target="tpu_custom_call" | custom-call | tf_op jit(solution)/shard_map/read_tile/pallas_call | solution.py:169
  149.0 6.4 %collective-permute-done.40 = s16[2,16,32,128]{3,2,1,0:T(8,128)(2,1)S(1)} collective-permute-done((s16[2,16,32,128]{3,2,1,0:T(8,128)(2,1)S(1)}, s16[2,16,32,128]{3,2,1,0:T(8,128)(2,1)S(1)}, u32[]{:S(2)}, u32[]{:S(2)}) %collective-permute-start.40) | collective-permute-done | bytes 262176 | tf_op jit(solution)/shard_map/ppermute | solution.py:256
  157.7 2.9 %collective-permute-done.41 = s16[1,16,32,128]{3,2,1,0:T(8,128)(2,1)S(1)} collective-permute-done((s16[1,16,32,128]{3,2,1,0:T(8,128)(2,1)S(1)}, s16[1,16,32,128]{3,2,1,0:T(8,128)(2,1)S(1)}, u32[]{:S(2)}, u32[]{:S(2)}) %collective-permute-start.41) | collective-permute-done | bytes 131104 | tf_op jit(solution)/shard_map/ppermute | solution.py:256
  160.6 3.4 %collective-permute-start.43 = (s16[16,32,128]{2,1,0:T(8,128)(2,1)S(1)}, s16[16,32,128]{2,1,0:T(8,128)(2,1)S(1)}, u32[]{:S(2)}, u32[]{:S(2)}) collective-permute-start(s16[16,32,128]{2,1,0:T(8,128)(2,1)S(1)} %fusion.35.refs_2_), channel_id=1, source_target_pairs={{0,8},{8,16},{16,24},{24,0},{1,9},{9,17},{17,25},{25,1},{2,10},{10... | collective-permute-start | bytes 393224 | tf_op jit(solution)/shard_map/ppermute | solution.py:442
  166.7 2.5 %collective-permute-start.44 = (s16[16,32,128]{2,1,0:T(8,128)(2,1)S(1)}, s16[16,32,128]{2,1,0:T(8,128)(2,1)S(1)}, u32[]{:S(2)}, u32[]{:S(2)}) collective-permute-start(s16[16,32,128]{2,1,0:T(8,128)(2,1)S(1)} %fusion.34.refs_1_), channel_id=1, source_target_pairs={{0,16},{8,24},{16,0},{24,8},{1,17},{9,25},{17,1},{25,9},{2,18},{10... | collective-permute-start | bytes 393224 | tf_op jit(solution)/shard_map/ppermute | solution.py:442
  169.2 2.5 %collective-permute-start.46 = (s16[16,32,128]{2,1,0:T(8,128)(2,1)S(1)}, s16[16,32,128]{2,1,0:T(8,128)(2,1)S(1)}, u32[]{:S(2)}, u32[]{:S(2)}) collective-permute-start(s16[16,32,128]{2,1,0:T(8,128)(2,1)S(1)} %fusion.34.refs_1_), channel_id=1, source_target_pairs={{0,24},{8,0},{16,8},{24,16},{1,25},{9,1},{17,9},{25,17},{2,26},{10... | collective-permute-start | bytes 393224 | tf_op jit(solution)/shard_map/ppermute | solution.py:442
  171.7 5.3 %collective-permute-done.45.refs_6_ = s16[16,32,128]{2,1,0:T(8,128)(2,1)S(1)} collective-permute-done((s16[16,32,128]{2,1,0:T(8,128)(2,1)S(1)}, s16[16,32,128]{2,1,0:T(8,128)(2,1)S(1)}, u32[]{:S(2)}, u32[]{:S(2)}) %collective-permute-start.45) | collective-permute-done | bytes 131104 | tf_op jit(solution)/shard_map/ppermute | solution.py:442
  177.3 6.8 %collective-permute-done.44.refs_5_ = s16[16,32,128]{2,1,0:T(8,128)(2,1)S(1)} collective-permute-done((s16[16,32,128]{2,1,0:T(8,128)(2,1)S(1)}, s16[16,32,128]{2,1,0:T(8,128)(2,1)S(1)}, u32[]{:S(2)}, u32[]{:S(2)}) %collective-permute-start.44) | collective-permute-done | bytes 131104 | tf_op jit(solution)/shard_map/ppermute | solution.py:442
  184.9 10.2 %update.3 = f32[32,64,256]{2,1,0:T(8,128)} custom-call(s32[3]{0:T(128)} %pad_add_fusion.1.refs_0_, s16[16,32,128]{2,1,0:T(8,128)(2,1)} %copy-done.9, s16[16,32,128]{2,1,0:T(8,128)(2,1)} %copy-done.7, s16[16,32,128]{2,1,0:T(8,128)(2,1)} %copy-done.29, s16[16,32,128]{2,1,0:T(8,128)(2,1)} %copy-done.20, s16[16,32,128]{2,1,0:T(8,128)(2,1)} %copy-done.31, ...), custom_call_target="tpu_custom_call" | custom-call | tf_op jit(solution)/shard_map/update/pallas_call | solution.py:241
  (289 shorter events, 67.9 us)
Async XLA Ops:
  3.8 32.3 %collective-permute-start.1 = (bf16[32,32,128]{2,1,0:T(8,128)(2,1)}, bf16[32,32,128]{2,1,0:T(8,128)(2,1)S(1)}, u32[]{:S(2)}, u32[]{:S(2)}) collective-permute-start(bf16[32,32,128]{2,1,0:T(8,128)(2,1)} %first_crop.1.refs_0_), channel_id=1, source_target_pairs={{0,2},{1,3},{2,0},{3,1},{4,6},{5,7},{6,4},{7,5},{8,10},{9,11},{10,... | collective-permute-start | bytes 786440 | tf_op jit(solution)/shard_map/ppermute | solution.py:256
  6.8 29.9 %collective-permute-start.3 = (bf16[32,32,128]{2,1,0:T(8,128)(2,1)}, bf16[32,32,128]{2,1,0:T(8,128)(2,1)S(1)}, u32[]{:S(2)}, u32[]{:S(2)}) collective-permute-start(bf16[32,32,128]{2,1,0:T(8,128)(2,1)} %first_crop.1.refs_0_), channel_id=1, source_target_pairs={{0,4},{1,5},{2,6},{3,7},{4,0},{5,1},{6,2},{7,3},{8,12},{9,13},{10,... | collective-permute-start | bytes 786440 | tf_op jit(solution)/shard_map/ppermute | solution.py:256
  28.5 14.6 %collective-permute-start = (bf16[32,32,128]{2,1,0:T(8,128)(2,1)S(1)}, bf16[32,32,128]{2,1,0:T(8,128)(2,1)S(1)}, u32[]{:S(2)}, u32[]{:S(2)}) collective-permute-start(bf16[32,32,128]{2,1,0:T(8,128)(2,1)S(1)} %copy-done), channel_id=1, source_target_pairs={{0,1},{1,0},{2,3},{3,2},{4,5},{5,4},{6,7},{7,6},{8,9},{9,8},{10,11... | collective-permute-start | bytes 786440 | tf_op jit(solution)/shard_map/ppermute | solution.py:256
  61.8 8.8 %collective-permute-start.16 = (s16[2,16,32,128]{3,2,1,0:T(8,128)(2,1)S(1)}, s16[2,16,32,128]{3,2,1,0:T(8,128)(2,1)S(1)}, u32[]{:S(2)}, u32[]{:S(2)}) collective-permute-start(s16[2,16,32,128]{3,2,1,0:T(8,128)(2,1)S(1)} %fusion.7), channel_id=1, source_target_pairs={{0,4},{1,5},{2,6},{3,7},{4,0},{5,1},{6,2},{7,3},{8,12},{9,13},{10,... | collective-permute-start | bytes 786440 | tf_op jit(solution)/shard_map/ppermute | solution.py:256
  63.7 8.5 %collective-permute-start.13 = (s16[2,16,32,128]{3,2,1,0:T(8,128)(2,1)S(1)}, s16[2,16,32,128]{3,2,1,0:T(8,128)(2,1)S(1)}, u32[]{:S(2)}, u32[]{:S(2)}) collective-permute-start(s16[2,16,32,128]{3,2,1,0:T(8,128)(2,1)S(1)} %fusion.9), channel_id=1, source_target_pairs={{0,2},{1,3},{2,0},{3,1},{4,6},{5,7},{6,4},{7,5},{8,10},{9,11},{10,... | collective-permute-start | bytes 786440 | tf_op jit(solution)/shard_map/ppermute | solution.py:256
  72.3 7.5 %collective-permute-start.14 = (s16[1,16,32,128]{3,2,1,0:T(8,128)(2,1)S(1)}, s16[1,16,32,128]{3,2,1,0:T(8,128)(2,1)S(1)}, u32[]{:S(2)}, u32[]{:S(2)}) collective-permute-start(s16[1,16,32,128]{3,2,1,0:T(8,128)(2,1)S(1)} %fusion.26), channel_id=1, source_target_pairs={{0,4},{1,5},{2,6},{3,7},{4,0},{5,1},{6,2},{7,3},{8,12},{9,13},{10,... | collective-permute-start | bytes 393224 | tf_op jit(solution)/shard_map/ppermute | solution.py:256
  75.9 8.3 %collective-permute-start.19 = (s16[16,32,128]{2,1,0:T(8,128)(2,1)S(1)}, s16[16,32,128]{2,1,0:T(8,128)(2,1)S(1)}, u32[]{:S(2)}, u32[]{:S(2)}) collective-permute-start(s16[16,32,128]{2,1,0:T(8,128)(2,1)S(1)} %fusion.33.refs_2_), channel_id=1, source_target_pairs={{0,8},{8,16},{16,24},{24,0},{1,9},{9,17},{17,25},{25,1},{2,10},{10... | collective-permute-start | bytes 393224 | tf_op jit(solution)/shard_map/ppermute | solution.py:442
  76.2 14.9 %collective-permute-start.21 = (s16[16,32,128]{2,1,0:T(8,128)(2,1)S(1)}, s16[16,32,128]{2,1,0:T(8,128)(2,1)S(1)}, u32[]{:S(2)}, u32[]{:S(2)}) collective-permute-start(s16[16,32,128]{2,1,0:T(8,128)(2,1)S(1)} %fusion.33.refs_2_), channel_id=1, source_target_pairs={{0,16},{8,24},{16,0},{24,8},{1,17},{9,25},{17,1},{25,9},{2,18},{10... | collective-permute-start | bytes 393224 | tf_op jit(solution)/shard_map/ppermute | solution.py:442
  79.6 11.5 %collective-permute-start.23 = (s16[16,32,128]{2,1,0:T(8,128)(2,1)S(1)}, s16[16,32,128]{2,1,0:T(8,128)(2,1)S(1)}, u32[]{:S(2)}, u32[]{:S(2)}) collective-permute-start(s16[16,32,128]{2,1,0:T(8,128)(2,1)S(1)} %fusion.33.refs_2_), channel_id=1, source_target_pairs={{0,24},{8,0},{16,8},{24,16},{1,25},{9,1},{17,9},{25,17},{2,26},{10... | collective-permute-start | bytes 393224 | tf_op jit(solution)/shard_map/ppermute | solution.py:442
  79.9 12.7 %collective-permute-start.18 = (s16[16,32,128]{2,1,0:T(8,128)(2,1)S(1)}, s16[16,32,128]{2,1,0:T(8,128)(2,1)S(1)}, u32[]{:S(2)}, u32[]{:S(2)}) collective-permute-start(s16[16,32,128]{2,1,0:T(8,128)(2,1)S(1)} %fusion.32.refs_1_), channel_id=1, source_target_pairs={{0,8},{8,16},{16,24},{24,0},{1,9},{9,17},{17,25},{25,1},{2,10},{10... | collective-permute-start | bytes 393224 | tf_op jit(solution)/shard_map/ppermute | solution.py:442
  81.8 17.0 %collective-permute-start.20 = (s16[16,32,128]{2,1,0:T(8,128)(2,1)S(1)}, s16[16,32,128]{2,1,0:T(8,128)(2,1)S(1)}, u32[]{:S(2)}, u32[]{:S(2)}) collective-permute-start(s16[16,32,128]{2,1,0:T(8,128)(2,1)S(1)} %fusion.32.refs_1_), channel_id=1, source_target_pairs={{0,16},{8,24},{16,0},{24,8},{1,17},{9,25},{17,1},{25,9},{2,18},{10... | collective-permute-start | bytes 393224 | tf_op jit(solution)/shard_map/ppermute | solution.py:442
  84.2 14.7 %collective-permute-start.22 = (s16[16,32,128]{2,1,0:T(8,128)(2,1)S(1)}, s16[16,32,128]{2,1,0:T(8,128)(2,1)S(1)}, u32[]{:S(2)}, u32[]{:S(2)}) collective-permute-start(s16[16,32,128]{2,1,0:T(8,128)(2,1)S(1)} %fusion.32.refs_1_), channel_id=1, source_target_pairs={{0,24},{8,0},{16,8},{24,16},{1,25},{9,1},{17,9},{25,17},{2,26},{10... | collective-permute-start | bytes 393224 | tf_op jit(solution)/shard_map/ppermute | solution.py:442
  112.5 8.1 %collective-permute-start.28 = (bf16[32,32,128]{2,1,0:T(8,128)(2,1)}, bf16[32,32,128]{2,1,0:T(8,128)(2,1)S(1)}, u32[]{:S(2)}, u32[]{:S(2)}) collective-permute-start(bf16[32,32,128]{2,1,0:T(8,128)(2,1)} %get-tuple-element.19.refs_0_), channel_id=1, source_target_pairs={{0,2},{1,3},{2,0},{3,1},{4,6},{5,7},{6,4},{7,5},{8,10},{9,11},{10,... | collective-permute-start | bytes 786440 | tf_op jit(solution)/shard_map/ppermute | solution.py:256
  112.9 9.3 %collective-permute-start.30 = (bf16[32,32,128]{2,1,0:T(8,128)(2,1)}, bf16[32,32,128]{2,1,0:T(8,128)(2,1)S(1)}, u32[]{:S(2)}, u32[]{:S(2)}) collective-permute-start(bf16[32,32,128]{2,1,0:T(8,128)(2,1)} %get-tuple-element.19.refs_0_), channel_id=1, source_target_pairs={{0,4},{1,5},{2,6},{3,7},{4,0},{5,1},{6,2},{7,3},{8,12},{9,13},{10,... | collective-permute-start | bytes 786440 | tf_op jit(solution)/shard_map/ppermute | solution.py:256
  114.5 13.7 %collective-permute-start.27 = (bf16[32,32,128]{2,1,0:T(8,128)(2,1)}, bf16[32,32,128]{2,1,0:T(8,128)(2,1)S(1)}, u32[]{:S(2)}, u32[]{:S(2)}) collective-permute-start(bf16[32,32,128]{2,1,0:T(8,128)(2,1)} %get-tuple-element.19.refs_0_), channel_id=1, source_target_pairs={{0,1},{1,0},{2,3},{3,2},{4,5},{5,4},{6,7},{7,6},{8,9},{9,8},{10,11... | collective-permute-start | bytes 786440 | tf_op jit(solution)/shard_map/ppermute | solution.py:256
  146.9 8.4 %collective-permute-start.40 = (s16[2,16,32,128]{3,2,1,0:T(8,128)(2,1)S(1)}, s16[2,16,32,128]{3,2,1,0:T(8,128)(2,1)S(1)}, u32[]{:S(2)}, u32[]{:S(2)}) collective-permute-start(s16[2,16,32,128]{3,2,1,0:T(8,128)(2,1)S(1)} %fusion.3), channel_id=1, source_target_pairs={{0,4},{1,5},{2,6},{3,7},{4,0},{5,1},{6,2},{7,3},{8,12},{9,13},{10,... | collective-permute-start | bytes 786440 | tf_op jit(solution)/shard_map/ppermute | solution.py:256
  147.8 8.3 %collective-permute-start.37 = (s16[2,16,32,128]{3,2,1,0:T(8,128)(2,1)S(1)}, s16[2,16,32,128]{3,2,1,0:T(8,128)(2,1)S(1)}, u32[]{:S(2)}, u32[]{:S(2)}) collective-permute-start(s16[2,16,32,128]{3,2,1,0:T(8,128)(2,1)S(1)} %fusion.5), channel_id=1, source_target_pairs={{0,2},{1,3},{2,0},{3,1},{4,6},{5,7},{6,4},{7,5},{8,10},{9,11},{10,... | collective-permute-start | bytes 786440 | tf_op jit(solution)/shard_map/ppermute | solution.py:256
  156.3 10.2 %collective-permute-start.38 = (s16[1,16,32,128]{3,2,1,0:T(8,128)(2,1)S(1)}, s16[1,16,32,128]{3,2,1,0:T(8,128)(2,1)S(1)}, u32[]{:S(2)}, u32[]{:S(2)}) collective-permute-start(s16[1,16,32,128]{3,2,1,0:T(8,128)(2,1)S(1)} %fusion.16), channel_id=1, source_target_pairs={{0,4},{1,5},{2,6},{3,7},{4,0},{5,1},{6,2},{7,3},{8,12},{9,13},{10,... | collective-permute-start | bytes 393224 | tf_op jit(solution)/shard_map/ppermute | solution.py:256
  160.6 8.5 %collective-permute-start.43 = (s16[16,32,128]{2,1,0:T(8,128)(2,1)S(1)}, s16[16,32,128]{2,1,0:T(8,128)(2,1)S(1)}, u32[]{:S(2)}, u32[]{:S(2)}) collective-permute-start(s16[16,32,128]{2,1,0:T(8,128)(2,1)S(1)} %fusion.35.refs_2_), channel_id=1, source_target_pairs={{0,8},{8,16},{16,24},{24,0},{1,9},{9,17},{17,25},{25,1},{2,10},{10... | collective-permute-start | bytes 393224 | tf_op jit(solution)/shard_map/ppermute | solution.py:442
  164.1 12.9 %collective-permute-start.45 = (s16[16,32,128]{2,1,0:T(8,128)(2,1)S(1)}, s16[16,32,128]{2,1,0:T(8,128)(2,1)S(1)}, u32[]{:S(2)}, u32[]{:S(2)}) collective-permute-start(s16[16,32,128]{2,1,0:T(8,128)(2,1)S(1)} %fusion.35.refs_2_), channel_id=1, source_target_pairs={{0,16},{8,24},{16,0},{24,8},{1,17},{9,25},{17,1},{25,9},{2,18},{10... | collective-permute-start | bytes 393224 | tf_op jit(solution)/shard_map/ppermute | solution.py:442
  164.2 12.7 %collective-permute-start.47 = (s16[16,32,128]{2,1,0:T(8,128)(2,1)S(1)}, s16[16,32,128]{2,1,0:T(8,128)(2,1)S(1)}, u32[]{:S(2)}, u32[]{:S(2)}) collective-permute-start(s16[16,32,128]{2,1,0:T(8,128)(2,1)S(1)} %fusion.35.refs_2_), channel_id=1, source_target_pairs={{0,24},{8,0},{16,8},{24,16},{1,25},{9,1},{17,9},{25,17},{2,26},{10... | collective-permute-start | bytes 393224 | tf_op jit(solution)/shard_map/ppermute | solution.py:442
  166.6 10.7 %collective-permute-start.42 = (s16[16,32,128]{2,1,0:T(8,128)(2,1)S(1)}, s16[16,32,128]{2,1,0:T(8,128)(2,1)S(1)}, u32[]{:S(2)}, u32[]{:S(2)}) collective-permute-start(s16[16,32,128]{2,1,0:T(8,128)(2,1)S(1)} %fusion.34.refs_1_), channel_id=1, source_target_pairs={{0,8},{8,16},{16,24},{24,0},{1,9},{9,17},{17,25},{25,1},{2,10},{10... | collective-permute-start | bytes 393224 | tf_op jit(solution)/shard_map/ppermute | solution.py:442
  166.7 17.5 %collective-permute-start.44 = (s16[16,32,128]{2,1,0:T(8,128)(2,1)S(1)}, s16[16,32,128]{2,1,0:T(8,128)(2,1)S(1)}, u32[]{:S(2)}, u32[]{:S(2)}) collective-permute-start(s16[16,32,128]{2,1,0:T(8,128)(2,1)S(1)} %fusion.34.refs_1_), channel_id=1, source_target_pairs={{0,16},{8,24},{16,0},{24,8},{1,17},{9,25},{17,1},{25,9},{2,18},{10... | collective-permute-start | bytes 393224 | tf_op jit(solution)/shard_map/ppermute | solution.py:442
  169.2 15.0 %collective-permute-start.46 = (s16[16,32,128]{2,1,0:T(8,128)(2,1)S(1)}, s16[16,32,128]{2,1,0:T(8,128)(2,1)S(1)}, u32[]{:S(2)}, u32[]{:S(2)}) collective-permute-start(s16[16,32,128]{2,1,0:T(8,128)(2,1)S(1)} %fusion.34.refs_1_), channel_id=1, source_target_pairs={{0,24},{8,0},{16,8},{24,16},{1,25},{9,1},{17,9},{25,17},{2,26},{10... | collective-permute-start | bytes 393224 | tf_op jit(solution)/shard_map/ppermute | solution.py:442
  (73 other events, 489.2 us)

commit v3 on v2

--- a/solution.py
+++ b/solution.py
@@ -6,6 +6,7 @@
 from jax.sharding import PartitionSpec as P
 
 ITERS = 2
+UNROLL = 8
 WIRE = jnp.int16
 FULL = 32000.0
 F32 = jnp.float32
@@ -74,7 +75,7 @@
     return (x + 0.5).astype(jnp.int32).astype(WIRE)
 
 
-def read_tile(pieces, measured, pattern, gather_mat, scatter_mat, z_mat, y_mat, slots):
+def read_tile(pieces, measured, mass, bound, gather_mat, scatter_mat, z_mat, y_mat, slots):
     owners = len(pieces)
     rows, tile_z = pieces[0][0].shape[1:]
     tile_y = sum(p.shape[0] for p in pieces[0])
@@ -119,7 +120,7 @@
                 buf[pl.ds(h * half + y + 1, tile_x, stride=tile_y), :] = out[tile_x:]
                 return carry
 
-            lax.fori_loop(0, half // 2, gather, 0, unroll=2)
+            lax.fori_loop(0, half // 2, gather, 0, unroll=UNROLL)
 
         def divide(i, carry):
             at = pl.multiple_of(i * 2 * group, 2 * group)
@@ -129,12 +130,12 @@
             out = dot(ym_ref[...], jnp.concatenate([hi, lo], axis=0))
             out = out[:group] + out[group:]
             data = m_ref[pl.ds(at, 2 * group), :].astype(F32)
-            pat = pat_ref[...]
+            pat = pat_ref[...] * (1.0 / bound)
             buf[pl.ds(at, group), :] = data[:group] * pat / out[:, :tile_z]
             buf[pl.ds(at + group, group), :] = data[group:] * pat / out[:, tile_z:]
             return carry
 
-        lax.fori_loop(0, groups // 2, divide, 0, unroll=2)
+        lax.fori_loop(0, groups // 2, divide, 0, unroll=UNROLL)
 
         for h in range(2):
             send_ref, keep_ref = outs[2 * h], outs[2 * h + 1]
@@ -159,7 +160,7 @@
                 put(y + 1, out[:, tile_z:])
                 return carry
 
-            lax.fori_loop(0, half // 2, scatter, 0, unroll=2)
+            lax.fori_loop(0, half // 2, scatter, 0, unroll=UNROLL)
 
     vmem = pl.BlockSpec(memory_space=pltpu.VMEM)
     shapes = []
@@ -173,32 +174,29 @@
         out_specs=(vmem,) * 4,
         scratch_shapes=[pltpu.VMEM((tile_x * tile_y, tile_z), F32)],
         name="read_tile",
-    )(*flat, measured, pattern, gather_mat, scatter_mat, z_mat, y_mat)
-
-
-def update(
-    scalars, sums, estimate, unit, z_place, y_place, outline, row_weight, tile_y, tile_z, last
-):
+    )(*flat, measured, mass, gather_mat, scatter_mat, z_mat, y_mat)
+
+
+def update(scalars, sums, estimate, bound, metas, z_place, y_place, outline, tile_y, tile_z, last):
     views = len(sums)
     rows, brick_y, brick_z = estimate.shape
     half = tile_y // 2
-    flat = [p for pair in sums for p in pair]
 
     def kernel(*refs):
         s_ref = refs[0]
-        in_refs = refs[1 : 1 + 2 * views]
-        est_ref, un_ref, zp_ref, yp_ref, pat_ref, rw_ref = refs[1 + 2 * views : 7 + 2 * views]
-        rest = refs[7 + 2 * views :]
+        in_refs = refs[1 : 1 + views]
+        est_ref, me_ref, zp_ref, yp_ref, pat_ref = refs[1 + views : 6 + views]
+        rest = refs[6 + views :]
         out_ref = rest[0]
         crop_ref = None if last else rest[1]
         placed, stage, crops = rest[-3:]
         me = s_ref[2]
         for s in range(views):
             view = lax.rem(me + views - s, views)
+            unit = me_ref[view, 8 + rows : 8 + 2 * rows, :] * (bound / FULL)
             for h in range(2):
-                src = in_refs[2 * s + h]
-                x = src[...].astype(jnp.int32).astype(F32) * un_ref[view][None]
-                x = x.reshape(half * rows, tile_z)
+                x = in_refs[s][h * half : (h + 1) * half].astype(jnp.int32).astype(F32)
+                x = (x * unit[None]).reshape(half * rows, tile_z)
                 hi, lo = split(x)
                 out = dot(jnp.concatenate([hi, lo], axis=1), zp_ref[view, 0])
                 out = out + dot(hi, zp_ref[view, 1, :tile_z, :])
@@ -219,7 +217,7 @@
             correction = out[:brick_y] + out[brick_y:]
             weight = jnp.zeros((brick_y, brick_z), F32)
             for v in range(views):
-                factor = rw_ref[v, pl.ds(r, 1), :]
+                factor = me_ref[v, pl.ds(8 + r, 1), :]
                 factor = jnp.concatenate([factor] * (brick_z // factor.shape[1]), axis=1)
                 weight = weight + factor * pat_ref[v]
             value = est_ref[r] * (1.0 + correction) / (1.0 + weight)
@@ -230,7 +228,7 @@
                 )
             return carry
 
-        lax.fori_loop(0, rows, step, 0, unroll=2)
+        lax.fori_loop(0, rows, step, 0, unroll=UNROLL)
         if not last:
             crop_ref[...] = crops[...].astype(BF16).reshape(tile_y, rows, tile_z)
 
@@ -241,7 +239,7 @@
     return pl.pallas_call(
         kernel,
         out_shape=tuple(shapes),
-        in_specs=[pl.BlockSpec(memory_space=pltpu.SMEM)] + [vmem] * (2 * views + 6),
+        in_specs=[pl.BlockSpec(memory_space=pltpu.SMEM)] + [vmem] * (views + 5),
         out_specs=(vmem,) * len(shapes),
         scratch_shapes=[
             pltpu.VMEM((brick_z // tile_z, views * tile_y * rows, tile_z), F32),
@@ -249,23 +247,31 @@
             pltpu.VMEM((tile_y * rows, tile_z), F32),
         ],
         name="update",
-    )(scalars, *flat, estimate, unit, z_place, y_place, outline, row_weight)
+    )(scalars, *sums, estimate, metas, z_place, y_place, outline)
 
 
 def flip(x, bit, count):
     return lax.ppermute(x, "brick", [(i, i ^ bit) for i in range(count)])
 
 
-def gather_owners(crop, count):
+def over_view(x, steps, count):
+    return lax.ppermute(x, "view", [(i, (i + steps) % count) for i in range(count)])
+
+
+def gather_first(crop, count):
+    wide = [1 << i for i in range(1, count.bit_length() - 1)]
+    return {bit: flip(crop, bit, count) for bit in wide} if len(wide) == 2 else {}
+
+
+def gather_owners(crop, near, count):
     half = crop.shape[0] // 2
-    bits = [1 << i for i in range(count.bit_length() - 1)]
-    wide = bits[1:]
+    wide = [1 << i for i in range(1, count.bit_length() - 1)]
     got = {0: (crop,)}
-    if len(wide) == 2:
+    if near:
         x, y = wide
-        got[x] = (flip(crop, x, count),)
-        got[y] = (flip(crop, y, count),)
-        got[x | y] = (flip(got[x][0][:half], y, count), flip(got[y][0][half:], x, count))
+        got[x | y] = (flip(near[x][:half], y, count), flip(near[y][half:], x, count))
+        got[x] = (near[x],)
+        got[y] = (near[y],)
         wide = []
     for bit in wide + [1]:
         for k in list(got):
@@ -302,6 +308,7 @@
 
     flat = estimate.reshape(own_rows, brick_y, brick_z)
     crop = first_crop(view_shift, flat, tile_y, tile_z)
+    near = gather_first(crop, owners)
     shifts = view_shift[0]
     scalars = jnp.concatenate([shifts, my_view[None].astype(jnp.int32)])
 
@@ -334,12 +341,17 @@
     totals = jnp.stack(
         [jnp.sum(x_mat, axis=1), jnp.sum(x_mat / x_mass[None, :], axis=1)], axis=0
     )
-    picked = picks(owner)
-    table = jnp.sum(totals[:, :, None] * picked[None], axis=1).reshape(-1, lanes)
+    table = jnp.sum(totals[:, :, None] * picks(owner)[None], axis=1).reshape(-1, lanes)
     table_rows = table.shape[0]
     table = jnp.pad(table, ((0, -table_rows % 8), (0, 0)))
-    for bit in [1 << i for i in range(owners.bit_length() - 1)]:
+    bits = [1 << i for i in range(owners.bit_length() - 1)]
+    table = table + flip(table, bits[0], owners)
+    near, table, x_mat, y_band, z_band, owner = lax.optimization_barrier(
+        (near, table, x_mat, y_band, z_band, owner)
+    )
+    for bit in bits[1:]:
         table = table + flip(table, bit, owners)
+    pieces = gather_owners(crop, near, owners)
     table = table[:table_rows].reshape(2, owners, own_rows)
     owner_ids = jnp.arange(owners, dtype=jnp.int32)
     mine_rows = jnp.sum(jnp.where((owner_ids == me)[None, :, None], table, 0.0), axis=1)
@@ -349,28 +361,6 @@
     ).reshape(-1)
     to_code = jnp.where(bound_rows > 0.0, FULL / jnp.maximum(bound_rows, 1e-30), 0.0)
 
-    meta = jnp.concatenate(
-        [
-            jnp.pad(taps, ((0, 0), (0, lanes - count))),
-            jnp.pad(shifts.astype(F32), (0, lanes - 2))[None],
-            jnp.pad(mine_rows, ((0, 0), (0, lanes - own_rows))),
-            jnp.zeros((2, lanes), F32),
-        ],
-        axis=0,
-    )
-    around = [meta] + [
-        lax.ppermute(meta, "view", [(i, (i + s) % views) for i in range(views)])
-        for s in range(1, views)
-    ]
-    view_ids = jnp.arange(views, dtype=jnp.int32)
-    steps_back = lax.rem(my_view - view_ids + views, views)
-    metas = sum(
-        jnp.where((steps_back == s)[:, None, None], around[s][None], 0.0) for s in range(views)
-    )
-    all_shifts = metas[:, 3, :2].astype(jnp.int32)
-    row_weight = jnp.broadcast_to(metas[:, 4, :own_rows, None], (views, own_rows, lanes))
-    row_unit = jnp.broadcast_to(metas[:, 5, :own_rows, None], (views, own_rows, lanes))
-
     relative_picks = picks(owner ^ me)
     rows_mat = jnp.einsum("tw,tr->wr", x_mat, relative_picks, precision=highest)
     hi, lo = split_outside(rows_mat)
@@ -391,32 +381,55 @@
     mass = jnp.sum(y_band, axis=0)[:, None] * jnp.sum(z_band, axis=0)[None, :]
     mass = jnp.tile(mass, (per_group, 1))
 
-    def placing(values, shift, long, short):
-        at = jnp.arange(long, dtype=jnp.int32) - shift
-        ids = jnp.arange(short, dtype=jnp.int32)
-        mat = band(values, at, ids)
-        mat = jnp.where(((at >= 0) & (at < short))[:, None], mat, 0.0)
-        return mat, jnp.sum(band(values, ids, ids), axis=0)
-
-    z_all, z_mass = jax.vmap(lambda m, s: placing(m[2, :count], s[1], brick_z, tile_z))(
-        metas, all_shifts
-    )
-    y_all, y_mass = jax.vmap(lambda m, s: placing(m[1, :count], s[0], brick_y, tile_y))(
-        metas, all_shifts
-    )
-    outline = jnp.sum(y_all, axis=2)[:, :, None] * jnp.sum(z_all, axis=2)[:, None, :]
-    z_all = jnp.transpose(z_all / z_mass[:, None, :], (0, 2, 1))
-    hi, lo = split_outside(z_all)
-    z_place = jnp.stack(
-        [jnp.concatenate([hi, hi], axis=1), jnp.concatenate([lo, lo], axis=1)], axis=1
-    )
-    y_wide = jnp.transpose(y_all / y_mass[:, None, :], (1, 0, 2)).reshape(
-        brick_y, views * tile_y
-    )
-    hi, lo = split_outside(y_wide)
-    y_place = jnp.concatenate(
-        [jnp.concatenate([hi, hi], axis=1), jnp.concatenate([lo, lo], axis=1)], axis=0
-    )
+    def view_metas(taps, shifts, mine_rows):
+        meta = jnp.concatenate(
+            [
+                jnp.pad(taps, ((0, 0), (0, lanes - count))),
+                jnp.pad(shifts.astype(F32), (0, lanes - 2))[None],
+                jnp.zeros((4, lanes), F32),
+                jnp.broadcast_to(mine_rows.reshape(-1, 1), (2 * own_rows, lanes)),
+            ],
+            axis=0,
+        )
+        around = [meta] + [over_view(meta, s, views) for s in range(1, views)]
+        view_ids = jnp.arange(views, dtype=jnp.int32)
+        steps_back = lax.rem(my_view - view_ids + views, views)
+        return sum(
+            jnp.where((steps_back == s)[:, None, None], around[s][None], 0.0)
+            for s in range(views)
+        )
+
+    def view_tables(metas):
+        all_shifts = metas[:, 3, :2].astype(jnp.int32)
+
+        def placing(values, shift, long, short):
+            at = jnp.arange(long, dtype=jnp.int32) - shift
+            ids = jnp.arange(short, dtype=jnp.int32)
+            mat = band(values, at, ids)
+            mat = jnp.where(((at >= 0) & (at < short))[:, None], mat, 0.0)
+            return mat, jnp.sum(band(values, ids, ids), axis=0)
+
+        z_all, z_mass = jax.vmap(lambda m, s: placing(m[2, :count], s[1], brick_z, tile_z))(
+            metas, all_shifts
+        )
+        y_all, y_mass = jax.vmap(lambda m, s: placing(m[1, :count], s[0], brick_y, tile_y))(
+            metas, all_shifts
+        )
+        outline = jnp.sum(y_all, axis=2)[:, :, None] * jnp.sum(z_all, axis=2)[:, None, :]
+        z_all = jnp.transpose(z_all / z_mass[:, None, :], (0, 2, 1))
+        hi, lo = split_outside(z_all)
+        z_place = jnp.stack(
+            [jnp.concatenate([hi, hi], axis=1), jnp.concatenate([lo, lo], axis=1)], axis=1
+        )
+        y_wide = jnp.transpose(y_all / y_mass[:, None, :], (1, 0, 2)).reshape(
+            brick_y, views * tile_y
+        )
+        hi, lo = split_outside(y_wide)
+        y_place = jnp.concatenate(
+            [jnp.concatenate([hi, hi], axis=1), jnp.concatenate([lo, lo], axis=1)], axis=0
+        )
+        return metas, z_place, y_place, outline
+
     measured = views_data.reshape(tile_x * tile_y, tile_z)
     orders, slots = halving_orders(owners)
 
@@ -424,9 +437,10 @@
     for sweep in range(ITERS):
         last = sweep == ITERS - 1
         bound = 4.04 if sweep == 0 else 16.8
-        pieces = gather_owners(crop, owners)
+        if sweep:
+            pieces = gather_owners(crop, gather_first(crop, owners), owners)
         outs = read_tile(
-            pieces, measured, mass / bound, gather_mat, scatter_mat, z_mat, y_mat, slots
+            pieces, measured, mass, bound, gather_mat, scatter_mat, z_mat, y_mat, slots
         )
         send = [outs[0], outs[2]]
         keep = [outs[1], outs[3]]
@@ -436,27 +450,17 @@
                 left = total.shape[0] // 2
                 send[h] = code(total[:left]) if left else None
                 keep[h] = total[left:]
-        mine = [code(k[0]) for k in keep]
-        sums = [tuple(mine)] + [
-            tuple(
-                lax.ppermute(p, "view", [(i, (i + s) % views) for i in range(views)])
-                for p in mine
-            )
-            for s in range(1, views)
-        ]
-        result = update(
-            scalars,
-            sums,
-            current,
-            row_unit * (bound / FULL),
-            z_place,
-            y_place,
-            outline,
-            row_weight,
-            tile_y,
-            tile_z,
-            last,
-        )
+            if sweep == 0 and i == 0:
+                send, keep, late = lax.optimization_barrier(
+                    (send, keep, (taps, shifts, mine_rows))
+                )
+                metas = view_metas(*late)
+        mine = jnp.concatenate([code(k[0]) for k in keep], axis=0)
+        if sweep == 0:
+            mine, metas = lax.optimization_barrier((mine, metas))
+            tables = view_tables(metas)
+        sums = [mine] + [over_view(mine, s, views) for s in range(1, views)]
+        result = update(scalars, sums, current, bound, *tables, tile_y, tile_z, last)
         current = result[0]
         if not last:
             crop = result[1]

time: 196 us -> 175 us (0.89)
  Pallas kernels: 51.9 us -> 39.7 us
  starting transfers between devices: 45.6 us -> 33.7 us
  waiting for transfers between devices: 68.3 us -> 76.7 us
  other arithmetic: 22.4 us -> 18.4 us
    ppermute x15 -> x9, starting transfers between devices: 25.1 us -> 12 us  [over_view(): lax.ppermute(x, 'view', [(i, (i + steps) % count) for i in range(count)])]
    pallas_call x2, Pallas kernels: 25.8 us -> 18 us  [read_tile(): pl.pallas_call(kernel, out_shape=tuple(shapes), in_specs=[vmem] * (n_flat...]
    ppermute x15 -> x9, waiting for transfers between devices: 26.6 us -> 33.8 us  [over_view(): lax.ppermute(x, 'view', [(i, (i + steps) % count) for i in range(count)])]
    pallas_call x2, Pallas kernels: 22.3 us -> 17.8 us  [update(): pl.pallas_call(kernel, out_shape=tuple(shapes), in_specs=[pl.BlockSpec(me...]
    unnamed x98 -> x70, local copies, waits for them, and re-layouts: 0.36 us -> 3.37 us
    broadcast_in_dim x5 -> x3, local copies, waits for them, and re-layouts: 2.15 us -> 0.09 us  [the longest x1 0.08 us: view_metas(): jnp.broadcast_to(mine_rows.reshape(-1, 1), (2 * own_rows, lanes))]
  transfers between devices with their start and end apart: 48 -> 42, of which waited for: 22 -> 28; matrix products, arithmetic and copies ran while one was open for 12% -> 11% of each run, Pallas kernels for 0% -> 0%
where the time goes in v3:
time: 175 us
  waiting for transfers between devices  76.7 us (44%)
  Pallas kernels  39.7 us (23%)
  starting transfers between devices  33.7 us (19%)
  other arithmetic  18.4 us (11%)
  local copies, waits for them, and re-layouts  5.3 us (3%)
    ppermute x33, waiting for transfers between devices, flip(): return lax.ppermute(x, 'brick', [(i, i ^ bit) for i in range(count)])  43 us
    ppermute x9, waiting for transfers between devices, over_view(): lax.ppermute(x, 'view', [(i, (i + steps) % count) for i in range(count)])  33.8 us
    ppermute x33, starting transfers between devices, flip(): return lax.ppermute(x, 'brick', [(i, i ^ bit) for i in range(count)])  21.7 us
    pallas_call x2, Pallas kernels, read_tile(): pl.pallas_call(kernel, out_shape=tuple(shapes), in_specs=[vmem] * (n_flat...  18 us
    pallas_call x2, Pallas kernels, update(): pl.pallas_call(kernel, out_shape=tuple(shapes), in_specs=[pl.BlockSpec(me...  17.8 us
    ppermute x9, starting transfers between devices, over_view(): lax.ppermute(x, 'view', [(i, (i + steps) % count) for i in range(count)])  12 us
    pallas_call x1, Pallas kernels, first_crop(): pl.pallas_call(kernel, out_shape=jax.ShapeDtypeStruct((tile_y, rows, tile...  3.79 us
    add x8, other arithmetic, on_device(): total = keep[h] + flip(send[h], orders[h][i], owners).astype(F32)  3.76 us
  transfers between devices with their start and end apart: 42, of which 28 were waited for; matrix products, arithmetic and copies ran while one was open for 11% of the time, Pallas kernels for 0%

profile of v3, /device:TPU:0, one launch (start us, length us, event | category | flops | bytes accessed | tf_op | source)
XLA Modules:
  0.0 174.8 jit_solution(911503456038243514)
XLA Ops:
  0.0 3.8 %first_crop.1.refs_0_ = bf16[32,32,128]{2,1,0:T(8,128)(2,1)} custom-call(s32[1,2]{1,0:T(1,128)} %shift_ref.1, f32[32,64,256]{2,1,0:T(8,128)} %bitcast.62), custom_call_target="tpu_custom_call" | custom-call | tf_op jit(solution)/shard_map/first_crop/pallas_call | solution.py:58
  3.8 3.0 %collective-permute-start.2 = (bf16[32,32,128]{2,1,0:T(8,128)(2,1)}, bf16[32,32,128]{2,1,0:T(8,128)(2,1)S(1)}, u32[]{:S(2)}, u32[]{:S(2)}) collective-permute-start(bf16[32,32,128]{2,1,0:T(8,128)(2,1)} %first_crop.1.refs_0_), channel_id=1, source_target_pairs={{0,4},{1,5},{2,6},{3,7},{4,0},{5,1},{6,2},{7,3},{8,12},{9,13},{10,... | collective-permute-start | bytes 786440 | tf_op jit(solution)/shard_map/ppermute | solution.py:254
  11.1 2.2 %collective-permute-done.2.refs_4_ = bf16[32,32,128]{2,1,0:T(8,128)(2,1)S(1)} collective-permute-done((bf16[32,32,128]{2,1,0:T(8,128)(2,1)}, bf16[32,32,128]{2,1,0:T(8,128)(2,1)S(1)}, u32[]{:S(2)}, u32[]{:S(2)}) %collective-permute-start.2) | collective-permute-done | bytes 262176 | tf_op jit(solution)/shard_map/ppermute | solution.py:254
  23.3 1.7 collective-permute-done.7.refs_7_
  25.0 2.2 %collective-permute-done.6.refs_6_ = bf16[16,32,128]{2,1,0:T(8,128)(2,1)S(1)} collective-permute-done((bf16[16,32,128]{2,1,0:T(8,128)(2,1)S(1)}, bf16[16,32,128]{2,1,0:T(8,128)(2,1)S(1)}, u32[]{:S(2)}, u32[]{:S(2)}) %collective-permute-start.6) | collective-permute-done | bytes 131104 | tf_op jit(solution)/shard_map/ppermute | solution.py:254
  29.4 9.0 %read_tile.2 = (s16[4,16,32,128]{3,2,1,0:T(8,128)(2,1)}, f32[4,16,32,128]{3,2,1,0:T(8,128)}, s16[4,16,32,128]{3,2,1,0:T(8,128)(2,1)}, f32[4,16,32,128]{3,2,1,0:T(8,128)}) custom-call(bf16[32,32,128]{2,1,0:T(8,128)(2,1)} %first_crop.1.refs_0_, bf16[32,32,128]{2,1,0:T(8,128)(2,1)} %copy-done.9, bf16[32,32,128]{2,1,0:T(8,128)(2,1)} %copy-done.6, ...), custom_call_target="tpu_custom_call" | custom-call | tf_op jit(solution)/shard_map/read_tile/pallas_call | solution.py:170
  43.2 3.6 %collective-permute-start.20 = (f32[72,128]{1,0:T(8,128)S(1)}, f32[72,128]{1,0:T(8,128)S(1)}, u32[]{:S(2)}, u32[]{:S(2)}) collective-permute-start(f32[72,128]{1,0:T(8,128)S(1)} %fusion.47), channel_id=1, source_target_pairs={{0,24},{8,0},{16,8},{24,16},{1,25},{9,1},{17,9},{25,17},{2,26},{10... | collective-permute-start | bytes 110600 | tf_op jit(solution)/shard_map/ppermute | solution.py:258
  52.7 2.8 %collective-permute-done.14 = s16[2,16,32,128]{3,2,1,0:T(8,128)(2,1)S(1)} collective-permute-done((s16[2,16,32,128]{3,2,1,0:T(8,128)(2,1)S(1)}, s16[2,16,32,128]{3,2,1,0:T(8,128)(2,1)S(1)}, u32[]{:S(2)}, u32[]{:S(2)}) %collective-permute-start.14) | collective-permute-done | bytes 262176 | tf_op jit(solution)/shard_map/ppermute | solution.py:254
  58.0 2.7 %collective-permute-done.15 = s16[1,16,32,128]{3,2,1,0:T(8,128)(2,1)S(1)} collective-permute-done((s16[1,16,32,128]{3,2,1,0:T(8,128)(2,1)S(1)}, s16[1,16,32,128]{3,2,1,0:T(8,128)(2,1)S(1)}, u32[]{:S(2)}, u32[]{:S(2)}) %collective-permute-start.15) | collective-permute-done | bytes 131104 | tf_op jit(solution)/shard_map/ppermute | solution.py:254
  60.7 2.1 %collective-permute-done.17 = s16[1,16,32,128]{3,2,1,0:T(8,128)(2,1)S(1)} collective-permute-done((s16[1,16,32,128]{3,2,1,0:T(8,128)(2,1)S(1)}, s16[1,16,32,128]{3,2,1,0:T(8,128)(2,1)S(1)}, u32[]{:S(2)}, u32[]{:S(2)}) %collective-permute-start.17) | collective-permute-done | bytes 131104 | tf_op jit(solution)/shard_map/ppermute | solution.py:254
  63.5 2.9 %collective-permute-start.23 = (s16[32,32,128]{2,1,0:T(8,128)(2,1)S(1)}, s16[32,32,128]{2,1,0:T(8,128)(2,1)S(1)}, u32[]{:S(2)}, u32[]{:S(2)}) collective-permute-start(s16[32,32,128]{2,1,0:T(8,128)(2,1)S(1)} %pad_add_fusion.refs_1_), channel_id=1, source_target_pairs={{0,24},{8,0},{16,8},{24,16},{1,25},{9,1},{17,9},{25,17},{2,26},{10... | collective-permute-start | bytes 786440 | tf_op jit(solution)/shard_map/ppermute | solution.py:258
  68.8 1.9 %select_reduce_fusion.1 = f32[4,128]{1,0:T(4,128)S(1)} fusion(f32[4,31]{1,0:T(4,128)S(1)} %bitcast.70, pred[128,128,31]{1,0,2:T(8,128)(4,1)S(1)} %iota_compare_fusion.2), kind=kLoop, calls=%fused_computation.2 | loop fusion | flops 4062720 | bytes 510448 | tf_op jit(solution)/shard_map/vmap()/reduce_sum | solution.py:410
  75.4 12.1 %collective-permute-done.22.refs_3_ = s16[32,32,128]{2,1,0:T(8,128)(2,1)S(1)} collective-permute-done((s16[32,32,128]{2,1,0:T(8,128)(2,1)S(1)}, s16[32,32,128]{2,1,0:T(8,128)(2,1)S(1)}, u32[]{:S(2)}, u32[]{:S(2)}) %collective-permute-start.22) | collective-permute-done | bytes 262176 | tf_op jit(solution)/shard_map/ppermute | solution.py:258
  88.9 9.4 %update.2 = (f32[32,64,256]{2,1,0:T(8,128)}, bf16[32,32,128]{2,1,0:T(8,128)(2,1)}) custom-call(s32[3]{0:T(128)} %pad_add_fusion.3.refs_0_, s16[32,32,128]{2,1,0:T(8,128)(2,1)} %copy-done.1, s16[32,32,128]{2,1,0:T(8,128)(2,1)} %copy-done.17, s16[32,32,128]{2,1,0:T(8,128)(2,1)} %copy-done.16, s16[32,32,128]{2,1,0:T(8,128)(2,1)} %copy-done.15, ...), custom_call_target="tpu_custom_call" | custom-call | tf_op jit(solution)/shard_map/update/pallas_call | solution.py:239
  100.3 4.6 %collective-permute-done.27.refs_4_ = bf16[32,32,128]{2,1,0:T(8,128)(2,1)S(1)} collective-permute-done((bf16[32,32,128]{2,1,0:T(8,128)(2,1)}, bf16[32,32,128]{2,1,0:T(8,128)(2,1)S(1)}, u32[]{:S(2)}, u32[]{:S(2)}) %collective-permute-start.27) | collective-permute-done | bytes 262176 | tf_op jit(solution)/shard_map/ppermute | solution.py:254
  108.2 1.8 %collective-permute-done.30.refs_7_ = bf16[16,32,128]{2,1,0:T(8,128)(2,1)S(1)} collective-permute-done((bf16[16,32,128]{2,1,0:T(8,128)(2,1)S(1)}, bf16[16,32,128]{2,1,0:T(8,128)(2,1)S(1)}, u32[]{:S(2)}, u32[]{:S(2)}) %collective-permute-start.30) | collective-permute-done | bytes 131104 | tf_op jit(solution)/shard_map/ppermute | solution.py:254
  110.0 2.8 %collective-permute-done.29.refs_6_ = bf16[16,32,128]{2,1,0:T(8,128)(2,1)S(1)} collective-permute-done((bf16[16,32,128]{2,1,0:T(8,128)(2,1)S(1)}, bf16[16,32,128]{2,1,0:T(8,128)(2,1)S(1)}, u32[]{:S(2)}, u32[]{:S(2)}) %collective-permute-start.29) | collective-permute-done | bytes 131104 | tf_op jit(solution)/shard_map/ppermute | solution.py:254
  114.9 9.0 %read_tile.3 = (s16[4,16,32,128]{3,2,1,0:T(8,128)(2,1)}, f32[4,16,32,128]{3,2,1,0:T(8,128)}, s16[4,16,32,128]{3,2,1,0:T(8,128)(2,1)}, f32[4,16,32,128]{3,2,1,0:T(8,128)}) custom-call(bf16[32,32,128]{2,1,0:T(8,128)(2,1)} %get-tuple-element.51.refs_0_, bf16[32,32,128]{2,1,0:T(8,128)(2,1)} %copy-done.12, bf16[32,32,128]{2,1,0:T(8,128)(2,1)} %copy-done.8, ...), custom_call_target="tpu_custom_call" | custom-call | tf_op jit(solution)/shard_map/read_tile/pallas_call | solution.py:170
  129.8 6.2 %collective-permute-done.34 = s16[2,16,32,128]{3,2,1,0:T(8,128)(2,1)S(1)} collective-permute-done((s16[2,16,32,128]{3,2,1,0:T(8,128)(2,1)S(1)}, s16[2,16,32,128]{3,2,1,0:T(8,128)(2,1)S(1)}, u32[]{:S(2)}, u32[]{:S(2)}) %collective-permute-start.34) | collective-permute-done | bytes 262176 | tf_op jit(solution)/shard_map/ppermute | solution.py:254
  138.4 2.9 %collective-permute-done.35 = s16[1,16,32,128]{3,2,1,0:T(8,128)(2,1)S(1)} collective-permute-done((s16[1,16,32,128]{3,2,1,0:T(8,128)(2,1)S(1)}, s16[1,16,32,128]{3,2,1,0:T(8,128)(2,1)S(1)}, u32[]{:S(2)}, u32[]{:S(2)}) %collective-permute-start.35) | collective-permute-done | bytes 131104 | tf_op jit(solution)/shard_map/ppermute | solution.py:254
  144.3 1.9 %collective-permute-start.39 = (s16[32,32,128]{2,1,0:T(8,128)(2,1)S(1)}, s16[32,32,128]{2,1,0:T(8,128)(2,1)S(1)}, u32[]{:S(2)}, u32[]{:S(2)}) collective-permute-start(s16[32,32,128]{2,1,0:T(8,128)(2,1)S(1)} %pad_add_fusion.1.refs_1_), channel_id=1, source_target_pairs={{0,8},{8,16},{16,24},{24,0},{1,9},{9,17},{17,25},{25,1},{2,10},{10... | collective-permute-start | bytes 786440 | tf_op jit(solution)/shard_map/ppermute | solution.py:258
  146.2 4.4 %collective-permute-done.41.refs_4_ = s16[32,32,128]{2,1,0:T(8,128)(2,1)S(1)} collective-permute-done((s16[32,32,128]{2,1,0:T(8,128)(2,1)S(1)}, s16[32,32,128]{2,1,0:T(8,128)(2,1)S(1)}, u32[]{:S(2)}, u32[]{:S(2)}) %collective-permute-start.41) | collective-permute-done | bytes 262176 | tf_op jit(solution)/shard_map/ppermute | solution.py:258
  150.6 15.0 %collective-permute-done.40.refs_3_ = s16[32,32,128]{2,1,0:T(8,128)(2,1)S(1)} collective-permute-done((s16[32,32,128]{2,1,0:T(8,128)(2,1)S(1)}, s16[32,32,128]{2,1,0:T(8,128)(2,1)S(1)}, u32[]{:S(2)}, u32[]{:S(2)}) %collective-permute-start.40) | collective-permute-done | bytes 262176 | tf_op jit(solution)/shard_map/ppermute | solution.py:258
  166.4 8.4 %update.3 = f32[32,64,256]{2,1,0:T(8,128)} custom-call(s32[3]{0:T(128)} %pad_add_fusion.3.refs_0_, s16[32,32,128]{2,1,0:T(8,128)(2,1)} %copy-done.4, s16[32,32,128]{2,1,0:T(8,128)(2,1)} %copy-done.20, s16[32,32,128]{2,1,0:T(8,128)(2,1)} %copy-done.19, s16[32,32,128]{2,1,0:T(8,128)(2,1)} %copy-done.18, f32[32,64,256]{2,1,0:T(8,128)} %get-tuple-element.56.refs_5_, ...), custom_call_target="tpu_custom_call" | custom-call | tf_op jit(solution)/shard_map/update/pallas_call | solution.py:239
  (252 shorter events, 57.5 us)
Async XLA Ops:
  3.8 9.5 %collective-permute-start.2 = (bf16[32,32,128]{2,1,0:T(8,128)(2,1)}, bf16[32,32,128]{2,1,0:T(8,128)(2,1)S(1)}, u32[]{:S(2)}, u32[]{:S(2)}) collective-permute-start(bf16[32,32,128]{2,1,0:T(8,128)(2,1)} %first_crop.1.refs_0_), channel_id=1, source_target_pairs={{0,4},{1,5},{2,6},{3,7},{4,0},{5,1},{6,2},{7,3},{8,12},{9,13},{10,... | collective-permute-start | bytes 786440 | tf_op jit(solution)/shard_map/ppermute | solution.py:254
  6.8 8.0 %collective-permute-start.1 = (bf16[32,32,128]{2,1,0:T(8,128)(2,1)}, bf16[32,32,128]{2,1,0:T(8,128)(2,1)S(1)}, u32[]{:S(2)}, u32[]{:S(2)}) collective-permute-start(bf16[32,32,128]{2,1,0:T(8,128)(2,1)} %first_crop.1.refs_0_), channel_id=1, source_target_pairs={{0,2},{1,3},{2,0},{3,1},{4,6},{5,7},{6,4},{7,5},{8,10},{9,11},{10,... | collective-permute-start | bytes 786440 | tf_op jit(solution)/shard_map/ppermute | solution.py:254
  8.3 19.9 %collective-permute-start = (bf16[32,32,128]{2,1,0:T(8,128)(2,1)}, bf16[32,32,128]{2,1,0:T(8,128)(2,1)S(1)}, u32[]{:S(2)}, u32[]{:S(2)}) collective-permute-start(bf16[32,32,128]{2,1,0:T(8,128)(2,1)} %first_crop.1.refs_0_), channel_id=1, source_target_pairs={{0,1},{1,0},{2,3},{3,2},{4,5},{5,4},{6,7},{7,6},{8,9},{9,8},{10,11... | collective-permute-start | bytes 786440 | tf_op jit(solution)/shard_map/ppermute | solution.py:254
  16.9 11.7 %collective-permute-start.4 = (bf16[32,32,128]{2,1,0:T(8,128)(2,1)S(1)}, bf16[32,32,128]{2,1,0:T(8,128)(2,1)S(1)}, u32[]{:S(2)}, u32[]{:S(2)}) collective-permute-start(bf16[32,32,128]{2,1,0:T(8,128)(2,1)S(1)} %collective-permute-done.1.refs_2_), channel_id=1, source_target_pairs={{0,1},{1,0},{2,3},{3,2},{4,5},{5,4},{6,7},{7,6},{8,9},{9,8},{10,11... | collective-permute-start | bytes 786440 | tf_op jit(solution)/shard_map/ppermute | solution.py:254
  16.9 11.6 %collective-permute-start.5 = (bf16[32,32,128]{2,1,0:T(8,128)(2,1)S(1)}, bf16[32,32,128]{2,1,0:T(8,128)(2,1)S(1)}, u32[]{:S(2)}, u32[]{:S(2)}) collective-permute-start(bf16[32,32,128]{2,1,0:T(8,128)(2,1)S(1)} %collective-permute-done.2.refs_4_), channel_id=1, source_target_pairs={{0,1},{1,0},{2,3},{3,2},{4,5},{5,4},{6,7},{7,6},{8,9},{9,8},{10,11... | collective-permute-start | bytes 786440 | tf_op jit(solution)/shard_map/ppermute | solution.py:254
  19.8 5.3 %collective-permute-start.7 = (bf16[16,32,128]{2,1,0:T(8,128)(2,1)S(1)}, bf16[16,32,128]{2,1,0:T(8,128)(2,1)S(1)}, u32[]{:S(2)}, u32[]{:S(2)}) collective-permute-start(bf16[16,32,128]{2,1,0:T(8,128)(2,1)S(1)} %slice.100), channel_id=1, source_target_pairs={{0,2},{1,3},{2,0},{3,1},{4,6},{5,7},{6,4},{7,5},{8,10},{9,11},{10,... | collective-permute-start | bytes 393224 | tf_op jit(solution)/shard_map/ppermute | solution.py:254
  43.2 7.2 %collective-permute-start.20 = (f32[72,128]{1,0:T(8,128)S(1)}, f32[72,128]{1,0:T(8,128)S(1)}, u32[]{:S(2)}, u32[]{:S(2)}) collective-permute-start(f32[72,128]{1,0:T(8,128)S(1)} %fusion.47), channel_id=1, source_target_pairs={{0,24},{8,0},{16,8},{24,16},{1,25},{9,1},{17,9},{25,17},{2,26},{10... | collective-permute-start | bytes 110600 | tf_op jit(solution)/shard_map/ppermute | solution.py:258
  46.8 5.8 %collective-permute-start.18 = (f32[72,128]{1,0:T(8,128)S(1)}, f32[72,128]{1,0:T(8,128)S(1)}, u32[]{:S(2)}, u32[]{:S(2)}) collective-permute-start(f32[72,128]{1,0:T(8,128)S(1)} %fusion.47), channel_id=1, source_target_pairs={{0,8},{8,16},{16,24},{24,0},{1,9},{9,17},{17,25},{25,1},{2,10},{10... | collective-permute-start | bytes 110600 | tf_op jit(solution)/shard_map/ppermute | solution.py:258
  47.8 7.6 %collective-permute-start.14 = (s16[2,16,32,128]{3,2,1,0:T(8,128)(2,1)S(1)}, s16[2,16,32,128]{3,2,1,0:T(8,128)(2,1)S(1)}, u32[]{:S(2)}, u32[]{:S(2)}) collective-permute-start(s16[2,16,32,128]{3,2,1,0:T(8,128)(2,1)S(1)} %get-tuple-element.43), channel_id=1, source_target_pairs={{0,2},{1,3},{2,0},{3,1},{4,6},{5,7},{6,4},{7,5},{8,10},{9,11},{10,... | collective-permute-start | bytes 786440 | tf_op jit(solution)/shard_map/ppermute | solution.py:254
  49.9 7.8 %collective-permute-start.16 = (s16[2,16,32,128]{3,2,1,0:T(8,128)(2,1)S(1)}, s16[2,16,32,128]{3,2,1,0:T(8,128)(2,1)S(1)}, u32[]{:S(2)}, u32[]{:S(2)}) collective-permute-start(s16[2,16,32,128]{3,2,1,0:T(8,128)(2,1)S(1)} %get-tuple-element.45), channel_id=1, source_target_pairs={{0,4},{1,5},{2,6},{3,7},{4,0},{5,1},{6,2},{7,3},{8,12},{9,13},{10,... | collective-permute-start | bytes 786440 | tf_op jit(solution)/shard_map/ppermute | solution.py:254
  63.5 11.9 %collective-permute-start.23 = (s16[32,32,128]{2,1,0:T(8,128)(2,1)S(1)}, s16[32,32,128]{2,1,0:T(8,128)(2,1)S(1)}, u32[]{:S(2)}, u32[]{:S(2)}) collective-permute-start(s16[32,32,128]{2,1,0:T(8,128)(2,1)S(1)} %pad_add_fusion.refs_1_), channel_id=1, source_target_pairs={{0,24},{8,0},{16,8},{24,16},{1,25},{9,1},{17,9},{25,17},{2,26},{10... | collective-permute-start | bytes 786440 | tf_op jit(solution)/shard_map/ppermute | solution.py:258
  66.3 21.1 %collective-permute-start.22 = (s16[32,32,128]{2,1,0:T(8,128)(2,1)S(1)}, s16[32,32,128]{2,1,0:T(8,128)(2,1)S(1)}, u32[]{:S(2)}, u32[]{:S(2)}) collective-permute-start(s16[32,32,128]{2,1,0:T(8,128)(2,1)S(1)} %pad_add_fusion.refs_1_), channel_id=1, source_target_pairs={{0,16},{8,24},{16,0},{24,8},{1,17},{9,25},{17,1},{25,9},{2,18},{10... | collective-permute-start | bytes 786440 | tf_op jit(solution)/shard_map/ppermute | solution.py:258
  67.5 20.0 %collective-permute-start.21 = (s16[32,32,128]{2,1,0:T(8,128)(2,1)S(1)}, s16[32,32,128]{2,1,0:T(8,128)(2,1)S(1)}, u32[]{:S(2)}, u32[]{:S(2)}) collective-permute-start(s16[32,32,128]{2,1,0:T(8,128)(2,1)S(1)} %pad_add_fusion.refs_1_), channel_id=1, source_target_pairs={{0,8},{8,16},{16,24},{24,0},{1,9},{9,17},{17,25},{25,1},{2,10},{10... | collective-permute-start | bytes 786440 | tf_op jit(solution)/shard_map/ppermute | solution.py:258
  98.3 6.6 %collective-permute-start.27 = (bf16[32,32,128]{2,1,0:T(8,128)(2,1)}, bf16[32,32,128]{2,1,0:T(8,128)(2,1)S(1)}, u32[]{:S(2)}, u32[]{:S(2)}) collective-permute-start(bf16[32,32,128]{2,1,0:T(8,128)(2,1)} %get-tuple-element.51.refs_0_), channel_id=1, source_target_pairs={{0,4},{1,5},{2,6},{3,7},{4,0},{5,1},{6,2},{7,3},{8,12},{9,13},{10,... | collective-permute-start | bytes 786440 | tf_op jit(solution)/shard_map/ppermute | solution.py:254
  98.8 8.0 %collective-permute-start.25 = (bf16[32,32,128]{2,1,0:T(8,128)(2,1)}, bf16[32,32,128]{2,1,0:T(8,128)(2,1)S(1)}, u32[]{:S(2)}, u32[]{:S(2)}) collective-permute-start(bf16[32,32,128]{2,1,0:T(8,128)(2,1)} %get-tuple-element.51.refs_0_), channel_id=1, source_target_pairs={{0,2},{1,3},{2,0},{3,1},{4,6},{5,7},{6,4},{7,5},{8,10},{9,11},{10,... | collective-permute-start | bytes 786440 | tf_op jit(solution)/shard_map/ppermute | solution.py:254
  100.3 12.5 %collective-permute-start.24 = (bf16[32,32,128]{2,1,0:T(8,128)(2,1)}, bf16[32,32,128]{2,1,0:T(8,128)(2,1)S(1)}, u32[]{:S(2)}, u32[]{:S(2)}) collective-permute-start(bf16[32,32,128]{2,1,0:T(8,128)(2,1)} %get-tuple-element.51.refs_0_), channel_id=1, source_target_pairs={{0,1},{1,0},{2,3},{3,2},{4,5},{5,4},{6,7},{7,6},{8,9},{9,8},{10,11... | collective-permute-start | bytes 786440 | tf_op jit(solution)/shard_map/ppermute | solution.py:254
  105.2 7.6 %collective-permute-start.28 = (bf16[32,32,128]{2,1,0:T(8,128)(2,1)S(1)}, bf16[32,32,128]{2,1,0:T(8,128)(2,1)S(1)}, u32[]{:S(2)}, u32[]{:S(2)}) collective-permute-start(bf16[32,32,128]{2,1,0:T(8,128)(2,1)S(1)} %collective-permute-done.27.refs_4_), channel_id=1, source_target_pairs={{0,1},{1,0},{2,3},{3,2},{4,5},{5,4},{6,7},{7,6},{8,9},{9,8},{10,11... | collective-permute-start | bytes 786440 | tf_op jit(solution)/shard_map/ppermute | solution.py:254
  106.8 6.0 %collective-permute-start.26 = (bf16[32,32,128]{2,1,0:T(8,128)(2,1)S(1)}, bf16[32,32,128]{2,1,0:T(8,128)(2,1)S(1)}, u32[]{:S(2)}, u32[]{:S(2)}) collective-permute-start(bf16[32,32,128]{2,1,0:T(8,128)(2,1)S(1)} %collective-permute-done.25.refs_2_), channel_id=1, source_target_pairs={{0,1},{1,0},{2,3},{3,2},{4,5},{5,4},{6,7},{7,6},{8,9},{9,8},{10,11... | collective-permute-start | bytes 786440 | tf_op jit(solution)/shard_map/ppermute | solution.py:254
  106.9 5.9 %collective-permute-start.29 = (bf16[16,32,128]{2,1,0:T(8,128)(2,1)S(1)}, bf16[16,32,128]{2,1,0:T(8,128)(2,1)S(1)}, u32[]{:S(2)}, u32[]{:S(2)}) collective-permute-start(bf16[16,32,128]{2,1,0:T(8,128)(2,1)S(1)} %slice.136), channel_id=1, source_target_pairs={{0,4},{1,5},{2,6},{3,7},{4,0},{5,1},{6,2},{7,3},{8,12},{9,13},{10,... | collective-permute-start | bytes 393224 | tf_op jit(solution)/shard_map/ppermute | solution.py:254
  127.6 8.4 %collective-permute-start.34 = (s16[2,16,32,128]{3,2,1,0:T(8,128)(2,1)S(1)}, s16[2,16,32,128]{3,2,1,0:T(8,128)(2,1)S(1)}, u32[]{:S(2)}, u32[]{:S(2)}) collective-permute-start(s16[2,16,32,128]{3,2,1,0:T(8,128)(2,1)S(1)} %fusion.5), channel_id=1, source_target_pairs={{0,2},{1,3},{2,0},{3,1},{4,6},{5,7},{6,4},{7,5},{8,10},{9,11},{10,... | collective-permute-start | bytes 786440 | tf_op jit(solution)/shard_map/ppermute | solution.py:254
  129.5 8.1 %collective-permute-start.37 = (s16[2,16,32,128]{3,2,1,0:T(8,128)(2,1)S(1)}, s16[2,16,32,128]{3,2,1,0:T(8,128)(2,1)S(1)}, u32[]{:S(2)}, u32[]{:S(2)}) collective-permute-start(s16[2,16,32,128]{3,2,1,0:T(8,128)(2,1)S(1)} %fusion.3), channel_id=1, source_target_pairs={{0,4},{1,5},{2,6},{3,7},{4,0},{5,1},{6,2},{7,3},{8,12},{9,13},{10,... | collective-permute-start | bytes 786440 | tf_op jit(solution)/shard_map/ppermute | solution.py:254
  142.9 7.7 %collective-permute-start.41 = (s16[32,32,128]{2,1,0:T(8,128)(2,1)S(1)}, s16[32,32,128]{2,1,0:T(8,128)(2,1)S(1)}, u32[]{:S(2)}, u32[]{:S(2)}) collective-permute-start(s16[32,32,128]{2,1,0:T(8,128)(2,1)S(1)} %pad_add_fusion.1.refs_1_), channel_id=1, source_target_pairs={{0,24},{8,0},{16,8},{24,16},{1,25},{9,1},{17,9},{25,17},{2,26},{10... | collective-permute-start | bytes 786440 | tf_op jit(solution)/shard_map/ppermute | solution.py:258
  143.0 22.7 %collective-permute-start.40 = (s16[32,32,128]{2,1,0:T(8,128)(2,1)S(1)}, s16[32,32,128]{2,1,0:T(8,128)(2,1)S(1)}, u32[]{:S(2)}, u32[]{:S(2)}) collective-permute-start(s16[32,32,128]{2,1,0:T(8,128)(2,1)S(1)} %pad_add_fusion.1.refs_1_), channel_id=1, source_target_pairs={{0,16},{8,24},{16,0},{24,8},{1,17},{9,25},{17,1},{25,9},{2,18},{10... | collective-permute-start | bytes 786440 | tf_op jit(solution)/shard_map/ppermute | solution.py:258
  144.3 21.4 %collective-permute-start.39 = (s16[32,32,128]{2,1,0:T(8,128)(2,1)S(1)}, s16[32,32,128]{2,1,0:T(8,128)(2,1)S(1)}, u32[]{:S(2)}, u32[]{:S(2)}) collective-permute-start(s16[32,32,128]{2,1,0:T(8,128)(2,1)S(1)} %pad_add_fusion.1.refs_1_), channel_id=1, source_target_pairs={{0,8},{8,16},{16,24},{24,0},{1,9},{9,17},{17,25},{25,1},{2,10},{10... | collective-permute-start | bytes 786440 | tf_op jit(solution)/shard_map/ppermute | solution.py:258
  (53 other events, 257.6 us)

commit v4 on v3

--- a/solution.py
+++ b/solution.py
@@ -34,26 +34,32 @@
     return jnp.sum(jnp.where(hit, taps, 0.0), axis=-1)
 
 
-def crop_rows(ref, r, shift_y, shift_z, tile_y, tile_z, stage):
-    brick_y, brick_z = ref.shape[1:]
+def put_crop(out_ref, ref, stage, shift_y, shift_z):
+    rows, brick_y, brick_z = ref.shape
+    tile_y, _, tile_z = out_ref.shape
+    tall = tile_y + 8
     base = pl.multiple_of(jnp.minimum(shift_y // 8, (brick_y - tile_y) // 8 - 1) * 8, 8)
-    value = ref[r, pl.ds(base, tile_y + 8), :]
-    stage[...] = pltpu.roll(value, lax.rem(brick_z - shift_z, brick_z), 1)[:, :tile_z]
-    return stage[pl.ds(shift_y - base, tile_y), :]
+    turn = lax.rem(brick_z - shift_z, brick_z)
+
+    def cut(r, carry):
+        value = ref[r, pl.ds(base, tall), :]
+        at = pl.multiple_of(r * tall, 8)
+        stage[pl.ds(at, tall), :] = pltpu.roll(value, turn, 1)[:, :tile_z]
+        return carry
+
+    def turn_over(y, carry):
+        out_ref[y] = stage[pl.ds(shift_y - base + y, rows, stride=tall), :].astype(BF16)
+        return carry
+
+    lax.fori_loop(0, rows, cut, 0, unroll=8)
+    lax.fori_loop(0, tile_y, turn_over, 0, unroll=8)
 
 
 def first_crop(shifts, estimate, tile_y, tile_z):
-    rows, brick_y, brick_z = estimate.shape
-
-    def kernel(shift_ref, est_ref, out_ref, stage, crops):
-        def step(r, carry):
-            crops[pl.ds(r, tile_y, stride=rows), :] = crop_rows(
-                est_ref, r, shift_ref[0, 0], shift_ref[0, 1], tile_y, tile_z, stage
-            )
-            return carry
-
-        lax.fori_loop(0, rows, step, 0, unroll=4)
-        out_ref[...] = crops[...].astype(BF16).reshape(tile_y, rows, tile_z)
+    rows = estimate.shape[0]
+
+    def kernel(shift_ref, est_ref, out_ref, stage):
+        put_crop(out_ref, est_ref, stage, shift_ref[0, 0], shift_ref[0, 1])
 
     return pl.pallas_call(
         kernel,
@@ -63,10 +69,7 @@
             pl.BlockSpec(memory_space=pltpu.VMEM),
         ],
         out_specs=pl.BlockSpec(memory_space=pltpu.VMEM),
-        scratch_shapes=[
-            pltpu.VMEM((tile_y + 8, tile_z), F32),
-            pltpu.VMEM((tile_y * rows, tile_z), F32),
-        ],
+        scratch_shapes=[pltpu.VMEM((rows * (tile_y + 8), tile_z), F32)],
         name="first_crop",
     )(shifts, estimate)
 
@@ -93,7 +96,7 @@
         g_refs = refs[:n_flat]
         m_ref, pat_ref, gm_ref, sm_ref, zm_ref, ym_ref = refs[n_flat : n_flat + 6]
         outs = refs[n_flat + 6 : n_flat + 10]
-        buf = refs[n_flat + 10]
+        lines, buf = refs[n_flat + 10 :]
         for h in range(2):
 
             def line(k, y, h=h):
@@ -116,16 +119,20 @@
                 hi, lo = split(stacked)
                 out = dot(jnp.concatenate([hi, lo], axis=1), zm_ref[...])
                 out = out[:, :tile_z] + out[:, tile_z:]
-                buf[pl.ds(h * half + y, tile_x, stride=tile_y), :] = out[:tile_x]
-                buf[pl.ds(h * half + y + 1, tile_x, stride=tile_y), :] = out[tile_x:]
+                at = pl.multiple_of((h * half + y) * tile_x, 2 * tile_x)
+                lines[pl.ds(at, 2 * tile_x), :] = out
                 return carry
 
             lax.fori_loop(0, half // 2, gather, 0, unroll=UNROLL)
 
         def divide(i, carry):
             at = pl.multiple_of(i * 2 * group, 2 * group)
-            first = buf[pl.ds(at, group), :]
-            second = buf[pl.ds(at + group, group), :]
+            x = i * 2 * per_group
+            both = [
+                lines[pl.ds(x + j, tile_y, stride=tile_x), :] for j in range(2 * per_group)
+            ]
+            first = jnp.concatenate(both[:per_group], axis=0)
+            second = jnp.concatenate(both[per_group:], axis=0)
             hi, lo = split(jnp.concatenate([first, second], axis=1))
             out = dot(ym_ref[...], jnp.concatenate([hi, lo], axis=0))
             out = out[:group] + out[group:]
@@ -135,7 +142,7 @@
             buf[pl.ds(at + group, group), :] = data[group:] * pat / out[:, tile_z:]
             return carry
 
-        lax.fori_loop(0, groups // 2, divide, 0, unroll=UNROLL)
+        lax.fori_loop(0, groups // 2, divide, 0, unroll=7)
 
         for h in range(2):
             send_ref, keep_ref = outs[2 * h], outs[2 * h + 1]
@@ -172,24 +179,50 @@
         out_shape=tuple(shapes),
         in_specs=[vmem] * (n_flat + 6),
         out_specs=(vmem,) * 4,
-        scratch_shapes=[pltpu.VMEM((tile_x * tile_y, tile_z), F32)],
+        scratch_shapes=[pltpu.VMEM((tile_x * tile_y, tile_z), F32)] * 2,
         name="read_tile",
     )(*flat, measured, mass, gather_mat, scatter_mat, z_mat, y_mat)
 
 
-def update(scalars, sums, estimate, bound, metas, z_place, y_place, outline, tile_y, tile_z, last):
+def over_weight(estimate, metas, outline):
+    rows, brick_y, brick_z = estimate.shape
+    views = metas.shape[0]
+
+    def kernel(est_ref, me_ref, pat_ref, out_ref):
+        def step(r, carry):
+            weight = jnp.ones((brick_y, brick_z), F32)
+            for v in range(views):
+                factor = me_ref[v, pl.ds(8 + r, 1), :]
+                factor = jnp.concatenate([factor] * (brick_z // factor.shape[1]), axis=1)
+                weight = weight + factor * pat_ref[v]
+            out_ref[r] = est_ref[r] / weight
+            return carry
+
+        lax.fori_loop(0, rows, step, 0, unroll=4)
+
+    vmem = pl.BlockSpec(memory_space=pltpu.VMEM)
+    return pl.pallas_call(
+        kernel,
+        out_shape=jax.ShapeDtypeStruct(estimate.shape, F32),
+        in_specs=[vmem] * 3,
+        out_specs=vmem,
+        name="over_weight",
+    )(estimate, metas, outline)
+
+
+def update(scalars, sums, ratio, bound, metas, z_place, y_place, tile_y, tile_z, last):
     views = len(sums)
-    rows, brick_y, brick_z = estimate.shape
+    rows, brick_y, brick_z = ratio.shape
     half = tile_y // 2
 
     def kernel(*refs):
         s_ref = refs[0]
         in_refs = refs[1 : 1 + views]
-        est_ref, me_ref, zp_ref, yp_ref, pat_ref = refs[1 + views : 6 + views]
-        rest = refs[6 + views :]
+        rt_ref, me_ref, zp_ref, yp_ref = refs[1 + views : 5 + views]
+        rest = refs[5 + views :]
         out_ref = rest[0]
         crop_ref = None if last else rest[1]
-        placed, stage, crops = rest[-3:]
+        placed = rest[1] if last else rest[2]
         me = s_ref[2]
         for s in range(views):
             view = lax.rem(me + views - s, views)
@@ -215,39 +248,28 @@
             hi, lo = split(x)
             out = dot(yp_ref[...], jnp.concatenate([hi, lo], axis=0))
             correction = out[:brick_y] + out[brick_y:]
-            weight = jnp.zeros((brick_y, brick_z), F32)
-            for v in range(views):
-                factor = me_ref[v, pl.ds(8 + r, 1), :]
-                factor = jnp.concatenate([factor] * (brick_z // factor.shape[1]), axis=1)
-                weight = weight + factor * pat_ref[v]
-            value = est_ref[r] * (1.0 + correction) / (1.0 + weight)
-            out_ref[r] = value
-            if not last:
-                crops[pl.ds(r, tile_y, stride=rows), :] = crop_rows(
-                    out_ref, r, s_ref[0], s_ref[1], tile_y, tile_z, stage
-                )
+            out_ref[r] = rt_ref[r] * (1.0 + correction)
             return carry
 
         lax.fori_loop(0, rows, step, 0, unroll=UNROLL)
         if not last:
-            crop_ref[...] = crops[...].astype(BF16).reshape(tile_y, rows, tile_z)
+            put_crop(crop_ref, out_ref, rest[3], s_ref[0], s_ref[1])
 
     vmem = pl.BlockSpec(memory_space=pltpu.VMEM)
-    shapes = [jax.ShapeDtypeStruct(estimate.shape, F32)]
+    shapes = [jax.ShapeDtypeStruct(ratio.shape, F32)]
     if not last:
         shapes.append(jax.ShapeDtypeStruct((tile_y, rows, tile_z), BF16))
+    scratch = [pltpu.VMEM((brick_z // tile_z, views * tile_y * rows, tile_z), F32)]
+    if not last:
+        scratch.append(pltpu.VMEM((rows * (tile_y + 8), tile_z), F32))
     return pl.pallas_call(
         kernel,
         out_shape=tuple(shapes),
-        in_specs=[pl.BlockSpec(memory_space=pltpu.SMEM)] + [vmem] * (views + 5),
+        in_specs=[pl.BlockSpec(memory_space=pltpu.SMEM)] + [vmem] * (views + 4),
         out_specs=(vmem,) * len(shapes),
-        scratch_shapes=[
-            pltpu.VMEM((brick_z // tile_z, views * tile_y * rows, tile_z), F32),
-            pltpu.VMEM((tile_y + 8, tile_z), F32),
-            pltpu.VMEM((tile_y * rows, tile_z), F32),
-        ],
+        scratch_shapes=scratch,
         name="update",
-    )(scalars, *sums, estimate, metas, z_place, y_place, outline)
+    )(scalars, *sums, ratio, metas, z_place, y_place)
 
 
 def flip(x, bit, count):
@@ -391,12 +413,14 @@
             ],
             axis=0,
         )
-        around = [meta] + [over_view(meta, s, views) for s in range(1, views)]
+        held = meta[None]
+        for bit in [1 << i for i in range(views.bit_length() - 1)]:
+            other = lax.ppermute(held, "view", [(i, i ^ bit) for i in range(views)])
+            held = jnp.concatenate([held, other], axis=0)
         view_ids = jnp.arange(views, dtype=jnp.int32)
-        steps_back = lax.rem(my_view - view_ids + views, views)
         return sum(
-            jnp.where((steps_back == s)[:, None, None], around[s][None], 0.0)
-            for s in range(views)
+            jnp.where(((view_ids ^ my_view) == j)[:, None, None], held[j][None], 0.0)
+            for j in range(views)
         )
 
     def view_tables(metas):
@@ -428,7 +452,7 @@
         y_place = jnp.concatenate(
             [jnp.concatenate([hi, hi], axis=1), jnp.concatenate([lo, lo], axis=1)], axis=0
         )
-        return metas, z_place, y_place, outline
+        return z_place, y_place, outline
 
     measured = views_data.reshape(tile_x * tile_y, tile_z)
     orders, slots = halving_orders(owners)
@@ -458,9 +482,10 @@
         mine = jnp.concatenate([code(k[0]) for k in keep], axis=0)
         if sweep == 0:
             mine, metas = lax.optimization_barrier((mine, metas))
-            tables = view_tables(metas)
+            *places, outline = view_tables(metas)
         sums = [mine] + [over_view(mine, s, views) for s in range(1, views)]
-        result = update(scalars, sums, current, bound, *tables, tile_y, tile_z, last)
+        ratio = over_weight(current, metas, outline)
+        result = update(scalars, sums, ratio, bound, metas, *places, tile_y, tile_z, last)
         current = result[0]
         if not last:
             crop = result[1]

time: 175 us -> 170 us (0.971)
  waiting for transfers between devices: 76.7 us -> 69.2 us
  Pallas kernels: 39.7 us -> 42.6 us
    ppermute x9 -> x6, waiting for transfers between devices: 33.8 us -> 23 us  [over_view(): lax.ppermute(x, 'view', [(i, (i + steps) % count) for i in range(count)])]
    pallas_call x0 -> x2, Pallas kernels: none -> 7.59 us  [over_weight(): pl.pallas_call(kernel, out_shape=jax.ShapeDtypeStruct(estimate.shape, F32...]
    ppermute x9 -> x6, starting transfers between devices: 12 us -> 5.16 us  [over_view(): lax.ppermute(x, 'view', [(i, (i + steps) % count) for i in range(count)])]
    ppermute x0 -> x2, starting transfers between devices: none -> 4.23 us  [view_metas(): other = lax.ppermute(held, 'view', [(i, i ^ bit) for i in range(views)])]
    pallas_call x2, Pallas kernels: 18 us -> 14.8 us  [read_tile(): pl.pallas_call(kernel, out_shape=tuple(shapes), in_specs=[vmem] * (n_flat...]
    ppermute x0 -> x2, waiting for transfers between devices: none -> 2.39 us  [view_metas(): other = lax.ppermute(held, 'view', [(i, i ^ bit) for i in range(views)])]
  transfers between devices with their start and end apart: 42 -> 41, of which waited for: 28 -> 27; matrix products, arithmetic and copies ran while one was open for 11% -> 11% of each run, Pallas kernels for 0% -> 4%
where the time goes in v4:
time: 170 us
  waiting for transfers between devices  69.2 us (41%)
  Pallas kernels  42.6 us (25%)
  starting transfers between devices  32.4 us (19%)
  other arithmetic  18.5 us (11%)
  local copies, waits for them, and re-layouts  5.91 us (3%)
    ppermute x33, waiting for transfers between devices, flip(): return lax.ppermute(x, 'brick', [(i, i ^ bit) for i in range(count)])  43.8 us
    ppermute x33, starting transfers between devices, flip(): return lax.ppermute(x, 'brick', [(i, i ^ bit) for i in range(count)])  23 us
    ppermute x6, waiting for transfers between devices, over_view(): lax.ppermute(x, 'view', [(i, (i + steps) % count) for i in range(count)])  23 us
    pallas_call x2, Pallas kernels, update(): pl.pallas_call(kernel, out_shape=tuple(shapes), in_specs=[pl.BlockSpec(me...  17.1 us
    pallas_call x2, Pallas kernels, read_tile(): pl.pallas_call(kernel, out_shape=tuple(shapes), in_specs=[vmem] * (n_flat...  14.8 us
    pallas_call x2, Pallas kernels, over_weight(): pl.pallas_call(kernel, out_shape=jax.ShapeDtypeStruct(estimate.shape, F32...  7.59 us
    ppermute x6, starting transfers between devices, over_view(): lax.ppermute(x, 'view', [(i, (i + steps) % count) for i in range(count)])  5.16 us
    ppermute x2, starting transfers between devices, view_metas(): other = lax.ppermute(held, 'view', [(i, i ^ bit) for i in range(views)])  4.23 us
  transfers between devices with their start and end apart: 41, of which 27 were waited for; matrix products, arithmetic and copies ran while one was open for 11% of the time, Pallas kernels for 4%

profile of v4, /device:TPU:0, one launch (start us, length us, event | category | flops | bytes accessed | tf_op | source)
XLA Modules:
  0.0 169.7 jit_solution(14503471754021508685)
XLA Ops:
  0.0 3.1 %first_crop.1.refs_0_ = bf16[32,32,128]{2,1,0:T(8,128)(2,1)} custom-call(s32[1,2]{1,0:T(1,128)} %shift_ref.1, f32[32,64,256]{2,1,0:T(8,128)} %bitcast.69), custom_call_target="tpu_custom_call" | custom-call | tf_op jit(solution)/shard_map/first_crop/pallas_call | solution.py:64
  3.1 3.0 %collective-permute-start.2 = (bf16[32,32,128]{2,1,0:T(8,128)(2,1)}, bf16[32,32,128]{2,1,0:T(8,128)(2,1)S(1)}, u32[]{:S(2)}, u32[]{:S(2)}) collective-permute-start(bf16[32,32,128]{2,1,0:T(8,128)(2,1)} %first_crop.1.refs_0_), channel_id=1, source_target_pairs={{0,4},{1,5},{2,6},{3,7},{4,0},{5,1},{6,2},{7,3},{8,12},{9,13},{10,... | collective-permute-start | bytes 786440 | tf_op jit(solution)/shard_map/ppermute | solution.py:276
  10.4 2.2 %collective-permute-done.2.refs_4_ = bf16[32,32,128]{2,1,0:T(8,128)(2,1)S(1)} collective-permute-done((bf16[32,32,128]{2,1,0:T(8,128)(2,1)}, bf16[32,32,128]{2,1,0:T(8,128)(2,1)S(1)}, u32[]{:S(2)}, u32[]{:S(2)}) %collective-permute-start.2) | collective-permute-done | bytes 262176 | tf_op jit(solution)/shard_map/ppermute | solution.py:276
  22.6 1.7 collective-permute-done.7.refs_7_
  24.3 2.2 %collective-permute-done.6.refs_6_ = bf16[16,32,128]{2,1,0:T(8,128)(2,1)S(1)} collective-permute-done((bf16[16,32,128]{2,1,0:T(8,128)(2,1)S(1)}, bf16[16,32,128]{2,1,0:T(8,128)(2,1)S(1)}, u32[]{:S(2)}, u32[]{:S(2)}) %collective-permute-start.6) | collective-permute-done | bytes 131104 | tf_op jit(solution)/shard_map/ppermute | solution.py:276
  28.7 7.4 %read_tile.2 = (s16[4,16,32,128]{3,2,1,0:T(8,128)(2,1)}, f32[4,16,32,128]{3,2,1,0:T(8,128)}, s16[4,16,32,128]{3,2,1,0:T(8,128)(2,1)}, f32[4,16,32,128]{3,2,1,0:T(8,128)}) custom-call(bf16[32,32,128]{2,1,0:T(8,128)(2,1)} %first_crop.1.refs_0_, bf16[32,32,128]{2,1,0:T(8,128)(2,1)} %copy-done.9, bf16[32,32,128]{2,1,0:T(8,128)(2,1)} %copy-done.6, ...), custom_call_target="tpu_custom_call" | custom-call | tf_op jit(solution)/shard_map/read_tile/pallas_call | solution.py:177
  42.5 2.4 %collective-permute-done.18 = f32[1,72,128]{2,1,0:T(8,128)S(1)} collective-permute-done((f32[1,72,128]{2,1,0:T(8,128)S(1)}, f32[1,72,128]{2,1,0:T(8,128)S(1)}, u32[]{:S(2)}, u32[]{:S(2)}) %collective-permute-start.18) | collective-permute-done | bytes 36896 | tf_op jit(solution)/shard_map/ppermute | solution.py:418
  44.9 2.6 %collective-permute-start.19 = (f32[2,72,128]{2,1,0:T(8,128)S(1)}, f32[2,72,128]{2,1,0:T(8,128)S(1)}, u32[]{:S(2)}, u32[]{:S(2)}) collective-permute-start(f32[2,72,128]{2,1,0:T(8,128)S(1)} %pad_maximum_fusion.2), channel_id=1, source_target_pairs={{0,16},{8,24},{16,0},{24,8},{1,17},{9,25},{17,1},{25,9},{2,18},{10... | collective-permute-start | bytes 221192 | tf_op jit(solution)/shard_map/ppermute | solution.py:418
  50.2 4.9 %collective-permute-done.14 = s16[2,16,32,128]{3,2,1,0:T(8,128)(2,1)S(1)} collective-permute-done((s16[2,16,32,128]{3,2,1,0:T(8,128)(2,1)S(1)}, s16[2,16,32,128]{3,2,1,0:T(8,128)(2,1)S(1)}, u32[]{:S(2)}, u32[]{:S(2)}) %collective-permute-start.14) | collective-permute-done | bytes 262176 | tf_op jit(solution)/shard_map/ppermute | solution.py:276
  57.6 2.8 %collective-permute-done.15 = s16[1,16,32,128]{3,2,1,0:T(8,128)(2,1)S(1)} collective-permute-done((s16[1,16,32,128]{3,2,1,0:T(8,128)(2,1)S(1)}, s16[1,16,32,128]{3,2,1,0:T(8,128)(2,1)S(1)}, u32[]{:S(2)}, u32[]{:S(2)}) %collective-permute-start.15) | collective-permute-done | bytes 131104 | tf_op jit(solution)/shard_map/ppermute | solution.py:276
  67.0 1.9 %select_reduce_fusion.1 = f32[4,128]{1,0:T(4,128)S(1)} fusion(f32[4,31]{1,0:T(4,128)S(1)} %bitcast.78, pred[128,128,31]{1,0,2:T(8,128)(4,1)S(1)} %iota_compare_fusion.2), kind=kLoop, calls=%fused_computation.2 | loop fusion | flops 4062720 | bytes 510448 | tf_op jit(solution)/shard_map/vmap()/reduce_sum | solution.py:434
  71.8 3.8 %over_weight.2.refs_5_ = f32[32,64,256]{2,1,0:T(8,128)} custom-call(f32[32,64,256]{2,1,0:T(8,128)} %bitcast.70, f32[4,72,128]{2,1,0:T(8,128)} %copy-done, f32[4,64,256]{2,1,0:T(8,128)} %broadcast_multiply_fusion.pat_ref), custom_call_target="tpu_custom_call" | custom-call | tf_op jit(solution)/shard_map/over_weight/pallas_call | solution.py:204
  77.4 7.4 %collective-permute-done.21.refs_3_ = s16[32,32,128]{2,1,0:T(8,128)(2,1)S(1)} collective-permute-done((s16[32,32,128]{2,1,0:T(8,128)(2,1)S(1)}, s16[32,32,128]{2,1,0:T(8,128)(2,1)S(1)}, u32[]{:S(2)}, u32[]{:S(2)}) %collective-permute-start.21) | collective-permute-done | bytes 262176 | tf_op jit(solution)/shard_map/ppermute | solution.py:280
  86.3 9.0 %update.2 = (f32[32,64,256]{2,1,0:T(8,128)}, bf16[32,32,128]{2,1,0:T(8,128)(2,1)}) custom-call(s32[3]{0:T(128)} %pad_add_fusion.3.refs_0_, s16[32,32,128]{2,1,0:T(8,128)(2,1)} %copy-done.1, s16[32,32,128]{2,1,0:T(8,128)(2,1)} %copy-done.17, s16[32,32,128]{2,1,0:T(8,128)(2,1)} %copy-done.16, s16[32,32,128]{2,1,0:T(8,128)(2,1)} %copy-done.15, ...), custom_call_target="tpu_custom_call" | custom-call | tf_op jit(solution)/shard_map/update/pallas_call | solution.py:265
  97.8 4.1 %collective-permute-done.26.refs_4_ = bf16[32,32,128]{2,1,0:T(8,128)(2,1)S(1)} collective-permute-done((bf16[32,32,128]{2,1,0:T(8,128)(2,1)}, bf16[32,32,128]{2,1,0:T(8,128)(2,1)S(1)}, u32[]{:S(2)}, u32[]{:S(2)}) %collective-permute-start.26) | collective-permute-done | bytes 262176 | tf_op jit(solution)/shard_map/ppermute | solution.py:276
  106.9 3.4 %collective-permute-done.28.refs_6_ = bf16[16,32,128]{2,1,0:T(8,128)(2,1)S(1)} collective-permute-done((bf16[16,32,128]{2,1,0:T(8,128)(2,1)S(1)}, bf16[16,32,128]{2,1,0:T(8,128)(2,1)S(1)}, u32[]{:S(2)}, u32[]{:S(2)}) %collective-permute-start.28) | collective-permute-done | bytes 131104 | tf_op jit(solution)/shard_map/ppermute | solution.py:276
  112.3 7.4 %read_tile.3 = (s16[4,16,32,128]{3,2,1,0:T(8,128)(2,1)}, f32[4,16,32,128]{3,2,1,0:T(8,128)}, s16[4,16,32,128]{3,2,1,0:T(8,128)(2,1)}, f32[4,16,32,128]{3,2,1,0:T(8,128)}) custom-call(bf16[32,32,128]{2,1,0:T(8,128)(2,1)} %get-tuple-element.51.refs_0_, bf16[32,32,128]{2,1,0:T(8,128)(2,1)} %copy-done.12, bf16[32,32,128]{2,1,0:T(8,128)(2,1)} %copy-done.8, ...), custom_call_target="tpu_custom_call" | custom-call | tf_op jit(solution)/shard_map/read_tile/pallas_call | solution.py:177
  125.6 6.2 %collective-permute-done.33 = s16[2,16,32,128]{3,2,1,0:T(8,128)(2,1)S(1)} collective-permute-done((s16[2,16,32,128]{3,2,1,0:T(8,128)(2,1)S(1)}, s16[2,16,32,128]{3,2,1,0:T(8,128)(2,1)S(1)}, u32[]{:S(2)}, u32[]{:S(2)}) %collective-permute-start.33) | collective-permute-done | bytes 262176 | tf_op jit(solution)/shard_map/ppermute | solution.py:276
  134.2 2.9 %collective-permute-done.34 = s16[1,16,32,128]{3,2,1,0:T(8,128)(2,1)S(1)} collective-permute-done((s16[1,16,32,128]{3,2,1,0:T(8,128)(2,1)S(1)}, s16[1,16,32,128]{3,2,1,0:T(8,128)(2,1)S(1)}, u32[]{:S(2)}, u32[]{:S(2)}) %collective-permute-start.34) | collective-permute-done | bytes 131104 | tf_op jit(solution)/shard_map/ppermute | solution.py:276
  138.9 1.9 %collective-permute-start.38 = (s16[32,32,128]{2,1,0:T(8,128)(2,1)S(1)}, s16[32,32,128]{2,1,0:T(8,128)(2,1)S(1)}, u32[]{:S(2)}, u32[]{:S(2)}) collective-permute-start(s16[32,32,128]{2,1,0:T(8,128)(2,1)S(1)} %pad_add_fusion.1.refs_1_), channel_id=1, source_target_pairs={{0,8},{8,16},{16,24},{24,0},{1,9},{9,17},{17,25},{25,1},{2,10},{10... | collective-permute-start | bytes 786440 | tf_op jit(solution)/shard_map/ppermute | solution.py:280
  140.8 3.8 %over_weight.3.refs_5_ = f32[32,64,256]{2,1,0:T(8,128)} custom-call(f32[32,64,256]{2,1,0:T(8,128)} %get-tuple-element.56.est_ref, f32[4,72,128]{2,1,0:T(8,128)} %copy-done, f32[4,64,256]{2,1,0:T(8,128)} %broadcast_multiply_fusion.pat_ref), custom_call_target="tpu_custom_call" | custom-call | tf_op jit(solution)/shard_map/over_weight/pallas_call | solution.py:204
  144.6 2.3 %collective-permute-done.40.refs_4_ = s16[32,32,128]{2,1,0:T(8,128)(2,1)S(1)} collective-permute-done((s16[32,32,128]{2,1,0:T(8,128)(2,1)S(1)}, s16[32,32,128]{2,1,0:T(8,128)(2,1)S(1)}, u32[]{:S(2)}, u32[]{:S(2)}) %collective-permute-start.40) | collective-permute-done | bytes 262176 | tf_op jit(solution)/shard_map/ppermute | solution.py:280
  146.9 13.3 %collective-permute-done.39.refs_3_ = s16[32,32,128]{2,1,0:T(8,128)(2,1)S(1)} collective-permute-done((s16[32,32,128]{2,1,0:T(8,128)(2,1)S(1)}, s16[32,32,128]{2,1,0:T(8,128)(2,1)S(1)}, u32[]{:S(2)}, u32[]{:S(2)}) %collective-permute-start.39) | collective-permute-done | bytes 262176 | tf_op jit(solution)/shard_map/ppermute | solution.py:280
  161.6 8.2 %update.3 = f32[32,64,256]{2,1,0:T(8,128)} custom-call(s32[3]{0:T(128)} %pad_add_fusion.3.refs_0_, s16[32,32,128]{2,1,0:T(8,128)(2,1)} %copy-done.2, s16[32,32,128]{2,1,0:T(8,128)(2,1)} %copy-done.20, s16[32,32,128]{2,1,0:T(8,128)(2,1)} %copy-done.19, s16[32,32,128]{2,1,0:T(8,128)(2,1)} %copy-done.18, f32[32,64,256]{2,1,0:T(8,128)} %over_weight.3.refs_5_, ...), custom_call_target="tpu_custom_call" | custom-call | tf_op jit(solution)/shard_map/update/pallas_call | solution.py:265
  (254 shorter events, 61.3 us)
Async XLA Ops:
  3.1 9.5 %collective-permute-start.2 = (bf16[32,32,128]{2,1,0:T(8,128)(2,1)}, bf16[32,32,128]{2,1,0:T(8,128)(2,1)S(1)}, u32[]{:S(2)}, u32[]{:S(2)}) collective-permute-start(bf16[32,32,128]{2,1,0:T(8,128)(2,1)} %first_crop.1.refs_0_), channel_id=1, source_target_pairs={{0,4},{1,5},{2,6},{3,7},{4,0},{5,1},{6,2},{7,3},{8,12},{9,13},{10,... | collective-permute-start | bytes 786440 | tf_op jit(solution)/shard_map/ppermute | solution.py:276
  6.1 8.0 %collective-permute-start.1 = (bf16[32,32,128]{2,1,0:T(8,128)(2,1)}, bf16[32,32,128]{2,1,0:T(8,128)(2,1)S(1)}, u32[]{:S(2)}, u32[]{:S(2)}) collective-permute-start(bf16[32,32,128]{2,1,0:T(8,128)(2,1)} %first_crop.1.refs_0_), channel_id=1, source_target_pairs={{0,2},{1,3},{2,0},{3,1},{4,6},{5,7},{6,4},{7,5},{8,10},{9,11},{10,... | collective-permute-start | bytes 786440 | tf_op jit(solution)/shard_map/ppermute | solution.py:276
  7.6 19.9 %collective-permute-start = (bf16[32,32,128]{2,1,0:T(8,128)(2,1)}, bf16[32,32,128]{2,1,0:T(8,128)(2,1)S(1)}, u32[]{:S(2)}, u32[]{:S(2)}) collective-permute-start(bf16[32,32,128]{2,1,0:T(8,128)(2,1)} %first_crop.1.refs_0_), channel_id=1, source_target_pairs={{0,1},{1,0},{2,3},{3,2},{4,5},{5,4},{6,7},{7,6},{8,9},{9,8},{10,11... | collective-permute-start | bytes 786440 | tf_op jit(solution)/shard_map/ppermute | solution.py:276
  16.2 11.7 %collective-permute-start.4 = (bf16[32,32,128]{2,1,0:T(8,128)(2,1)S(1)}, bf16[32,32,128]{2,1,0:T(8,128)(2,1)S(1)}, u32[]{:S(2)}, u32[]{:S(2)}) collective-permute-start(bf16[32,32,128]{2,1,0:T(8,128)(2,1)S(1)} %collective-permute-done.1.refs_2_), channel_id=1, source_target_pairs={{0,1},{1,0},{2,3},{3,2},{4,5},{5,4},{6,7},{7,6},{8,9},{9,8},{10,11... | collective-permute-start | bytes 786440 | tf_op jit(solution)/shard_map/ppermute | solution.py:276
  16.3 11.6 %collective-permute-start.5 = (bf16[32,32,128]{2,1,0:T(8,128)(2,1)S(1)}, bf16[32,32,128]{2,1,0:T(8,128)(2,1)S(1)}, u32[]{:S(2)}, u32[]{:S(2)}) collective-permute-start(bf16[32,32,128]{2,1,0:T(8,128)(2,1)S(1)} %collective-permute-done.2.refs_4_), channel_id=1, source_target_pairs={{0,1},{1,0},{2,3},{3,2},{4,5},{5,4},{6,7},{7,6},{8,9},{9,8},{10,11... | collective-permute-start | bytes 786440 | tf_op jit(solution)/shard_map/ppermute | solution.py:276
  19.1 5.3 %collective-permute-start.7 = (bf16[16,32,128]{2,1,0:T(8,128)(2,1)S(1)}, bf16[16,32,128]{2,1,0:T(8,128)(2,1)S(1)}, u32[]{:S(2)}, u32[]{:S(2)}) collective-permute-start(bf16[16,32,128]{2,1,0:T(8,128)(2,1)S(1)} %slice.106), channel_id=1, source_target_pairs={{0,2},{1,3},{2,0},{3,1},{4,6},{5,7},{6,4},{7,5},{8,10},{9,11},{10,... | collective-permute-start | bytes 393224 | tf_op jit(solution)/shard_map/ppermute | solution.py:276
  44.9 5.3 %collective-permute-start.19 = (f32[2,72,128]{2,1,0:T(8,128)S(1)}, f32[2,72,128]{2,1,0:T(8,128)S(1)}, u32[]{:S(2)}, u32[]{:S(2)}) collective-permute-start(f32[2,72,128]{2,1,0:T(8,128)S(1)} %pad_maximum_fusion.2), channel_id=1, source_target_pairs={{0,16},{8,24},{16,0},{24,8},{1,17},{9,25},{17,1},{25,9},{2,18},{10... | collective-permute-start | bytes 221192 | tf_op jit(solution)/shard_map/ppermute | solution.py:418
  48.1 7.1 %collective-permute-start.14 = (s16[2,16,32,128]{3,2,1,0:T(8,128)(2,1)S(1)}, s16[2,16,32,128]{3,2,1,0:T(8,128)(2,1)S(1)}, u32[]{:S(2)}, u32[]{:S(2)}) collective-permute-start(s16[2,16,32,128]{3,2,1,0:T(8,128)(2,1)S(1)} %get-tuple-element.43), channel_id=1, source_target_pairs={{0,2},{1,3},{2,0},{3,1},{4,6},{5,7},{6,4},{7,5},{8,10},{9,11},{10,... | collective-permute-start | bytes 786440 | tf_op jit(solution)/shard_map/ppermute | solution.py:276
  49.6 7.2 %collective-permute-start.16 = (s16[2,16,32,128]{3,2,1,0:T(8,128)(2,1)S(1)}, s16[2,16,32,128]{3,2,1,0:T(8,128)(2,1)S(1)}, u32[]{:S(2)}, u32[]{:S(2)}) collective-permute-start(s16[2,16,32,128]{3,2,1,0:T(8,128)(2,1)S(1)} %get-tuple-element.45), channel_id=1, source_target_pairs={{0,4},{1,5},{2,6},{3,7},{4,0},{5,1},{6,2},{7,3},{8,12},{9,13},{10,... | collective-permute-start | bytes 786440 | tf_op jit(solution)/shard_map/ppermute | solution.py:276
  62.6 14.9 %collective-permute-start.22 = (s16[32,32,128]{2,1,0:T(8,128)(2,1)S(1)}, s16[32,32,128]{2,1,0:T(8,128)(2,1)S(1)}, u32[]{:S(2)}, u32[]{:S(2)}) collective-permute-start(s16[32,32,128]{2,1,0:T(8,128)(2,1)S(1)} %pad_add_fusion.refs_1_), channel_id=1, source_target_pairs={{0,24},{8,0},{16,8},{24,16},{1,25},{9,1},{17,9},{25,17},{2,26},{10... | collective-permute-start | bytes 786440 | tf_op jit(solution)/shard_map/ppermute | solution.py:280
  64.0 20.9 %collective-permute-start.21 = (s16[32,32,128]{2,1,0:T(8,128)(2,1)S(1)}, s16[32,32,128]{2,1,0:T(8,128)(2,1)S(1)}, u32[]{:S(2)}, u32[]{:S(2)}) collective-permute-start(s16[32,32,128]{2,1,0:T(8,128)(2,1)S(1)} %pad_add_fusion.refs_1_), channel_id=1, source_target_pairs={{0,16},{8,24},{16,0},{24,8},{1,17},{9,25},{17,1},{25,9},{2,18},{10... | collective-permute-start | bytes 786440 | tf_op jit(solution)/shard_map/ppermute | solution.py:280
  65.7 19.2 %collective-permute-start.20 = (s16[32,32,128]{2,1,0:T(8,128)(2,1)S(1)}, s16[32,32,128]{2,1,0:T(8,128)(2,1)S(1)}, u32[]{:S(2)}, u32[]{:S(2)}) collective-permute-start(s16[32,32,128]{2,1,0:T(8,128)(2,1)S(1)} %pad_add_fusion.refs_1_), channel_id=1, source_target_pairs={{0,8},{8,16},{16,24},{24,0},{1,9},{9,17},{17,25},{25,1},{2,10},{10... | collective-permute-start | bytes 786440 | tf_op jit(solution)/shard_map/ppermute | solution.py:280
  95.2 6.6 %collective-permute-start.26 = (bf16[32,32,128]{2,1,0:T(8,128)(2,1)}, bf16[32,32,128]{2,1,0:T(8,128)(2,1)S(1)}, u32[]{:S(2)}, u32[]{:S(2)}) collective-permute-start(bf16[32,32,128]{2,1,0:T(8,128)(2,1)} %get-tuple-element.51.refs_0_), channel_id=1, source_target_pairs={{0,4},{1,5},{2,6},{3,7},{4,0},{5,1},{6,2},{7,3},{8,12},{9,13},{10,... | collective-permute-start | bytes 786440 | tf_op jit(solution)/shard_map/ppermute | solution.py:276
  96.3 8.0 %collective-permute-start.24 = (bf16[32,32,128]{2,1,0:T(8,128)(2,1)}, bf16[32,32,128]{2,1,0:T(8,128)(2,1)S(1)}, u32[]{:S(2)}, u32[]{:S(2)}) collective-permute-start(bf16[32,32,128]{2,1,0:T(8,128)(2,1)} %get-tuple-element.51.refs_0_), channel_id=1, source_target_pairs={{0,2},{1,3},{2,0},{3,1},{4,6},{5,7},{6,4},{7,5},{8,10},{9,11},{10,... | collective-permute-start | bytes 786440 | tf_op jit(solution)/shard_map/ppermute | solution.py:276
  97.8 12.5 %collective-permute-start.23 = (bf16[32,32,128]{2,1,0:T(8,128)(2,1)}, bf16[32,32,128]{2,1,0:T(8,128)(2,1)S(1)}, u32[]{:S(2)}, u32[]{:S(2)}) collective-permute-start(bf16[32,32,128]{2,1,0:T(8,128)(2,1)} %get-tuple-element.51.refs_0_), channel_id=1, source_target_pairs={{0,1},{1,0},{2,3},{3,2},{4,5},{5,4},{6,7},{7,6},{8,9},{9,8},{10,11... | collective-permute-start | bytes 786440 | tf_op jit(solution)/shard_map/ppermute | solution.py:276
  102.9 7.4 %collective-permute-start.27 = (bf16[32,32,128]{2,1,0:T(8,128)(2,1)S(1)}, bf16[32,32,128]{2,1,0:T(8,128)(2,1)S(1)}, u32[]{:S(2)}, u32[]{:S(2)}) collective-permute-start(bf16[32,32,128]{2,1,0:T(8,128)(2,1)S(1)} %collective-permute-done.26.refs_4_), channel_id=1, source_target_pairs={{0,1},{1,0},{2,3},{3,2},{4,5},{5,4},{6,7},{7,6},{8,9},{9,8},{10,11... | collective-permute-start | bytes 786440 | tf_op jit(solution)/shard_map/ppermute | solution.py:276
  104.3 6.0 %collective-permute-start.25 = (bf16[32,32,128]{2,1,0:T(8,128)(2,1)S(1)}, bf16[32,32,128]{2,1,0:T(8,128)(2,1)S(1)}, u32[]{:S(2)}, u32[]{:S(2)}) collective-permute-start(bf16[32,32,128]{2,1,0:T(8,128)(2,1)S(1)} %collective-permute-done.24.refs_2_), channel_id=1, source_target_pairs={{0,1},{1,0},{2,3},{3,2},{4,5},{5,4},{6,7},{7,6},{8,9},{9,8},{10,11... | collective-permute-start | bytes 786440 | tf_op jit(solution)/shard_map/ppermute | solution.py:276
  104.3 5.9 %collective-permute-start.28 = (bf16[16,32,128]{2,1,0:T(8,128)(2,1)S(1)}, bf16[16,32,128]{2,1,0:T(8,128)(2,1)S(1)}, u32[]{:S(2)}, u32[]{:S(2)}) collective-permute-start(bf16[16,32,128]{2,1,0:T(8,128)(2,1)S(1)} %slice.146), channel_id=1, source_target_pairs={{0,4},{1,5},{2,6},{3,7},{4,0},{5,1},{6,2},{7,3},{8,12},{9,13},{10,... | collective-permute-start | bytes 393224 | tf_op jit(solution)/shard_map/ppermute | solution.py:276
  119.9 5.1 %collective-permute-start.35 = (s16[4,16,32,128]{3,2,1,0:T(8,128)(2,1)}, s16[4,16,32,128]{3,2,1,0:T(8,128)(2,1)S(1)}, u32[]{:S(2)}, u32[]{:S(2)}) collective-permute-start(s16[4,16,32,128]{3,2,1,0:T(8,128)(2,1)} %get-tuple-element.55), channel_id=1, source_target_pairs={{0,1},{1,0},{2,3},{3,2},{4,5},{5,4},{6,7},{7,6},{8,9},{9,8},{10,11... | collective-permute-start | bytes 1572872 | tf_op jit(solution)/shard_map/ppermute | solution.py:276
  123.4 8.4 %collective-permute-start.33 = (s16[2,16,32,128]{3,2,1,0:T(8,128)(2,1)S(1)}, s16[2,16,32,128]{3,2,1,0:T(8,128)(2,1)S(1)}, u32[]{:S(2)}, u32[]{:S(2)}) collective-permute-start(s16[2,16,32,128]{3,2,1,0:T(8,128)(2,1)S(1)} %fusion.5), channel_id=1, source_target_pairs={{0,2},{1,3},{2,0},{3,1},{4,6},{5,7},{6,4},{7,5},{8,10},{9,11},{10,... | collective-permute-start | bytes 786440 | tf_op jit(solution)/shard_map/ppermute | solution.py:276
  125.3 8.1 %collective-permute-start.36 = (s16[2,16,32,128]{3,2,1,0:T(8,128)(2,1)S(1)}, s16[2,16,32,128]{3,2,1,0:T(8,128)(2,1)S(1)}, u32[]{:S(2)}, u32[]{:S(2)}) collective-permute-start(s16[2,16,32,128]{3,2,1,0:T(8,128)(2,1)S(1)} %fusion.3), channel_id=1, source_target_pairs={{0,4},{1,5},{2,6},{3,7},{4,0},{5,1},{6,2},{7,3},{8,12},{9,13},{10,... | collective-permute-start | bytes 786440 | tf_op jit(solution)/shard_map/ppermute | solution.py:276
  138.7 8.2 %collective-permute-start.40 = (s16[32,32,128]{2,1,0:T(8,128)(2,1)S(1)}, s16[32,32,128]{2,1,0:T(8,128)(2,1)S(1)}, u32[]{:S(2)}, u32[]{:S(2)}) collective-permute-start(s16[32,32,128]{2,1,0:T(8,128)(2,1)S(1)} %pad_add_fusion.1.refs_1_), channel_id=1, source_target_pairs={{0,24},{8,0},{16,8},{24,16},{1,25},{9,1},{17,9},{25,17},{2,26},{10... | collective-permute-start | bytes 786440 | tf_op jit(solution)/shard_map/ppermute | solution.py:280
  138.8 21.4 %collective-permute-start.39 = (s16[32,32,128]{2,1,0:T(8,128)(2,1)S(1)}, s16[32,32,128]{2,1,0:T(8,128)(2,1)S(1)}, u32[]{:S(2)}, u32[]{:S(2)}) collective-permute-start(s16[32,32,128]{2,1,0:T(8,128)(2,1)S(1)} %pad_add_fusion.1.refs_1_), channel_id=1, source_target_pairs={{0,16},{8,24},{16,0},{24,8},{1,17},{9,25},{17,1},{25,9},{2,18},{10... | collective-permute-start | bytes 786440 | tf_op jit(solution)/shard_map/ppermute | solution.py:280
  138.9 21.3 %collective-permute-start.38 = (s16[32,32,128]{2,1,0:T(8,128)(2,1)S(1)}, s16[32,32,128]{2,1,0:T(8,128)(2,1)S(1)}, u32[]{:S(2)}, u32[]{:S(2)}) collective-permute-start(s16[32,32,128]{2,1,0:T(8,128)(2,1)S(1)} %pad_add_fusion.1.refs_1_), channel_id=1, source_target_pairs={{0,8},{8,16},{16,24},{24,0},{1,9},{9,17},{17,25},{25,1},{2,10},{10... | collective-permute-start | bytes 786440 | tf_op jit(solution)/shard_map/ppermute | solution.py:280
  (52 other events, 226.8 us)

commit v5 on v4

--- a/solution.py
+++ b/solution.py
@@ -34,9 +34,8 @@
     return jnp.sum(jnp.where(hit, taps, 0.0), axis=-1)
 
 
-def put_crop(out_ref, ref, stage, shift_y, shift_z):
+def put_crop(out_ref, ref, stage, shift_y, shift_z, tile_y, tile_z):
     rows, brick_y, brick_z = ref.shape
-    tile_y, _, tile_z = out_ref.shape
     tall = tile_y + 8
     base = pl.multiple_of(jnp.minimum(shift_y // 8, (brick_y - tile_y) // 8 - 1) * 8, 8)
     turn = lax.rem(brick_z - shift_z, brick_z)
@@ -55,48 +54,80 @@
     lax.fori_loop(0, tile_y, turn_over, 0, unroll=8)
 
 
-def first_crop(shifts, estimate, tile_y, tile_z):
+def first_crop(shifts, estimate, lines, tile_y, tile_z):
     rows = estimate.shape[0]
-
-    def kernel(shift_ref, est_ref, out_ref, stage):
-        put_crop(out_ref, est_ref, stage, shift_ref[0, 0], shift_ref[0, 1])
+    extra = lines.shape[0]
+
+    def kernel(shift_ref, est_ref, line_ref, out_ref, stage):
+        put_crop(out_ref, est_ref, stage, shift_ref[0, 0], shift_ref[0, 1], tile_y, tile_z)
+        out_ref[tile_y:] = line_ref[...]
 
     return pl.pallas_call(
         kernel,
-        out_shape=jax.ShapeDtypeStruct((tile_y, rows, tile_z), BF16),
+        out_shape=jax.ShapeDtypeStruct((tile_y + extra, rows, tile_z), BF16),
         in_specs=[
             pl.BlockSpec(memory_space=pltpu.SMEM),
+            pl.BlockSpec(memory_space=pltpu.VMEM),
             pl.BlockSpec(memory_space=pltpu.VMEM),
         ],
         out_specs=pl.BlockSpec(memory_space=pltpu.VMEM),
         scratch_shapes=[pltpu.VMEM((rows * (tile_y + 8), tile_z), F32)],
         name="first_crop",
-    )(shifts, estimate)
+    )(shifts, estimate, lines)
 
 
 def code(x):
     return (x + 0.5).astype(jnp.int32).astype(WIRE)
 
 
-def read_tile(pieces, measured, mass, bound, gather_mat, scatter_mat, z_mat, y_mat, slots):
+def read_tile(
+    me, pieces, tile_y, measured, mass, bound, scale, gather_mat, scatter_mat, z_mat, y_mat, slots
+):
     owners = len(pieces)
     rows, tile_z = pieces[0][0].shape[1:]
-    tile_y = sum(p.shape[0] for p in pieces[0])
+    group = y_mat.shape[1] // 2
     half = tile_y // 2
     tile_x = measured.shape[0] // tile_y
     flat = [p for parts in pieces for p in parts]
     n_flat = len(flat)
     firsts = [sum(len(p) for p in pieces[:k]) for k in range(owners)]
     n_send = owners // 2
-    group = y_mat.shape[1] // 2
     per_group = group // tile_y
     groups = tile_x // per_group
+    known = scale is not None
+    extra = sum(p.shape[0] for p in pieces[0]) - tile_y
 
     def kernel(*refs):
-        g_refs = refs[:n_flat]
-        m_ref, pat_ref, gm_ref, sm_ref, zm_ref, ym_ref = refs[n_flat : n_flat + 6]
-        outs = refs[n_flat + 6 : n_flat + 10]
-        lines, buf = refs[n_flat + 10 :]
+        me_ref = refs[0]
+        g_refs = refs[1 : 1 + n_flat]
+        m_ref, pat_ref, gm_ref, sm_ref, zm_ref, ym_ref = refs[1 + n_flat : 7 + n_flat]
+        rest = refs[7 + n_flat :]
+        if known:
+            scale_ref, rest = rest[0], rest[1:]
+        outs = rest[:4]
+        lines, buf = rest[-2:]
+        if not known:
+            scale_ref, own_ref = rest[4:6]
+            table = []
+            for j in range(extra):
+                held = []
+                for k in range(owners):
+                    ref = g_refs[firsts[k] + len(pieces[k]) - 1]
+                    held.append(ref[ref.shape[0] - extra + j].astype(F32))
+                table.append(sum(held))
+            lane = lax.broadcasted_iota(jnp.int32, (rows, tile_z), 1) & (2 * owners - 1)
+
+            def column(which, k):
+                hit = lane == which * owners + (me_ref[0] ^ k)
+                picked = sum(jnp.where(hit, t, 0.0) for t in table)
+                return jnp.sum(picked, axis=1, keepdims=True)
+
+            for k in range(owners):
+                total = column(1, k)
+                value = jnp.where(total > 0.0, FULL / jnp.maximum(total, 1e-30), 0.0)
+                scale_ref[k * rows : (k + 1) * rows, :] = jnp.broadcast_to(value, (rows, tile_z))
+            for which in range(2):
+                own_ref[which] = jnp.broadcast_to(column(which, 0), (rows, tile_z))
         for h in range(2):
 
             def line(k, y, h=h):
@@ -137,7 +168,7 @@
             out = dot(ym_ref[...], jnp.concatenate([hi, lo], axis=0))
             out = out[:group] + out[group:]
             data = m_ref[pl.ds(at, 2 * group), :].astype(F32)
-            pat = pat_ref[...] * (1.0 / bound)
+            pat = jnp.concatenate([pat_ref[...] * (1.0 / bound)] * per_group, axis=0)
             buf[pl.ds(at, group), :] = data[:group] * pat / out[:, :tile_z]
             buf[pl.ds(at + group, group), :] = data[group:] * pat / out[:, tile_z:]
             return carry
@@ -163,25 +194,28 @@
                 hi, lo = split(jnp.concatenate([first, second], axis=1))
                 out = dot(sm_ref[...], jnp.concatenate([hi, lo], axis=0))
                 out = out[: owners * rows] + out[owners * rows :]
-                put(y, out[:, :tile_z])
-                put(y + 1, out[:, tile_z:])
+                put(y, out[:, :tile_z] * scale_ref[...])
+                put(y + 1, out[:, tile_z:] * scale_ref[...])
                 return carry
 
             lax.fori_loop(0, half // 2, scatter, 0, unroll=UNROLL)
 
     vmem = pl.BlockSpec(memory_space=pltpu.VMEM)
     shapes = []
-    for h in range(2):
+    for _ in range(2):
         for dtype in (WIRE, F32):
             shapes.append(jax.ShapeDtypeStruct((n_send, half, rows, tile_z), dtype))
+    if not known:
+        shapes.append(jax.ShapeDtypeStruct((owners * rows, tile_z), F32))
+        shapes.append(jax.ShapeDtypeStruct((2, rows, tile_z), F32))
     return pl.pallas_call(
         kernel,
         out_shape=tuple(shapes),
-        in_specs=[vmem] * (n_flat + 6),
-        out_specs=(vmem,) * 4,
+        in_specs=[pl.BlockSpec(memory_space=pltpu.SMEM)] + [vmem] * (n_flat + 6 + known),
+        out_specs=(vmem,) * len(shapes),
         scratch_shapes=[pltpu.VMEM((tile_x * tile_y, tile_z), F32)] * 2,
         name="read_tile",
-    )(*flat, measured, mass, gather_mat, scatter_mat, z_mat, y_mat)
+    )(me, *flat, measured, mass, gather_mat, scatter_mat, z_mat, y_mat, *([scale] if known else []))
 
 
 def over_weight(estimate, metas, outline):
@@ -225,11 +259,11 @@
         placed = rest[1] if last else rest[2]
         me = s_ref[2]
         for s in range(views):
-            view = lax.rem(me + views - s, views)
+            view = me ^ s
             unit = me_ref[view, 8 + rows : 8 + 2 * rows, :] * (bound / FULL)
             for h in range(2):
-                x = in_refs[s][h * half : (h + 1) * half].astype(jnp.int32).astype(F32)
-                x = (x * unit[None]).reshape(half * rows, tile_z)
+                x = in_refs[s][h * half : (h + 1) * half].astype(jnp.int32)
+                x = (x.astype(F32) * unit[None]).reshape(half * rows, tile_z)
                 hi, lo = split(x)
                 out = dot(jnp.concatenate([hi, lo], axis=1), zp_ref[view, 0])
                 out = out + dot(hi, zp_ref[view, 1, :tile_z, :])
@@ -253,7 +287,7 @@
 
         lax.fori_loop(0, rows, step, 0, unroll=UNROLL)
         if not last:
-            put_crop(crop_ref, out_ref, rest[3], s_ref[0], s_ref[1])
+            put_crop(crop_ref, out_ref, rest[3], s_ref[0], s_ref[1], tile_y, tile_z)
 
     vmem = pl.BlockSpec(memory_space=pltpu.VMEM)
     shapes = [jax.ShapeDtypeStruct(ratio.shape, F32)]
@@ -276,8 +310,12 @@
     return lax.ppermute(x, "brick", [(i, i ^ bit) for i in range(count)])
 
 
-def over_view(x, steps, count):
-    return lax.ppermute(x, "view", [(i, (i + steps) % count) for i in range(count)])
+def pair_views(x, bit, count):
+    return lax.ppermute(x, "view", [(i, i ^ bit) for i in range(count)])
+
+
+def exchange_views(mine, count):
+    return [mine] + [pair_views(mine, j, count) for j in range(1, count)]
 
 
 def gather_first(crop, count):
@@ -285,8 +323,7 @@
     return {bit: flip(crop, bit, count) for bit in wide} if len(wide) == 2 else {}
 
 
-def gather_owners(crop, near, count):
-    half = crop.shape[0] // 2
+def gather_owners(crop, near, half, count):
     wide = [1 << i for i in range(1, count.bit_length() - 1)]
     got = {0: (crop,)}
     if near:
@@ -329,23 +366,32 @@
     highest = lax.Precision.HIGHEST
 
     flat = estimate.reshape(own_rows, brick_y, brick_z)
-    crop = first_crop(view_shift, flat, tile_y, tile_z)
-    near = gather_first(crop, owners)
     shifts = view_shift[0]
     scalars = jnp.concatenate([shifts, my_view[None].astype(jnp.int32)])
 
-    taps = psf_taps[0] / jnp.sum(psf_taps[0], axis=1, keepdims=True)
-    count = taps.shape[1]
+    lanes = 128
+    count = psf_taps.shape[2]
+    small = jnp.concatenate(
+        [
+            jnp.pad(psf_taps[0], ((0, 0), (0, lanes - count))),
+            jnp.concatenate(
+                [seg_owner[0, 0, :, 0], seg_local[0, 0], seg_offset[0, 0], seg_extent[0, 0]]
+            ).astype(F32).reshape(-1, lanes),
+        ],
+        axis=0,
+    )
+    small = lax.optimization_barrier(small)
+    taps = small[:3, :count] / jnp.sum(small[:3, :count], axis=1, keepdims=True)
+    owner, local, offset, extent = small[3:].reshape(4, -1).astype(jnp.int32)
     tile_rows = jnp.arange(tile_x, dtype=jnp.int32)
     tile_cols = jnp.arange(tile_z, dtype=jnp.int32)
     tile_mids = jnp.arange(tile_y, dtype=jnp.int32)
-    extent = seg_extent[0, 0]
     seg_ids = jnp.arange(extent.shape[0], dtype=jnp.int32)
     starts = jnp.sum(jnp.where(seg_ids[None, :] < seg_ids[:, None], extent[None, :], 0), axis=1)
     inside = (starts[None, :] <= tile_rows[:, None]) & (
         tile_rows[:, None] < (starts + extent)[None, :]
     )
-    in_owner = seg_local[0, 0] * brick_x + seg_offset[0, 0] - starts
+    in_owner = local * brick_x + offset - starts
     all_rows = jnp.arange(owners * own_rows, dtype=jnp.int32)[None, :]
 
     def picks(owner):
@@ -353,41 +399,30 @@
         source = jnp.sum(jnp.where(inside, base[None, :], 0), axis=1) + tile_rows
         return (source[:, None] == all_rows).astype(F32)
 
-    owner = seg_owner[0, 0, :, 0]
     x_mat = band(taps[0], tile_rows, tile_rows)
     y_band = band(taps[1], tile_mids, tile_mids)
     z_band = band(taps[2], tile_cols, tile_cols)
     x_mass = jnp.sum(x_mat, axis=0)
 
-    lanes = 128
     totals = jnp.stack(
         [jnp.sum(x_mat, axis=1), jnp.sum(x_mat / x_mass[None, :], axis=1)], axis=0
     )
-    table = jnp.sum(totals[:, :, None] * picks(owner)[None], axis=1).reshape(-1, lanes)
-    table_rows = table.shape[0]
-    table = jnp.pad(table, ((0, -table_rows % 8), (0, 0)))
-    bits = [1 << i for i in range(owners.bit_length() - 1)]
-    table = table + flip(table, bits[0], owners)
-    near, table, x_mat, y_band, z_band, owner = lax.optimization_barrier(
-        (near, table, x_mat, y_band, z_band, owner)
-    )
-    for bit in bits[1:]:
-        table = table + flip(table, bit, owners)
-    pieces = gather_owners(crop, near, owners)
-    table = table[:table_rows].reshape(2, owners, own_rows)
-    owner_ids = jnp.arange(owners, dtype=jnp.int32)
-    mine_rows = jnp.sum(jnp.where((owner_ids == me)[None, :, None], table, 0.0), axis=1)
-    relative = (owner_ids[:, None] ^ me) == owner_ids[None, :]
-    bound_rows = jnp.sum(
-        jnp.where(relative[:, :, None], table[1][None], 0.0), axis=1
-    ).reshape(-1)
-    to_code = jnp.where(bound_rows > 0.0, FULL / jnp.maximum(bound_rows, 1e-30), 0.0)
+    table = jnp.sum(totals[:, :, None] * picks(owner)[None], axis=1)
+    table = table.reshape(2 * owners, own_rows).T
+    hi = lax.reduce_precision(table, 8, 7)
+    mid = lax.reduce_precision(table - hi, 8, 7)
+    parts = jnp.concatenate([hi, mid, table - hi - mid], axis=1).astype(BF16)
+    parts = jnp.pad(parts, ((0, 0), (0, -parts.shape[1] % lanes)))
+    parts = jnp.transpose(parts.reshape(own_rows, -1, lanes), (1, 0, 2))
+    crop = first_crop(view_shift, flat, parts, tile_y, tile_z)
+    near = gather_first(crop, owners)
+    pieces = gather_owners(crop, near, tile_y // 2, owners)
 
     relative_picks = picks(owner ^ me)
     rows_mat = jnp.einsum("tw,tr->wr", x_mat, relative_picks, precision=highest)
     hi, lo = split_outside(rows_mat)
     gather_mat = jnp.concatenate([hi, lo], axis=0)
-    hi, lo = split_outside(rows_mat.T * to_code[:, None])
+    hi, lo = split_outside(rows_mat.T)
     scatter_mat = jnp.concatenate(
         [jnp.concatenate([hi, hi], axis=1), jnp.concatenate([lo, lo], axis=1)], axis=0
     )
@@ -401,22 +436,18 @@
         [jnp.concatenate([hi, hi], axis=1), jnp.concatenate([lo, lo], axis=1)], axis=0
     )
     mass = jnp.sum(y_band, axis=0)[:, None] * jnp.sum(z_band, axis=0)[None, :]
-    mass = jnp.tile(mass, (per_group, 1))
-
-    def view_metas(taps, shifts, mine_rows):
+
+    def view_metas(taps, shifts, own_totals):
         meta = jnp.concatenate(
             [
                 jnp.pad(taps, ((0, 0), (0, lanes - count))),
                 jnp.pad(shifts.astype(F32), (0, lanes - 2))[None],
                 jnp.zeros((4, lanes), F32),
-                jnp.broadcast_to(mine_rows.reshape(-1, 1), (2 * own_rows, lanes)),
+                own_totals.reshape(2 * own_rows, lanes),
             ],
             axis=0,
         )
-        held = meta[None]
-        for bit in [1 << i for i in range(views.bit_length() - 1)]:
-            other = lax.ppermute(held, "view", [(i, i ^ bit) for i in range(views)])
-            held = jnp.concatenate([held, other], axis=0)
+        held = exchange_views(meta, views)
         view_ids = jnp.arange(views, dtype=jnp.int32)
         return sum(
             jnp.where(((view_ids ^ my_view) == j)[:, None, None], held[j][None], 0.0)
@@ -457,33 +488,47 @@
     measured = views_data.reshape(tile_x * tile_y, tile_z)
     orders, slots = halving_orders(owners)
 
-    current = flat
+    current, scale = flat, None
     for sweep in range(ITERS):
         last = sweep == ITERS - 1
         bound = 4.04 if sweep == 0 else 16.8
         if sweep:
-            pieces = gather_owners(crop, gather_first(crop, owners), owners)
+            pieces = gather_owners(crop, gather_first(crop, owners), tile_y // 2, owners)
         outs = read_tile(
-            pieces, measured, mass, bound, gather_mat, scatter_mat, z_mat, y_mat, slots
-        )
+            me[None].astype(jnp.int32),
+            pieces,
+            tile_y,
+            measured,
+            mass,
+            bound,
+            scale,
+            gather_mat,
+            scatter_mat,
+            z_mat,
+            y_mat,
+            slots,
+        )
+        if sweep == 0:
+            scale, own_totals = outs[4:]
         send = [outs[0], outs[2]]
         keep = [outs[1], outs[3]]
         for i in range(len(orders[0])):
             for h in range(2):
-                total = keep[h] + flip(send[h], orders[h][i], owners).astype(F32)
+                got = flip(send[h], orders[h][i], owners)
+                total = keep[h] + got.astype(F32)
                 left = total.shape[0] // 2
                 send[h] = code(total[:left]) if left else None
                 keep[h] = total[left:]
             if sweep == 0 and i == 0:
                 send, keep, late = lax.optimization_barrier(
-                    (send, keep, (taps, shifts, mine_rows))
+                    (send, keep, (taps, shifts, own_totals))
                 )
                 metas = view_metas(*late)
         mine = jnp.concatenate([code(k[0]) for k in keep], axis=0)
         if sweep == 0:
             mine, metas = lax.optimization_barrier((mine, metas))
             *places, outline = view_tables(metas)
-        sums = [mine] + [over_view(mine, s, views) for s in range(1, views)]
+        sums = exchange_views(mine, views)
         ratio = over_weight(current, metas, outline)
         result = update(scalars, sums, ratio, bound, metas, *places, tile_y, tile_z, last)
         current = result[0]
@@ -503,6 +548,7 @@
         P("view", "brick", None),
         P("view", None),
     )
+
     return jax.shard_map(
         on_device,
         mesh=mesh,

time: 170 us -> 167 us (0.982)
  waiting for transfers between devices: 69.2 us -> 59.5 us
  starting transfers between devices: 32.4 us -> 36.3 us
  other arithmetic: 18.5 us -> 20.7 us
    ppermute x33 -> x30, waiting for transfers between devices: 43.8 us -> 36.5 us  [flip(): return lax.ppermute(x, 'brick', [(i, i ^ bit) for i in range(count)])]
    ppermute x8 -> x9, starting transfers between devices: 9.4 us -> 13.3 us  [pair_views(): return lax.ppermute(x, 'view', [(i, i ^ bit) for i in range(count)])]
    ppermute x8 -> x9, waiting for transfers between devices: 25.4 us -> 23 us  [pair_views(): return lax.ppermute(x, 'view', [(i, i ^ bit) for i in range(count)])]
    unnamed x70 -> x63, local copies, waits for them, and re-layouts: 3.99 us -> 5.3 us
    ppermute x33 -> x30, starting transfers between devices: 23 us -> 23 us  [flip(): return lax.ppermute(x, 'brick', [(i, i ^ bit) for i in range(count)])]
    add x13 -> x8, other arithmetic: 3.79 us -> 3.76 us  [on_device(): total = keep[h] + got.astype(F32)]
  transfers between devices with their start and end apart: 41 -> 39, of which waited for: 27 -> 19; matrix products, arithmetic and copies ran while one was open for 11% -> 11% of each run, Pallas kernels for 4% -> 5%
where the time goes in v5:
time: 167 us
  waiting for transfers between devices  59.5 us (36%)
  Pallas kernels  42.9 us (26%)
  starting transfers between devices  36.3 us (22%)
  other arithmetic  20.7 us (12%)
  local copies, waits for them, and re-layouts  6.35 us (4%)
    ppermute x30, waiting for transfers between devices, flip(): return lax.ppermute(x, 'brick', [(i, i ^ bit) for i in range(count)])  36.5 us
    ppermute x9, waiting for transfers between devices, pair_views(): return lax.ppermute(x, 'view', [(i, i ^ bit) for i in range(count)])  23 us
    ppermute x30, starting transfers between devices, flip(): return lax.ppermute(x, 'brick', [(i, i ^ bit) for i in range(count)])  23 us
    pallas_call x2, Pallas kernels, update(): pl.pallas_call(kernel, out_shape=tuple(shapes), in_specs=[pl.BlockSpec(me...  17.1 us
    pallas_call x2, Pallas kernels, read_tile(): pl.pallas_call(kernel, out_shape=tuple(shapes), in_specs=[pl.BlockSpec(me...  15.2 us
    ppermute x9, starting transfers between devices, pair_views(): return lax.ppermute(x, 'view', [(i, i ^ bit) for i in range(count)])  13.3 us
    pallas_call x2, Pallas kernels, over_weight(): pl.pallas_call(kernel, out_shape=jax.ShapeDtypeStruct(estimate.shape, F32...  7.59 us
    unnamed x63, local copies, waits for them, and re-layouts  5.3 us
  transfers between devices with their start and end apart: 39, of which 19 were waited for; matrix products, arithmetic and copies ran while one was open for 11% of the time, Pallas kernels for 5%

profile of v5, /device:TPU:0, one launch (start us, length us, event | category | flops | bytes accessed | tf_op | source)
XLA Modules:
  0.0 166.8 jit_solution(11332353693172479655)
XLA Ops:
  3.9 3.0 %first_crop.1.refs_1_ = bf16[33,32,128]{2,1,0:T(8,128)(2,1)} custom-call(s32[1,2]{1,0:T(1,128)} %shift_ref.1, f32[32,64,256]{2,1,0:T(8,128)} %bitcast.81, bf16[1,32,128]{2,1,0:T(8,128)(2,1)} %fusion.57.line_ref), custom_call_target="tpu_custom_call" | custom-call | tf_op jit(solution)/shard_map/first_crop/pallas_call | solution.py:65
  6.9 3.0 %collective-permute-start.3 = (bf16[33,32,128]{2,1,0:T(8,128)(2,1)}, bf16[33,32,128]{2,1,0:T(8,128)(2,1)S(1)}, u32[]{:S(2)}, u32[]{:S(2)}) collective-permute-start(bf16[33,32,128]{2,1,0:T(8,128)(2,1)} %first_crop.1.refs_1_), channel_id=1, source_target_pairs={{0,4},{1,5},{2,6},{3,7},{4,0},{5,1},{6,2},{7,3},{8,12},{9,13},{10,... | collective-permute-start | bytes 811016 | tf_op jit(solution)/shard_map/ppermute | solution.py:310
  13.9 2.7 %collective-permute-done.3.refs_5_ = bf16[33,32,128]{2,1,0:T(8,128)(2,1)S(1)} collective-permute-done((bf16[33,32,128]{2,1,0:T(8,128)(2,1)}, bf16[33,32,128]{2,1,0:T(8,128)(2,1)S(1)}, u32[]{:S(2)}, u32[]{:S(2)}) %collective-permute-start.3) | collective-permute-done | bytes 270368 | tf_op jit(solution)/shard_map/ppermute | solution.py:310
  25.8 7.7 %read_tile.2 = (s16[4,16,32,128]{3,2,1,0:T(8,128)(2,1)}, f32[4,16,32,128]{3,2,1,0:T(8,128)}, s16[4,16,32,128]{3,2,1,0:T(8,128)(2,1)}, f32[4,16,32,128]{3,2,1,0:T...) custom-call(s32[1]{0:T(128)} %bitcast.2.refs_0_, bf16[33,32,128]{2,1,0:T(8,128)(2,1)} %first_crop.1.refs_1_, ...), custom_call_target="tpu_custom_call" | custom-call | tf_op jit(solution)/shard_map/read_tile/pallas_call | solution.py:211
  38.2 3.6 %collective-permute-start.17 = (f32[72,128]{1,0:T(8,128)S(1)}, f32[72,128]{1,0:T(8,128)S(1)}, u32[]{:S(2)}, u32[]{:S(2)}) collective-permute-start(f32[72,128]{1,0:T(8,128)S(1)} %fusion.47), channel_id=1, source_target_pairs={{0,24},{8,16},{16,8},{24,0},{1,25},{9,17},{17,9},{25,1},{2,26},{10... | collective-permute-start | bytes 110600 | tf_op jit(solution)/shard_map/ppermute | solution.py:314
  46.8 3.5 %collective-permute-done.11 = s16[2,16,32,128]{3,2,1,0:T(8,128)(2,1)S(1)} collective-permute-done((s16[2,16,32,128]{3,2,1,0:T(8,128)(2,1)S(1)}, s16[2,16,32,128]{3,2,1,0:T(8,128)(2,1)S(1)}, u32[]{:S(2)}, u32[]{:S(2)}) %collective-permute-start.11) | collective-permute-done | bytes 262176 | tf_op jit(solution)/shard_map/ppermute | solution.py:310
  52.8 2.6 %collective-permute-done.12 = s16[1,16,32,128]{3,2,1,0:T(8,128)(2,1)S(1)} collective-permute-done((s16[1,16,32,128]{3,2,1,0:T(8,128)(2,1)S(1)}, s16[1,16,32,128]{3,2,1,0:T(8,128)(2,1)S(1)}, u32[]{:S(2)}, u32[]{:S(2)}) %collective-permute-start.12) | collective-permute-done | bytes 131104 | tf_op jit(solution)/shard_map/ppermute | solution.py:310
  57.8 3.5 %collective-permute-start.20 = (s16[32,32,128]{2,1,0:T(8,128)(2,1)S(1)}, s16[32,32,128]{2,1,0:T(8,128)(2,1)S(1)}, u32[]{:S(2)}, u32[]{:S(2)}) collective-permute-start(s16[32,32,128]{2,1,0:T(8,128)(2,1)S(1)} %pad_add_fusion.refs_1_), channel_id=1, source_target_pairs={{0,24},{8,16},{16,8},{24,0},{1,25},{9,17},{17,9},{25,1},{2,26},{10... | collective-permute-start | bytes 786440 | tf_op jit(solution)/shard_map/ppermute | solution.py:314
  63.6 1.9 %select_reduce_fusion.1 = f32[4,128]{1,0:T(4,128)S(1)} fusion(f32[4,31]{1,0:T(4,128)S(1)} %bitcast.88, pred[128,128,31]{1,0,2:T(8,128)(4,1)S(1)} %iota_compare_fusion.2), kind=kLoop, calls=%fused_computation.2 | loop fusion | flops 4062720 | bytes 510448 | tf_op jit(solution)/shard_map/vmap()/reduce_sum | solution.py:465
  68.4 3.8 %over_weight.2.refs_5_ = f32[32,64,256]{2,1,0:T(8,128)} custom-call(f32[32,64,256]{2,1,0:T(8,128)} %bitcast.82, f32[4,72,128]{2,1,0:T(8,128)} %copy-done, f32[4,64,256]{2,1,0:T(8,128)} %broadcast_multiply_fusion.pat_ref), custom_call_target="tpu_custom_call" | custom-call | tf_op jit(solution)/shard_map/over_weight/pallas_call | solution.py:238
  74.0 7.4 %collective-permute-done.19.refs_3_ = s16[32,32,128]{2,1,0:T(8,128)(2,1)S(1)} collective-permute-done((s16[32,32,128]{2,1,0:T(8,128)(2,1)S(1)}, s16[32,32,128]{2,1,0:T(8,128)(2,1)S(1)}, u32[]{:S(2)}, u32[]{:S(2)}) %collective-permute-start.19) | collective-permute-done | bytes 262176 | tf_op jit(solution)/shard_map/ppermute | solution.py:314
  82.8 9.0 %update.2 = (f32[32,64,256]{2,1,0:T(8,128)}, bf16[32,32,128]{2,1,0:T(8,128)(2,1)}) custom-call(s32[3]{0:T(128)} %pad_add_fusion.2.refs_0_, s16[32,32,128]{2,1,0:T(8,128)(2,1)} %copy-done.1, s16[32,32,128]{2,1,0:T(8,128)(2,1)} %copy-done.15, s16[32,32,128]{2,1,0:T(8,128)(2,1)} %copy-done.14, s16[32,32,128]{2,1,0:T(8,128)(2,1)} %copy-done.12, ...), custom_call_target="tpu_custom_call" | custom-call | tf_op jit(solution)/shard_map/update/pallas_call | solution.py:299
  93.9 5.5 %collective-permute-done.24.refs_5_ = bf16[32,32,128]{2,1,0:T(8,128)(2,1)S(1)} collective-permute-done((bf16[32,32,128]{2,1,0:T(8,128)(2,1)}, bf16[32,32,128]{2,1,0:T(8,128)(2,1)S(1)}, u32[]{:S(2)}, u32[]{:S(2)}) %collective-permute-start.24) | collective-permute-done | bytes 262176 | tf_op jit(solution)/shard_map/ppermute | solution.py:310
  102.2 2.3 %collective-permute-done.27.refs_8_ = bf16[16,32,128]{2,1,0:T(8,128)(2,1)S(1)} collective-permute-done((bf16[16,32,128]{2,1,0:T(8,128)(2,1)S(1)}, bf16[16,32,128]{2,1,0:T(8,128)(2,1)S(1)}, u32[]{:S(2)}, u32[]{:S(2)}) %collective-permute-start.27) | collective-permute-done | bytes 131104 | tf_op jit(solution)/shard_map/ppermute | solution.py:310
  104.4 2.0 %collective-permute-done.26.refs_7_ = bf16[16,32,128]{2,1,0:T(8,128)(2,1)S(1)} collective-permute-done((bf16[16,32,128]{2,1,0:T(8,128)(2,1)S(1)}, bf16[16,32,128]{2,1,0:T(8,128)(2,1)S(1)}, u32[]{:S(2)}, u32[]{:S(2)}) %collective-permute-start.26) | collective-permute-done | bytes 131104 | tf_op jit(solution)/shard_map/ppermute | solution.py:310
  108.4 7.5 %read_tile.3 = (s16[4,16,32,128]{3,2,1,0:T(8,128)(2,1)}, f32[4,16,32,128]{3,2,1,0:T(8,128)}, s16[4,16,32,128]{3,2,1,0:T(8,128)(2,1)}, f32[4,16,32,128]{3,2,1,0:T(8,128)}) custom-call(s32[1]{0:T(128)} %bitcast.2.refs_0_, bf16[32,32,128]{2,1,0:T(8,128)(2,1)} %get-tuple-element.40.refs_1_, bf16[32,32,128]{2,1,0:T(8,128)(2,1)} %copy-done.13, ...), custom_call_target="tpu_custom_call" | custom-call | tf_op jit(solution)/shard_map/read_tile/pallas_call | solution.py:211
  121.7 6.4 %collective-permute-done.31 = s16[2,16,32,128]{3,2,1,0:T(8,128)(2,1)S(1)} collective-permute-done((s16[2,16,32,128]{3,2,1,0:T(8,128)(2,1)S(1)}, s16[2,16,32,128]{3,2,1,0:T(8,128)(2,1)S(1)}, u32[]{:S(2)}, u32[]{:S(2)}) %collective-permute-start.31) | collective-permute-done | bytes 262176 | tf_op jit(solution)/shard_map/ppermute | solution.py:310
  130.4 2.8 %collective-permute-done.32 = s16[1,16,32,128]{3,2,1,0:T(8,128)(2,1)S(1)} collective-permute-done((s16[1,16,32,128]{3,2,1,0:T(8,128)(2,1)S(1)}, s16[1,16,32,128]{3,2,1,0:T(8,128)(2,1)S(1)}, u32[]{:S(2)}, u32[]{:S(2)}) %collective-permute-start.32) | collective-permute-done | bytes 131104 | tf_op jit(solution)/shard_map/ppermute | solution.py:310
  134.8 2.6 %collective-permute-start.38 = (s16[32,32,128]{2,1,0:T(8,128)(2,1)S(1)}, s16[32,32,128]{2,1,0:T(8,128)(2,1)S(1)}, u32[]{:S(2)}, u32[]{:S(2)}) collective-permute-start(s16[32,32,128]{2,1,0:T(8,128)(2,1)S(1)} %pad_add_fusion.1.refs_1_), channel_id=1, source_target_pairs={{0,24},{8,16},{16,8},{24,0},{1,25},{9,17},{17,9},{25,1},{2,26},{10... | collective-permute-start | bytes 786440 | tf_op jit(solution)/shard_map/ppermute | solution.py:314
  137.4 1.9 %collective-permute-start.36 = (s16[32,32,128]{2,1,0:T(8,128)(2,1)S(1)}, s16[32,32,128]{2,1,0:T(8,128)(2,1)S(1)}, u32[]{:S(2)}, u32[]{:S(2)}) collective-permute-start(s16[32,32,128]{2,1,0:T(8,128)(2,1)S(1)} %pad_add_fusion.1.refs_1_), channel_id=1, source_target_pairs={{0,8},{8,0},{16,24},{24,16},{1,9},{9,1},{17,25},{25,17},{2,10},{10... | collective-permute-start | bytes 786440 | tf_op jit(solution)/shard_map/ppermute | solution.py:314
  139.3 3.8 %over_weight.3.refs_5_ = f32[32,64,256]{2,1,0:T(8,128)} custom-call(f32[32,64,256]{2,1,0:T(8,128)} %get-tuple-element.46.est_ref, f32[4,72,128]{2,1,0:T(8,128)} %copy-done, f32[4,64,256]{2,1,0:T(8,128)} %broadcast_multiply_fusion.pat_ref), custom_call_target="tpu_custom_call" | custom-call | tf_op jit(solution)/shard_map/over_weight/pallas_call | solution.py:238
  143.1 2.9 %collective-permute-done.38.refs_4_ = s16[32,32,128]{2,1,0:T(8,128)(2,1)S(1)} collective-permute-done((s16[32,32,128]{2,1,0:T(8,128)(2,1)S(1)}, s16[32,32,128]{2,1,0:T(8,128)(2,1)S(1)}, u32[]{:S(2)}, u32[]{:S(2)}) %collective-permute-start.38) | collective-permute-done | bytes 262176 | tf_op jit(solution)/shard_map/ppermute | solution.py:314
  146.0 11.3 %collective-permute-done.37.refs_3_ = s16[32,32,128]{2,1,0:T(8,128)(2,1)S(1)} collective-permute-done((s16[32,32,128]{2,1,0:T(8,128)(2,1)S(1)}, s16[32,32,128]{2,1,0:T(8,128)(2,1)S(1)}, u32[]{:S(2)}, u32[]{:S(2)}) %collective-permute-start.37) | collective-permute-done | bytes 262176 | tf_op jit(solution)/shard_map/ppermute | solution.py:314
  158.6 8.2 %update.3 = f32[32,64,256]{2,1,0:T(8,128)} custom-call(s32[3]{0:T(128)} %pad_add_fusion.2.refs_0_, s16[32,32,128]{2,1,0:T(8,128)(2,1)} %copy-done.2, s16[32,32,128]{2,1,0:T(8,128)(2,1)} %copy-done.20, s16[32,32,128]{2,1,0:T(8,128)(2,1)} %copy-done.19, s16[32,32,128]{2,1,0:T(8,128)(2,1)} %copy-done.18, f32[32,64,256]{2,1,0:T(8,128)} %over_weight.3.refs_5_, ...), custom_call_target="tpu_custom_call" | custom-call | tf_op jit(solution)/shard_map/update/pallas_call | solution.py:299
  (227 shorter events, 57.3 us)
Async XLA Ops:
  6.9 9.7 %collective-permute-start.3 = (bf16[33,32,128]{2,1,0:T(8,128)(2,1)}, bf16[33,32,128]{2,1,0:T(8,128)(2,1)S(1)}, u32[]{:S(2)}, u32[]{:S(2)}) collective-permute-start(bf16[33,32,128]{2,1,0:T(8,128)(2,1)} %first_crop.1.refs_1_), channel_id=1, source_target_pairs={{0,4},{1,5},{2,6},{3,7},{4,0},{5,1},{6,2},{7,3},{8,12},{9,13},{10,... | collective-permute-start | bytes 811016 | tf_op jit(solution)/shard_map/ppermute | solution.py:310
  9.9 8.5 %collective-permute-start.1 = (bf16[33,32,128]{2,1,0:T(8,128)(2,1)}, bf16[33,32,128]{2,1,0:T(8,128)(2,1)S(1)}, u32[]{:S(2)}, u32[]{:S(2)}) collective-permute-start(bf16[33,32,128]{2,1,0:T(8,128)(2,1)} %first_crop.1.refs_1_), channel_id=1, source_target_pairs={{0,2},{1,3},{2,0},{3,1},{4,6},{5,7},{6,4},{7,5},{8,10},{9,11},{10,... | collective-permute-start | bytes 811016 | tf_op jit(solution)/shard_map/ppermute | solution.py:310
  11.4 13.4 %collective-permute-start = (bf16[33,32,128]{2,1,0:T(8,128)(2,1)}, bf16[33,32,128]{2,1,0:T(8,128)(2,1)S(1)}, u32[]{:S(2)}, u32[]{:S(2)}) collective-permute-start(bf16[33,32,128]{2,1,0:T(8,128)(2,1)} %first_crop.1.refs_1_), channel_id=1, source_target_pairs={{0,1},{1,0},{2,3},{3,2},{4,5},{5,4},{6,7},{7,6},{8,9},{9,8},{10,11... | collective-permute-start | bytes 811016 | tf_op jit(solution)/shard_map/ppermute | solution.py:310
  16.6 6.8 %collective-permute-start.6 = (bf16[17,32,128]{2,1,0:T(8,128)(2,1)S(1)}, bf16[17,32,128]{2,1,0:T(8,128)(2,1)S(1)}, u32[]{:S(2)}, u32[]{:S(2)}) collective-permute-start(bf16[17,32,128]{2,1,0:T(8,128)(2,1)S(1)} %slice.132), channel_id=1, source_target_pairs={{0,2},{1,3},{2,0},{3,1},{4,6},{5,7},{6,4},{7,5},{8,10},{9,11},{10,... | collective-permute-start | bytes 417800 | tf_op jit(solution)/shard_map/ppermute | solution.py:310
  18.4 5.0 %collective-permute-start.5 = (bf16[16,32,128]{2,1,0:T(8,128)(2,1)S(1)}, bf16[16,32,128]{2,1,0:T(8,128)(2,1)S(1)}, u32[]{:S(2)}, u32[]{:S(2)}) collective-permute-start(bf16[16,32,128]{2,1,0:T(8,128)(2,1)S(1)} %slice.131), channel_id=1, source_target_pairs={{0,4},{1,5},{2,6},{3,7},{4,0},{5,1},{6,2},{7,3},{8,12},{9,13},{10,... | collective-permute-start | bytes 393224 | tf_op jit(solution)/shard_map/ppermute | solution.py:310
  38.2 7.0 %collective-permute-start.17 = (f32[72,128]{1,0:T(8,128)S(1)}, f32[72,128]{1,0:T(8,128)S(1)}, u32[]{:S(2)}, u32[]{:S(2)}) collective-permute-start(f32[72,128]{1,0:T(8,128)S(1)} %fusion.47), channel_id=1, source_target_pairs={{0,24},{8,16},{16,8},{24,0},{1,25},{9,17},{17,9},{25,1},{2,26},{10... | collective-permute-start | bytes 110600 | tf_op jit(solution)/shard_map/ppermute | solution.py:314
  42.6 7.7 %collective-permute-start.11 = (s16[2,16,32,128]{3,2,1,0:T(8,128)(2,1)S(1)}, s16[2,16,32,128]{3,2,1,0:T(8,128)(2,1)S(1)}, u32[]{:S(2)}, u32[]{:S(2)}) collective-permute-start(s16[2,16,32,128]{3,2,1,0:T(8,128)(2,1)S(1)} %get-tuple-element.32), channel_id=1, source_target_pairs={{0,2},{1,3},{2,0},{3,1},{4,6},{5,7},{6,4},{7,5},{8,10},{9,11},{10,... | collective-permute-start | bytes 786440 | tf_op jit(solution)/shard_map/ppermute | solution.py:310
  44.3 7.7 %collective-permute-start.13 = (s16[2,16,32,128]{3,2,1,0:T(8,128)(2,1)S(1)}, s16[2,16,32,128]{3,2,1,0:T(8,128)(2,1)S(1)}, u32[]{:S(2)}, u32[]{:S(2)}) collective-permute-start(s16[2,16,32,128]{3,2,1,0:T(8,128)(2,1)S(1)} %get-tuple-element.34), channel_id=1, source_target_pairs={{0,4},{1,5},{2,6},{3,7},{4,0},{5,1},{6,2},{7,3},{8,12},{9,13},{10,... | collective-permute-start | bytes 786440 | tf_op jit(solution)/shard_map/ppermute | solution.py:310
  50.4 5.0 %collective-permute-start.12 = (s16[1,16,32,128]{3,2,1,0:T(8,128)(2,1)S(1)}, s16[1,16,32,128]{3,2,1,0:T(8,128)(2,1)S(1)}, u32[]{:S(2)}, u32[]{:S(2)}) collective-permute-start(s16[1,16,32,128]{3,2,1,0:T(8,128)(2,1)S(1)} %fusion.26), channel_id=1, source_target_pairs={{0,4},{1,5},{2,6},{3,7},{4,0},{5,1},{6,2},{7,3},{8,12},{9,13},{10,... | collective-permute-start | bytes 393224 | tf_op jit(solution)/shard_map/ppermute | solution.py:310
  52.2 5.0 %collective-permute-start.14 = (s16[1,16,32,128]{3,2,1,0:T(8,128)(2,1)S(1)}, s16[1,16,32,128]{3,2,1,0:T(8,128)(2,1)S(1)}, u32[]{:S(2)}, u32[]{:S(2)}) collective-permute-start(s16[1,16,32,128]{3,2,1,0:T(8,128)(2,1)S(1)} %fusion.21), channel_id=1, source_target_pairs={{0,2},{1,3},{2,0},{3,1},{4,6},{5,7},{6,4},{7,5},{8,10},{9,11},{10,... | collective-permute-start | bytes 393224 | tf_op jit(solution)/shard_map/ppermute | solution.py:310
  57.8 16.2 %collective-permute-start.20 = (s16[32,32,128]{2,1,0:T(8,128)(2,1)S(1)}, s16[32,32,128]{2,1,0:T(8,128)(2,1)S(1)}, u32[]{:S(2)}, u32[]{:S(2)}) collective-permute-start(s16[32,32,128]{2,1,0:T(8,128)(2,1)S(1)} %pad_add_fusion.refs_1_), channel_id=1, source_target_pairs={{0,24},{8,16},{16,8},{24,0},{1,25},{9,17},{17,9},{25,1},{2,26},{10... | collective-permute-start | bytes 786440 | tf_op jit(solution)/shard_map/ppermute | solution.py:314
  61.4 20.1 %collective-permute-start.19 = (s16[32,32,128]{2,1,0:T(8,128)(2,1)S(1)}, s16[32,32,128]{2,1,0:T(8,128)(2,1)S(1)}, u32[]{:S(2)}, u32[]{:S(2)}) collective-permute-start(s16[32,32,128]{2,1,0:T(8,128)(2,1)S(1)} %pad_add_fusion.refs_1_), channel_id=1, source_target_pairs={{0,16},{8,24},{16,0},{24,8},{1,17},{9,25},{17,1},{25,9},{2,18},{10... | collective-permute-start | bytes 786440 | tf_op jit(solution)/shard_map/ppermute | solution.py:314
  61.4 20.1 %collective-permute-start.18 = (s16[32,32,128]{2,1,0:T(8,128)(2,1)S(1)}, s16[32,32,128]{2,1,0:T(8,128)(2,1)S(1)}, u32[]{:S(2)}, u32[]{:S(2)}) collective-permute-start(s16[32,32,128]{2,1,0:T(8,128)(2,1)S(1)} %pad_add_fusion.refs_1_), channel_id=1, source_target_pairs={{0,8},{8,0},{16,24},{24,16},{1,9},{9,1},{17,25},{25,17},{2,10},{10... | collective-permute-start | bytes 786440 | tf_op jit(solution)/shard_map/ppermute | solution.py:314
  91.8 7.6 %collective-permute-start.24 = (bf16[32,32,128]{2,1,0:T(8,128)(2,1)}, bf16[32,32,128]{2,1,0:T(8,128)(2,1)S(1)}, u32[]{:S(2)}, u32[]{:S(2)}) collective-permute-start(bf16[32,32,128]{2,1,0:T(8,128)(2,1)} %get-tuple-element.40.refs_1_), channel_id=1, source_target_pairs={{0,4},{1,5},{2,6},{3,7},{4,0},{5,1},{6,2},{7,3},{8,12},{9,13},{10,... | collective-permute-start | bytes 786440 | tf_op jit(solution)/shard_map/ppermute | solution.py:310
  92.1 8.2 %collective-permute-start.22 = (bf16[32,32,128]{2,1,0:T(8,128)(2,1)}, bf16[32,32,128]{2,1,0:T(8,128)(2,1)S(1)}, u32[]{:S(2)}, u32[]{:S(2)}) collective-permute-start(bf16[32,32,128]{2,1,0:T(8,128)(2,1)} %get-tuple-element.40.refs_1_), channel_id=1, source_target_pairs={{0,2},{1,3},{2,0},{3,1},{4,6},{5,7},{6,4},{7,5},{8,10},{9,11},{10,... | collective-permute-start | bytes 786440 | tf_op jit(solution)/shard_map/ppermute | solution.py:310
  93.9 12.5 %collective-permute-start.21 = (bf16[32,32,128]{2,1,0:T(8,128)(2,1)}, bf16[32,32,128]{2,1,0:T(8,128)(2,1)S(1)}, u32[]{:S(2)}, u32[]{:S(2)}) collective-permute-start(bf16[32,32,128]{2,1,0:T(8,128)(2,1)} %get-tuple-element.40.refs_1_), channel_id=1, source_target_pairs={{0,1},{1,0},{2,3},{3,2},{4,5},{5,4},{6,7},{7,6},{8,9},{9,8},{10,11... | collective-permute-start | bytes 786440 | tf_op jit(solution)/shard_map/ppermute | solution.py:310
  100.4 6.1 %collective-permute-start.25 = (bf16[32,32,128]{2,1,0:T(8,128)(2,1)S(1)}, bf16[32,32,128]{2,1,0:T(8,128)(2,1)S(1)}, u32[]{:S(2)}, u32[]{:S(2)}) collective-permute-start(bf16[32,32,128]{2,1,0:T(8,128)(2,1)S(1)} %collective-permute-done.24.refs_5_), channel_id=1, source_target_pairs={{0,1},{1,0},{2,3},{3,2},{4,5},{5,4},{6,7},{7,6},{8,9},{9,8},{10,11... | collective-permute-start | bytes 786440 | tf_op jit(solution)/shard_map/ppermute | solution.py:310
  100.4 6.1 %collective-permute-start.23 = (bf16[32,32,128]{2,1,0:T(8,128)(2,1)S(1)}, bf16[32,32,128]{2,1,0:T(8,128)(2,1)S(1)}, u32[]{:S(2)}, u32[]{:S(2)}) collective-permute-start(bf16[32,32,128]{2,1,0:T(8,128)(2,1)S(1)} %collective-permute-done.22.refs_3_), channel_id=1, source_target_pairs={{0,1},{1,0},{2,3},{3,2},{4,5},{5,4},{6,7},{7,6},{8,9},{9,8},{10,11... | collective-permute-start | bytes 786440 | tf_op jit(solution)/shard_map/ppermute | solution.py:310
  101.0 5.5 %collective-permute-start.26 = (bf16[16,32,128]{2,1,0:T(8,128)(2,1)S(1)}, bf16[16,32,128]{2,1,0:T(8,128)(2,1)S(1)}, u32[]{:S(2)}, u32[]{:S(2)}) collective-permute-start(bf16[16,32,128]{2,1,0:T(8,128)(2,1)S(1)} %slice.141), channel_id=1, source_target_pairs={{0,4},{1,5},{2,6},{3,7},{4,0},{5,1},{6,2},{7,3},{8,12},{9,13},{10,... | collective-permute-start | bytes 393224 | tf_op jit(solution)/shard_map/ppermute | solution.py:310
  119.7 8.4 %collective-permute-start.31 = (s16[2,16,32,128]{3,2,1,0:T(8,128)(2,1)S(1)}, s16[2,16,32,128]{3,2,1,0:T(8,128)(2,1)S(1)}, u32[]{:S(2)}, u32[]{:S(2)}) collective-permute-start(s16[2,16,32,128]{3,2,1,0:T(8,128)(2,1)S(1)} %fusion.5), channel_id=1, source_target_pairs={{0,2},{1,3},{2,0},{3,1},{4,6},{5,7},{6,4},{7,5},{8,10},{9,11},{10,... | collective-permute-start | bytes 786440 | tf_op jit(solution)/shard_map/ppermute | solution.py:310
  121.2 8.3 %collective-permute-start.34 = (s16[2,16,32,128]{3,2,1,0:T(8,128)(2,1)S(1)}, s16[2,16,32,128]{3,2,1,0:T(8,128)(2,1)S(1)}, u32[]{:S(2)}, u32[]{:S(2)}) collective-permute-start(s16[2,16,32,128]{3,2,1,0:T(8,128)(2,1)S(1)} %fusion.3), channel_id=1, source_target_pairs={{0,4},{1,5},{2,6},{3,7},{4,0},{5,1},{6,2},{7,3},{8,12},{9,13},{10,... | collective-permute-start | bytes 786440 | tf_op jit(solution)/shard_map/ppermute | solution.py:310
  134.8 11.1 %collective-permute-start.38 = (s16[32,32,128]{2,1,0:T(8,128)(2,1)S(1)}, s16[32,32,128]{2,1,0:T(8,128)(2,1)S(1)}, u32[]{:S(2)}, u32[]{:S(2)}) collective-permute-start(s16[32,32,128]{2,1,0:T(8,128)(2,1)S(1)} %pad_add_fusion.1.refs_1_), channel_id=1, source_target_pairs={{0,24},{8,16},{16,8},{24,0},{1,25},{9,17},{17,9},{25,1},{2,26},{10... | collective-permute-start | bytes 786440 | tf_op jit(solution)/shard_map/ppermute | solution.py:314
  137.4 19.8 %collective-permute-start.37 = (s16[32,32,128]{2,1,0:T(8,128)(2,1)S(1)}, s16[32,32,128]{2,1,0:T(8,128)(2,1)S(1)}, u32[]{:S(2)}, u32[]{:S(2)}) collective-permute-start(s16[32,32,128]{2,1,0:T(8,128)(2,1)S(1)} %pad_add_fusion.1.refs_1_), channel_id=1, source_target_pairs={{0,16},{8,24},{16,0},{24,8},{1,17},{9,25},{17,1},{25,9},{2,18},{10... | collective-permute-start | bytes 786440 | tf_op jit(solution)/shard_map/ppermute | solution.py:314
  137.4 19.8 %collective-permute-start.36 = (s16[32,32,128]{2,1,0:T(8,128)(2,1)S(1)}, s16[32,32,128]{2,1,0:T(8,128)(2,1)S(1)}, u32[]{:S(2)}, u32[]{:S(2)}) collective-permute-start(s16[32,32,128]{2,1,0:T(8,128)(2,1)S(1)} %pad_add_fusion.1.refs_1_), channel_id=1, source_target_pairs={{0,8},{8,0},{16,24},{24,16},{1,9},{9,1},{17,25},{25,17},{2,10},{10... | collective-permute-start | bytes 786440 | tf_op jit(solution)/shard_map/ppermute | solution.py:314
  (46 other events, 159.0 us)

commit v6 on v5

--- a/solution.py
+++ b/solution.py
@@ -72,6 +72,7 @@
         ],
         out_specs=pl.BlockSpec(memory_space=pltpu.VMEM),
         scratch_shapes=[pltpu.VMEM((rows * (tile_y + 8), tile_z), F32)],
+        compiler_params=pltpu.CompilerParams(vmem_limit_bytes=24 << 20),
         name="first_crop",
     )(shifts, estimate, lines)
 
@@ -214,6 +215,9 @@
         in_specs=[pl.BlockSpec(memory_space=pltpu.SMEM)] + [vmem] * (n_flat + 6 + known),
         out_specs=(vmem,) * len(shapes),
         scratch_shapes=[pltpu.VMEM((tile_x * tile_y, tile_z), F32)] * 2,
+        compiler_params=pltpu.CompilerParams(
+            vmem_limit_bytes=(24 << 20) if owners <= 8 else None
+        ),
         name="read_tile",
     )(me, *flat, measured, mass, gather_mat, scatter_mat, z_mat, y_mat, *([scale] if known else []))
 
@@ -240,6 +244,7 @@
         out_shape=jax.ShapeDtypeStruct(estimate.shape, F32),
         in_specs=[vmem] * 3,
         out_specs=vmem,
+        compiler_params=pltpu.CompilerParams(vmem_limit_bytes=24 << 20),
         name="over_weight",
     )(estimate, metas, outline)
 
@@ -302,6 +307,7 @@
         in_specs=[pl.BlockSpec(memory_space=pltpu.SMEM)] + [vmem] * (views + 4),
         out_specs=(vmem,) * len(shapes),
         scratch_shapes=scratch,
+        compiler_params=pltpu.CompilerParams(vmem_limit_bytes=24 << 20),
         name="update",
     )(scalars, *sums, ratio, metas, z_place, y_place)
 

time: 167 us -> 153 us (0.916)
  Pallas kernels: 42.9 us -> 25.2 us
    pallas_call x2, Pallas kernels: 15.2 us -> 9.04 us  [read_tile(): pl.pallas_call(kernel, out_shape=tuple(shapes), in_specs=[pl.BlockSpec(me...]
    pallas_call x2, Pallas kernels: 7.59 us -> 1.65 us  [over_weight(): pl.pallas_call(kernel, out_shape=jax.ShapeDtypeStruct(estimate.shape, F32...]
    pallas_call x2, Pallas kernels: 17.1 us -> 13.2 us  [update(): pl.pallas_call(kernel, out_shape=tuple(shapes), in_specs=[pl.BlockSpec(me...]
    convert_element_type x5, other arithmetic: 0.25 us -> 3.14 us  [split_outside(): return (hi.astype(BF16), lax.reduce_precision(x - hi, 8, 7).astype(BF16))]
    add x8, other arithmetic: 3.76 us -> 1.14 us  [on_device(): total = keep[h] + got.astype(F32)]
    reduce_sum x1, local copies, waits for them, and re-layouts: 0.2 us -> 2.19 us  [band(): return jnp.sum(jnp.where(hit, taps, 0.0), axis=-1)]
    unnamed x63 -> x35, local copies, waits for them, and re-layouts: 5.3 us -> 3.33 us
    ppermute x9, waiting for transfers between devices: 23 us -> 24.8 us  [pair_views(): return lax.ppermute(x, 'view', [(i, i ^ bit) for i in range(count)])]
  transfers between devices with their start and end apart: 39 -> 39, of which waited for: 19 -> 19; matrix products, arithmetic and copies ran while one was open for 11% -> 13% of each run, Pallas kernels for 5% -> 1%
where the time goes in v6:
time: 153 us
  waiting for transfers between devices  61 us (40%)
  starting transfers between devices  37.1 us (24%)
  Pallas kernels  25.2 us (16%)
  other arithmetic  20.6 us (13%)
  local copies, waits for them, and re-layouts  7.68 us (5%)
    ppermute x30, waiting for transfers between devices, flip(): return lax.ppermute(x, 'brick', [(i, i ^ bit) for i in range(count)])  36.2 us
    ppermute x9, waiting for transfers between devices, pair_views(): return lax.ppermute(x, 'view', [(i, i ^ bit) for i in range(count)])  24.8 us
    ppermute x30, starting transfers between devices, flip(): return lax.ppermute(x, 'brick', [(i, i ^ bit) for i in range(count)])  23.9 us
    ppermute x9, starting transfers between devices, pair_views(): return lax.ppermute(x, 'view', [(i, i ^ bit) for i in range(count)])  13.2 us
    pallas_call x2, Pallas kernels, update(): pl.pallas_call(kernel, out_shape=tuple(shapes), in_specs=[pl.BlockSpec(me...  13.2 us
    pallas_call x2, Pallas kernels, read_tile(): pl.pallas_call(kernel, out_shape=tuple(shapes), in_specs=[pl.BlockSpec(me...  9.04 us
    reduce_sum x4, other arithmetic, band(): return jnp.sum(jnp.where(hit, taps, 0.0), axis=-1)  3.78 us
    unnamed x35, local copies, waits for them, and re-layouts  3.33 us
  transfers between devices with their start and end apart: 39, of which 19 were waited for; matrix products, arithmetic and copies ran while one was open for 13% of the time, Pallas kernels for 1%

profile of v6, /device:TPU:0, one launch (start us, length us, event | category | flops | bytes accessed | tf_op | source)
XLA Modules:
  0.0 152.6 jit_solution(7230139791376869244)
XLA Ops:
  6.8 3.1 %collective-permute-start.3 = (bf16[33,32,128]{2,1,0:T(8,128)(2,1)S(1)}, bf16[33,32,128]{2,1,0:T(8,128)(2,1)S(1)}, u32[]{:S(2)}, u32[]{:S(2)}) collective-permute-start(bf16[33,32,128]{2,1,0:T(8,128)(2,1)S(1)} %first_crop.1.refs_1_), channel_id=1, source_target_pairs={{0,4},{1,5},{2,6},{3,7},{4,0},{5,1},{6,2},{7,3},{8,12},{9,13},{10,... | collective-permute-start | bytes 811016 | tf_op jit(solution)/shard_map/ppermute | solution.py:316
  14.5 1.8 %collective-permute-done.3.refs_5_ = bf16[33,32,128]{2,1,0:T(8,128)(2,1)S(1)} collective-permute-done((bf16[33,32,128]{2,1,0:T(8,128)(2,1)S(1)}, bf16[33,32,128]{2,1,0:T(8,128)(2,1)S(1)}, u32[]{:S(2)}, u32[]{:S(2)}) %collective-permute-start.3) | collective-permute-done | bytes 270368 | tf_op jit(solution)/shard_map/ppermute | solution.py:316
  21.6 2.9 %collective-permute-done.5.refs_7_ = bf16[16,32,128]{2,1,0:T(8,128)(2,1)S(1)} collective-permute-done((bf16[16,32,128]{2,1,0:T(8,128)(2,1)}, bf16[16,32,128]{2,1,0:T(8,128)(2,1)S(1)}, u32[]{:S(2)}, u32[]{:S(2)}) %collective-permute-start.5) | collective-permute-done | bytes 131104 | tf_op jit(solution)/shard_map/ppermute | solution.py:316
  26.1 4.6 %read_tile.2 = (s16[4,16,32,128]{3,2,1,0:T(8,128)(2,1)S(1)}, f32[4,16,32,128]{3,2,1,0:T(8,128)S(1)}, s16[4,16,32,128]{3,2,1,0:T(8,128)(2,1)S(1)}, f32[4,16,32,12...) custom-call(s32[1]{0:T(128)} %bitcast.2.refs_0_, bf16[33,32,128]{2,1,0:T(8,128)(2,1)S(1)} %first_crop.1.refs_1_, ...), custom_call_target="tpu_custom_call" | custom-call | tf_op jit(solution)/shard_map/read_tile/pallas_call | solution.py:212
  34.2 3.6 %collective-permute-start.17 = (f32[72,128]{1,0:T(8,128)S(1)}, f32[72,128]{1,0:T(8,128)S(1)}, u32[]{:S(2)}, u32[]{:S(2)}) collective-permute-start(f32[72,128]{1,0:T(8,128)S(1)} %fusion.47), channel_id=1, source_target_pairs={{0,24},{8,16},{16,8},{24,0},{1,25},{9,17},{17,9},{25,1},{2,26},{10... | collective-permute-start | bytes 110600 | tf_op jit(solution)/shard_map/ppermute | solution.py:320
  42.8 3.6 %collective-permute-done.11 = s16[2,16,32,128]{3,2,1,0:T(8,128)(2,1)S(1)} collective-permute-done((s16[2,16,32,128]{3,2,1,0:T(8,128)(2,1)S(1)}, s16[2,16,32,128]{3,2,1,0:T(8,128)(2,1)S(1)}, u32[]{:S(2)}, u32[]{:S(2)}) %collective-permute-start.11) | collective-permute-done | bytes 262176 | tf_op jit(solution)/shard_map/ppermute | solution.py:316
  49.3 2.3 %collective-permute-done.12 = s16[1,16,32,128]{3,2,1,0:T(8,128)(2,1)S(1)} collective-permute-done((s16[1,16,32,128]{3,2,1,0:T(8,128)(2,1)S(1)}, s16[1,16,32,128]{3,2,1,0:T(8,128)(2,1)S(1)}, u32[]{:S(2)}, u32[]{:S(2)}) %collective-permute-start.12) | collective-permute-done | bytes 131104 | tf_op jit(solution)/shard_map/ppermute | solution.py:316
  55.2 3.5 %collective-permute-start.20 = (s16[32,32,128]{2,1,0:T(8,128)(2,1)}, s16[32,32,128]{2,1,0:T(8,128)(2,1)}, u32[]{:S(2)}, u32[]{:S(2)}) collective-permute-start(s16[32,32,128]{2,1,0:T(8,128)(2,1)} %pad_add_fusion.refs_1_), channel_id=1, source_target_pairs={{0,24},{8,16},{16,8},{24,0},{1,25},{9,17},{17,9},{25,1},{2,26},{10... | collective-permute-start | bytes 786440 | tf_op jit(solution)/shard_map/ppermute | solution.py:320
  62.1 2.5 %select_reduce_fusion.1 = f32[4,128]{1,0:T(4,128)} fusion(f32[4,31]{1,0:T(4,128)S(1)} %bitcast.90, pred[128,128,31]{1,0,2:T(8,128)(4,1)S(1)} %iota_compare_fusion.2), kind=kLoop, calls=%fused_computation.2 | loop fusion | flops 4062720 | bytes 510448 | tf_op jit(solution)/shard_map/vmap()/reduce_sum | solution.py:471
  64.6 2.4 %select_reduce_fusion = f32[4,256,128]{2,1,0:T(8,128)} fusion(f32[4,31]{1,0:T(4,128)S(1)} %bitcast.91, s32[4,256,128]{2,1,0:T(8,128)S(1)} %subtract_add_fusion), kind=kLoop, calls=%fused_computation | loop fusion | flops 12058624 | bytes 1049072 | tf_op jit(solution)/shard_map/vmap()/reduce_sum | solution.py:34
  67.0 2.2 %copy.31 = f32[4,256,128]{1,2,0:T(8,128)} copy(f32[4,256,128]{2,1,0:T(8,128)} %select_reduce_fusion) | data formatting | bytes 1048576 | tf_op jit(solution)/shard_map/vmap()/reduce_sum | solution.py:34
  72.8 6.4 %collective-permute-done.19.refs_3_ = s16[32,32,128]{2,1,0:T(8,128)(2,1)} collective-permute-done((s16[32,32,128]{2,1,0:T(8,128)(2,1)}, s16[32,32,128]{2,1,0:T(8,128)(2,1)}, u32[]{:S(2)}, u32[]{:S(2)}) %collective-permute-start.19) | collective-permute-done | bytes 262176 | tf_op jit(solution)/shard_map/ppermute | solution.py:320
  79.2 6.8 %update.2 = (f32[32,64,256]{2,1,0:T(8,128)S(1)}, bf16[32,32,128]{2,1,0:T(8,128)(2,1)S(1)}) custom-call(s32[3]{0:T(128)S(1)} %copy-done.11, s16[32,32,128]{2,1,0:T(8,128)(2,1)} %pad_add_fusion.refs_1_, s16[32,32,128]{2,1,0:T(8,128)(2,1)} %collective-permute-done.18.refs_2_, s16[32,32,128]{2,1,0:T(8,128)(2,1)} %collective-permute-done.19.refs_3_, ...), custom_call_target="tpu_custom_call" | custom-call | tf_op jit(solution)/shard_map/update/pallas_call | solution.py:304
  86.4 1.8 %collective-permute-start.22 = (bf16[32,32,128]{2,1,0:T(8,128)(2,1)S(1)}, bf16[32,32,128]{2,1,0:T(8,128)(2,1)S(1)}, u32[]{:S(2)}, u32[]{:S(2)}) collective-permute-start(bf16[32,32,128]{2,1,0:T(8,128)(2,1)S(1)} %get-tuple-element.40.refs_1_), channel_id=1, source_target_pairs={{0,2},{1,3},{2,0},{3,1},{4,6},{5,7},{6,4},{7,5},{8,10},{9,11},{10,... | collective-permute-start | bytes 786440 | tf_op jit(solution)/shard_map/ppermute | solution.py:316
  88.2 5.2 %collective-permute-done.24.refs_5_ = bf16[32,32,128]{2,1,0:T(8,128)(2,1)S(1)} collective-permute-done((bf16[32,32,128]{2,1,0:T(8,128)(2,1)S(1)}, bf16[32,32,128]{2,1,0:T(8,128)(2,1)S(1)}, u32[]{:S(2)}, u32[]{:S(2)}) %collective-permute-start.24) | collective-permute-done | bytes 262176 | tf_op jit(solution)/shard_map/ppermute | solution.py:316
  96.3 2.2 %collective-permute-done.27.refs_8_ = bf16[16,32,128]{2,1,0:T(8,128)(2,1)S(1)} collective-permute-done((bf16[16,32,128]{2,1,0:T(8,128)(2,1)S(1)}, bf16[16,32,128]{2,1,0:T(8,128)(2,1)S(1)}, u32[]{:S(2)}, u32[]{:S(2)}) %collective-permute-start.27) | collective-permute-done | bytes 131104 | tf_op jit(solution)/shard_map/ppermute | solution.py:316
  101.6 4.4 %read_tile.3 = (s16[4,16,32,128]{3,2,1,0:T(8,128)(2,1)S(1)}, f32[4,16,32,128]{3,2,1,0:T(8,128)S(1)}, s16[4,16,32,128]{3,2,1,0:T(8,128)(2,1)S(1)}, f32[4,16,32,128]{3,2,1,0:T(8,128)S(1)}) custom-call(s32[1]{0:T(128)} %bitcast.2.refs_0_, bf16[32,32,128]{2,1,0:T(8,128)(2,1)S(1)} %get-tuple-element.40.refs_1_, ...), custom_call_target="tpu_custom_call" | custom-call | tf_op jit(solution)/shard_map/read_tile/pallas_call | solution.py:212
  110.6 6.1 %collective-permute-done.31 = s16[2,16,32,128]{3,2,1,0:T(8,128)(2,1)S(1)} collective-permute-done((s16[2,16,32,128]{3,2,1,0:T(8,128)(2,1)S(1)}, s16[2,16,32,128]{3,2,1,0:T(8,128)(2,1)S(1)}, u32[]{:S(2)}, u32[]{:S(2)}) %collective-permute-start.31) | collective-permute-done | bytes 262176 | tf_op jit(solution)/shard_map/ppermute | solution.py:316
  119.0 2.8 %collective-permute-done.32 = s16[1,16,32,128]{3,2,1,0:T(8,128)(2,1)S(1)} collective-permute-done((s16[1,16,32,128]{3,2,1,0:T(8,128)(2,1)S(1)}, s16[1,16,32,128]{3,2,1,0:T(8,128)(2,1)S(1)}, u32[]{:S(2)}, u32[]{:S(2)}) %collective-permute-start.32) | collective-permute-done | bytes 131104 | tf_op jit(solution)/shard_map/ppermute | solution.py:316
  123.7 2.5 %collective-permute-start.38 = (s16[32,32,128]{2,1,0:T(8,128)(2,1)S(1)}, s16[32,32,128]{2,1,0:T(8,128)(2,1)S(1)}, u32[]{:S(2)}, u32[]{:S(2)}) collective-permute-start(s16[32,32,128]{2,1,0:T(8,128)(2,1)S(1)} %pad_add_fusion.1.refs_1_), channel_id=1, source_target_pairs={{0,24},{8,16},{16,8},{24,0},{1,25},{9,17},{17,9},{25,1},{2,26},{10... | collective-permute-start | bytes 786440 | tf_op jit(solution)/shard_map/ppermute | solution.py:320
  126.3 1.9 %collective-permute-start.36 = (s16[32,32,128]{2,1,0:T(8,128)(2,1)S(1)}, s16[32,32,128]{2,1,0:T(8,128)(2,1)S(1)}, u32[]{:S(2)}, u32[]{:S(2)}) collective-permute-start(s16[32,32,128]{2,1,0:T(8,128)(2,1)S(1)} %pad_add_fusion.1.refs_1_), channel_id=1, source_target_pairs={{0,8},{8,0},{16,24},{24,16},{1,9},{9,1},{17,25},{25,17},{2,10},{10... | collective-permute-start | bytes 786440 | tf_op jit(solution)/shard_map/ppermute | solution.py:320
  129.0 5.9 %collective-permute-done.38.refs_4_ = s16[32,32,128]{2,1,0:T(8,128)(2,1)S(1)} collective-permute-done((s16[32,32,128]{2,1,0:T(8,128)(2,1)S(1)}, s16[32,32,128]{2,1,0:T(8,128)(2,1)S(1)}, u32[]{:S(2)}, u32[]{:S(2)}) %collective-permute-start.38) | collective-permute-done | bytes 262176 | tf_op jit(solution)/shard_map/ppermute | solution.py:320
  134.9 11.2 %collective-permute-done.37.refs_3_ = s16[32,32,128]{2,1,0:T(8,128)(2,1)S(1)} collective-permute-done((s16[32,32,128]{2,1,0:T(8,128)(2,1)S(1)}, s16[32,32,128]{2,1,0:T(8,128)(2,1)S(1)}, u32[]{:S(2)}, u32[]{:S(2)}) %collective-permute-start.37) | collective-permute-done | bytes 262176 | tf_op jit(solution)/shard_map/ppermute | solution.py:320
  146.1 6.5 %update.3 = f32[32,64,256]{2,1,0:T(8,128)} custom-call(s32[3]{0:T(128)S(1)} %copy-done.11, s16[32,32,128]{2,1,0:T(8,128)(2,1)S(1)} %pad_add_fusion.1.refs_1_, s16[32,32,128]{2,1,0:T(8,128)(2,1)S(1)} %collective-permute-done.36.refs_2_, s16[32,32,128]{2,1,0:T(8,128)(2,1)S(1)} %collective-permute-done.37.refs_3_, ...), custom_call_target="tpu_custom_call" | custom-call | tf_op jit(solution)/shard_map/update/pallas_call | solution.py:304
  (199 shorter events, 55.7 us)
Async XLA Ops:
  6.8 9.5 %collective-permute-start.3 = (bf16[33,32,128]{2,1,0:T(8,128)(2,1)S(1)}, bf16[33,32,128]{2,1,0:T(8,128)(2,1)S(1)}, u32[]{:S(2)}, u32[]{:S(2)}) collective-permute-start(bf16[33,32,128]{2,1,0:T(8,128)(2,1)S(1)} %first_crop.1.refs_1_), channel_id=1, source_target_pairs={{0,4},{1,5},{2,6},{3,7},{4,0},{5,1},{6,2},{7,3},{8,12},{9,13},{10,... | collective-permute-start | bytes 811016 | tf_op jit(solution)/shard_map/ppermute | solution.py:316
  9.8 8.9 %collective-permute-start.1 = (bf16[33,32,128]{2,1,0:T(8,128)(2,1)S(1)}, bf16[33,32,128]{2,1,0:T(8,128)(2,1)S(1)}, u32[]{:S(2)}, u32[]{:S(2)}) collective-permute-start(bf16[33,32,128]{2,1,0:T(8,128)(2,1)S(1)} %first_crop.1.refs_1_), channel_id=1, source_target_pairs={{0,2},{1,3},{2,0},{3,1},{4,6},{5,7},{6,4},{7,5},{8,10},{9,11},{10,... | collective-permute-start | bytes 811016 | tf_op jit(solution)/shard_map/ppermute | solution.py:316
  11.3 14.7 %collective-permute-start = (bf16[33,32,128]{2,1,0:T(8,128)(2,1)S(1)}, bf16[33,32,128]{2,1,0:T(8,128)(2,1)S(1)}, u32[]{:S(2)}, u32[]{:S(2)}) collective-permute-start(bf16[33,32,128]{2,1,0:T(8,128)(2,1)S(1)} %first_crop.1.refs_1_), channel_id=1, source_target_pairs={{0,1},{1,0},{2,3},{3,2},{4,5},{5,4},{6,7},{7,6},{8,9},{9,8},{10,11... | collective-permute-start | bytes 811016 | tf_op jit(solution)/shard_map/ppermute | solution.py:316
  17.0 7.6 %collective-permute-start.6 = (bf16[17,32,128]{2,1,0:T(8,128)(2,1)}, bf16[17,32,128]{2,1,0:T(8,128)(2,1)S(1)}, u32[]{:S(2)}, u32[]{:S(2)}) collective-permute-start(bf16[17,32,128]{2,1,0:T(8,128)(2,1)} %slice.132), channel_id=1, source_target_pairs={{0,2},{1,3},{2,0},{3,1},{4,6},{5,7},{6,4},{7,5},{8,10},{9,11},{10,... | collective-permute-start | bytes 417800 | tf_op jit(solution)/shard_map/ppermute | solution.py:316
  19.4 5.2 %collective-permute-start.5 = (bf16[16,32,128]{2,1,0:T(8,128)(2,1)}, bf16[16,32,128]{2,1,0:T(8,128)(2,1)S(1)}, u32[]{:S(2)}, u32[]{:S(2)}) collective-permute-start(bf16[16,32,128]{2,1,0:T(8,128)(2,1)} %slice.131), channel_id=1, source_target_pairs={{0,4},{1,5},{2,6},{3,7},{4,0},{5,1},{6,2},{7,3},{8,12},{9,13},{10,... | collective-permute-start | bytes 393224 | tf_op jit(solution)/shard_map/ppermute | solution.py:316
  21.0 5.0 %collective-permute-start.4 = (bf16[33,32,128]{2,1,0:T(8,128)(2,1)S(1)}, bf16[33,32,128]{2,1,0:T(8,128)(2,1)S(1)}, u32[]{:S(2)}, u32[]{:S(2)}) collective-permute-start(bf16[33,32,128]{2,1,0:T(8,128)(2,1)S(1)} %collective-permute-done.3.refs_5_), channel_id=1, source_target_pairs={{0,1},{1,0},{2,3},{3,2},{4,5},{5,4},{6,7},{7,6},{8,9},{9,8},{10,11... | collective-permute-start | bytes 811016 | tf_op jit(solution)/shard_map/ppermute | solution.py:316
  34.2 7.1 %collective-permute-start.17 = (f32[72,128]{1,0:T(8,128)S(1)}, f32[72,128]{1,0:T(8,128)S(1)}, u32[]{:S(2)}, u32[]{:S(2)}) collective-permute-start(f32[72,128]{1,0:T(8,128)S(1)} %fusion.47), channel_id=1, source_target_pairs={{0,24},{8,16},{16,8},{24,0},{1,25},{9,17},{17,9},{25,1},{2,26},{10... | collective-permute-start | bytes 110600 | tf_op jit(solution)/shard_map/ppermute | solution.py:320
  38.7 7.8 %collective-permute-start.11 = (s16[2,16,32,128]{3,2,1,0:T(8,128)(2,1)S(1)}, s16[2,16,32,128]{3,2,1,0:T(8,128)(2,1)S(1)}, u32[]{:S(2)}, u32[]{:S(2)}) collective-permute-start(s16[2,16,32,128]{3,2,1,0:T(8,128)(2,1)S(1)} %get-tuple-element.32), channel_id=1, source_target_pairs={{0,2},{1,3},{2,0},{3,1},{4,6},{5,7},{6,4},{7,5},{8,10},{9,11},{10,... | collective-permute-start | bytes 786440 | tf_op jit(solution)/shard_map/ppermute | solution.py:316
  39.9 8.3 %collective-permute-start.13 = (s16[2,16,32,128]{3,2,1,0:T(8,128)(2,1)S(1)}, s16[2,16,32,128]{3,2,1,0:T(8,128)(2,1)S(1)}, u32[]{:S(2)}, u32[]{:S(2)}) collective-permute-start(s16[2,16,32,128]{3,2,1,0:T(8,128)(2,1)S(1)} %get-tuple-element.34), channel_id=1, source_target_pairs={{0,4},{1,5},{2,6},{3,7},{4,0},{5,1},{6,2},{7,3},{8,12},{9,13},{10,... | collective-permute-start | bytes 786440 | tf_op jit(solution)/shard_map/ppermute | solution.py:316
  46.6 5.0 %collective-permute-start.12 = (s16[1,16,32,128]{3,2,1,0:T(8,128)(2,1)S(1)}, s16[1,16,32,128]{3,2,1,0:T(8,128)(2,1)S(1)}, u32[]{:S(2)}, u32[]{:S(2)}) collective-permute-start(s16[1,16,32,128]{3,2,1,0:T(8,128)(2,1)S(1)} %fusion.26), channel_id=1, source_target_pairs={{0,4},{1,5},{2,6},{3,7},{4,0},{5,1},{6,2},{7,3},{8,12},{9,13},{10,... | collective-permute-start | bytes 393224 | tf_op jit(solution)/shard_map/ppermute | solution.py:316
  55.2 17.6 %collective-permute-start.20 = (s16[32,32,128]{2,1,0:T(8,128)(2,1)}, s16[32,32,128]{2,1,0:T(8,128)(2,1)}, u32[]{:S(2)}, u32[]{:S(2)}) collective-permute-start(s16[32,32,128]{2,1,0:T(8,128)(2,1)} %pad_add_fusion.refs_1_), channel_id=1, source_target_pairs={{0,24},{8,16},{16,8},{24,0},{1,25},{9,17},{17,9},{25,1},{2,26},{10... | collective-permute-start | bytes 786440 | tf_op jit(solution)/shard_map/ppermute | solution.py:320
  58.7 20.5 %collective-permute-start.19 = (s16[32,32,128]{2,1,0:T(8,128)(2,1)}, s16[32,32,128]{2,1,0:T(8,128)(2,1)}, u32[]{:S(2)}, u32[]{:S(2)}) collective-permute-start(s16[32,32,128]{2,1,0:T(8,128)(2,1)} %pad_add_fusion.refs_1_), channel_id=1, source_target_pairs={{0,16},{8,24},{16,0},{24,8},{1,17},{9,25},{17,1},{25,9},{2,18},{10... | collective-permute-start | bytes 786440 | tf_op jit(solution)/shard_map/ppermute | solution.py:320
  58.7 20.5 %collective-permute-start.18 = (s16[32,32,128]{2,1,0:T(8,128)(2,1)}, s16[32,32,128]{2,1,0:T(8,128)(2,1)}, u32[]{:S(2)}, u32[]{:S(2)}) collective-permute-start(s16[32,32,128]{2,1,0:T(8,128)(2,1)} %pad_add_fusion.refs_1_), channel_id=1, source_target_pairs={{0,8},{8,0},{16,24},{24,16},{1,9},{9,1},{17,25},{25,17},{2,10},{10... | collective-permute-start | bytes 786440 | tf_op jit(solution)/shard_map/ppermute | solution.py:320
  85.9 7.5 %collective-permute-start.24 = (bf16[32,32,128]{2,1,0:T(8,128)(2,1)S(1)}, bf16[32,32,128]{2,1,0:T(8,128)(2,1)S(1)}, u32[]{:S(2)}, u32[]{:S(2)}) collective-permute-start(bf16[32,32,128]{2,1,0:T(8,128)(2,1)S(1)} %get-tuple-element.40.refs_1_), channel_id=1, source_target_pairs={{0,4},{1,5},{2,6},{3,7},{4,0},{5,1},{6,2},{7,3},{8,12},{9,13},{10,... | collective-permute-start | bytes 786440 | tf_op jit(solution)/shard_map/ppermute | solution.py:316
  86.4 7.7 %collective-permute-start.22 = (bf16[32,32,128]{2,1,0:T(8,128)(2,1)S(1)}, bf16[32,32,128]{2,1,0:T(8,128)(2,1)S(1)}, u32[]{:S(2)}, u32[]{:S(2)}) collective-permute-start(bf16[32,32,128]{2,1,0:T(8,128)(2,1)S(1)} %get-tuple-element.40.refs_1_), channel_id=1, source_target_pairs={{0,2},{1,3},{2,0},{3,1},{4,6},{5,7},{6,4},{7,5},{8,10},{9,11},{10,... | collective-permute-start | bytes 786440 | tf_op jit(solution)/shard_map/ppermute | solution.py:316
  88.2 12.0 %collective-permute-start.21 = (bf16[32,32,128]{2,1,0:T(8,128)(2,1)S(1)}, bf16[32,32,128]{2,1,0:T(8,128)(2,1)S(1)}, u32[]{:S(2)}, u32[]{:S(2)}) collective-permute-start(bf16[32,32,128]{2,1,0:T(8,128)(2,1)S(1)} %get-tuple-element.40.refs_1_), channel_id=1, source_target_pairs={{0,1},{1,0},{2,3},{3,2},{4,5},{5,4},{6,7},{7,6},{8,9},{9,8},{10,11... | collective-permute-start | bytes 786440 | tf_op jit(solution)/shard_map/ppermute | solution.py:316
  94.1 6.1 %collective-permute-start.25 = (bf16[32,32,128]{2,1,0:T(8,128)(2,1)S(1)}, bf16[32,32,128]{2,1,0:T(8,128)(2,1)S(1)}, u32[]{:S(2)}, u32[]{:S(2)}) collective-permute-start(bf16[32,32,128]{2,1,0:T(8,128)(2,1)S(1)} %collective-permute-done.24.refs_5_), channel_id=1, source_target_pairs={{0,1},{1,0},{2,3},{3,2},{4,5},{5,4},{6,7},{7,6},{8,9},{9,8},{10,11... | collective-permute-start | bytes 786440 | tf_op jit(solution)/shard_map/ppermute | solution.py:316
  94.2 6.1 %collective-permute-start.23 = (bf16[32,32,128]{2,1,0:T(8,128)(2,1)S(1)}, bf16[32,32,128]{2,1,0:T(8,128)(2,1)S(1)}, u32[]{:S(2)}, u32[]{:S(2)}) collective-permute-start(bf16[32,32,128]{2,1,0:T(8,128)(2,1)S(1)} %collective-permute-done.22.refs_3_), channel_id=1, source_target_pairs={{0,1},{1,0},{2,3},{3,2},{4,5},{5,4},{6,7},{7,6},{8,9},{9,8},{10,11... | collective-permute-start | bytes 786440 | tf_op jit(solution)/shard_map/ppermute | solution.py:316
  94.7 5.5 %collective-permute-start.26 = (bf16[16,32,128]{2,1,0:T(8,128)(2,1)S(1)}, bf16[16,32,128]{2,1,0:T(8,128)(2,1)S(1)}, u32[]{:S(2)}, u32[]{:S(2)}) collective-permute-start(bf16[16,32,128]{2,1,0:T(8,128)(2,1)S(1)} %slice.141), channel_id=1, source_target_pairs={{0,4},{1,5},{2,6},{3,7},{4,0},{5,1},{6,2},{7,3},{8,12},{9,13},{10,... | collective-permute-start | bytes 393224 | tf_op jit(solution)/shard_map/ppermute | solution.py:316
  108.3 8.4 %collective-permute-start.31 = (s16[2,16,32,128]{3,2,1,0:T(8,128)(2,1)S(1)}, s16[2,16,32,128]{3,2,1,0:T(8,128)(2,1)S(1)}, u32[]{:S(2)}, u32[]{:S(2)}) collective-permute-start(s16[2,16,32,128]{3,2,1,0:T(8,128)(2,1)S(1)} %fusion.5), channel_id=1, source_target_pairs={{0,2},{1,3},{2,0},{3,1},{4,6},{5,7},{6,4},{7,5},{8,10},{9,11},{10,... | collective-permute-start | bytes 786440 | tf_op jit(solution)/shard_map/ppermute | solution.py:316
  110.0 8.4 %collective-permute-start.34 = (s16[2,16,32,128]{3,2,1,0:T(8,128)(2,1)S(1)}, s16[2,16,32,128]{3,2,1,0:T(8,128)(2,1)S(1)}, u32[]{:S(2)}, u32[]{:S(2)}) collective-permute-start(s16[2,16,32,128]{3,2,1,0:T(8,128)(2,1)S(1)} %fusion.3), channel_id=1, source_target_pairs={{0,4},{1,5},{2,6},{3,7},{4,0},{5,1},{6,2},{7,3},{8,12},{9,13},{10,... | collective-permute-start | bytes 786440 | tf_op jit(solution)/shard_map/ppermute | solution.py:316
  123.7 11.1 %collective-permute-start.38 = (s16[32,32,128]{2,1,0:T(8,128)(2,1)S(1)}, s16[32,32,128]{2,1,0:T(8,128)(2,1)S(1)}, u32[]{:S(2)}, u32[]{:S(2)}) collective-permute-start(s16[32,32,128]{2,1,0:T(8,128)(2,1)S(1)} %pad_add_fusion.1.refs_1_), channel_id=1, source_target_pairs={{0,24},{8,16},{16,8},{24,0},{1,25},{9,17},{17,9},{25,1},{2,26},{10... | collective-permute-start | bytes 786440 | tf_op jit(solution)/shard_map/ppermute | solution.py:320
  126.2 19.8 %collective-permute-start.37 = (s16[32,32,128]{2,1,0:T(8,128)(2,1)S(1)}, s16[32,32,128]{2,1,0:T(8,128)(2,1)S(1)}, u32[]{:S(2)}, u32[]{:S(2)}) collective-permute-start(s16[32,32,128]{2,1,0:T(8,128)(2,1)S(1)} %pad_add_fusion.1.refs_1_), channel_id=1, source_target_pairs={{0,16},{8,24},{16,0},{24,8},{1,17},{9,25},{17,1},{25,9},{2,18},{10... | collective-permute-start | bytes 786440 | tf_op jit(solution)/shard_map/ppermute | solution.py:320
  126.3 19.8 %collective-permute-start.36 = (s16[32,32,128]{2,1,0:T(8,128)(2,1)S(1)}, s16[32,32,128]{2,1,0:T(8,128)(2,1)S(1)}, u32[]{:S(2)}, u32[]{:S(2)}) collective-permute-start(s16[32,32,128]{2,1,0:T(8,128)(2,1)S(1)} %pad_add_fusion.1.refs_1_), channel_id=1, source_target_pairs={{0,8},{8,0},{16,24},{24,16},{1,9},{9,1},{17,25},{25,17},{2,10},{10... | collective-permute-start | bytes 786440 | tf_op jit(solution)/shard_map/ppermute | solution.py:320
  (32 other events, 236.5 us)

commit v7 on v6

--- a/solution.py
+++ b/solution.py
@@ -254,20 +254,22 @@
     rows, brick_y, brick_z = ratio.shape
     half = tile_y // 2
 
+    chunk = max(1, rows // 4)
+
     def kernel(*refs):
         s_ref = refs[0]
-        in_refs = refs[1 : 1 + views]
-        rt_ref, me_ref, zp_ref, yp_ref = refs[1 + views : 5 + views]
-        rest = refs[5 + views :]
-        out_ref = rest[0]
-        crop_ref = None if last else rest[1]
-        placed = rest[1] if last else rest[2]
+        sum_refs = refs[1 : 1 + views]
+        rt_ref, me_ref, zp_ref, yp_ref, out_ref = refs[1 + views : 6 + views]
+        crop_ref = None if last else refs[6 + views]
+        placed, rt_buf, out_buf, rt_sem, out_sem = refs[6 + views + (not last) :][:5]
+        rt_load = pltpu.make_async_copy(rt_ref, rt_buf, rt_sem)
+        rt_load.start()
         me = s_ref[2]
         for s in range(views):
             view = me ^ s
             unit = me_ref[view, 8 + rows : 8 + 2 * rows, :] * (bound / FULL)
             for h in range(2):
-                x = in_refs[s][h * half : (h + 1) * half].astype(jnp.int32)
+                x = sum_refs[s][h * half : (h + 1) * half].astype(jnp.int32)
                 x = (x.astype(F32) * unit[None]).reshape(half * rows, tile_z)
                 hi, lo = split(x)
                 out = dot(jnp.concatenate([hi, lo], axis=1), zp_ref[view, 0])
@@ -275,37 +277,55 @@
                 at = pl.multiple_of((view * 2 + h) * half * rows, half * rows)
                 for j in range(brick_z // tile_z):
                     placed[j, pl.ds(at, half * rows), :] = out[:, j * tile_z : (j + 1) * tile_z]
-
-        def step(r, carry):
-            x = jnp.concatenate(
-                [
-                    placed[j, pl.ds(r, views * tile_y, stride=rows), :]
-                    for j in range(brick_z // tile_z)
-                ],
-                axis=1,
-            )
-            hi, lo = split(x)
-            out = dot(yp_ref[...], jnp.concatenate([hi, lo], axis=0))
-            correction = out[:brick_y] + out[brick_y:]
-            out_ref[r] = rt_ref[r] * (1.0 + correction)
-            return carry
-
-        lax.fori_loop(0, rows, step, 0, unroll=UNROLL)
+        rt_load.wait()
+
+        def store(i):
+            some = pl.ds(i * chunk, chunk)
+            return pltpu.make_async_copy(out_buf.at[some], out_ref.at[some], out_sem.at[i])
+
+        for i in range(rows // chunk):
+
+            def step(j, carry, i=i):
+                r = i * chunk + j
+                x = jnp.concatenate(
+                    [
+                        placed[k, pl.ds(r, views * tile_y, stride=rows), :]
+                        for k in range(brick_z // tile_z)
+                    ],
+                    axis=1,
+                )
+                hi, lo = split(x)
+                out = dot(yp_ref[...], jnp.concatenate([hi, lo], axis=0))
+                correction = out[:brick_y] + out[brick_y:]
+                out_buf[r] = rt_buf[r] * (1.0 + correction)
+                return carry
+
+            lax.fori_loop(0, chunk, step, 0, unroll=UNROLL)
+            store(i).start()
         if not last:
-            put_crop(crop_ref, out_ref, rest[3], s_ref[0], s_ref[1], tile_y, tile_z)
+            put_crop(crop_ref, out_buf, refs[-1], s_ref[0], s_ref[1], tile_y, tile_z)
+        for i in range(rows // chunk):
+            store(i).wait()
 
     vmem = pl.BlockSpec(memory_space=pltpu.VMEM)
+    where = pl.BlockSpec(memory_space=pl.ANY)
     shapes = [jax.ShapeDtypeStruct(ratio.shape, F32)]
     if not last:
         shapes.append(jax.ShapeDtypeStruct((tile_y, rows, tile_z), BF16))
-    scratch = [pltpu.VMEM((brick_z // tile_z, views * tile_y * rows, tile_z), F32)]
+    scratch = [
+        pltpu.VMEM((brick_z // tile_z, views * tile_y * rows, tile_z), F32),
+        pltpu.VMEM(ratio.shape, F32),
+        pltpu.VMEM(ratio.shape, F32),
+        pltpu.SemaphoreType.DMA,
+        pltpu.SemaphoreType.DMA((rows // chunk,)),
+    ]
     if not last:
         scratch.append(pltpu.VMEM((rows * (tile_y + 8), tile_z), F32))
     return pl.pallas_call(
         kernel,
         out_shape=tuple(shapes),
-        in_specs=[pl.BlockSpec(memory_space=pltpu.SMEM)] + [vmem] * (views + 4),
-        out_specs=(vmem,) * len(shapes),
+        in_specs=[pl.BlockSpec(memory_space=pltpu.SMEM)] + [vmem] * views + [where] + [vmem] * 3,
+        out_specs=(where, vmem)[: len(shapes)],
         scratch_shapes=scratch,
         compiler_params=pltpu.CompilerParams(vmem_limit_bytes=24 << 20),
         name="update",

time: 153 us -> 153 us (level)
  no operation moved by 1% of the time
where the time goes in v7:
time: 153 us
  waiting for transfers between devices  61 us (40%)
  starting transfers between devices  37.1 us (24%)
  Pallas kernels  25 us (16%)
  other arithmetic  20.6 us (13%)
  local copies, waits for them, and re-layouts  7.68 us (5%)
    ppermute x30, waiting for transfers between devices, flip(): return lax.ppermute(x, 'brick', [(i, i ^ bit) for i in range(count)])  36.2 us
    ppermute x9, waiting for transfers between devices, pair_views(): return lax.ppermute(x, 'view', [(i, i ^ bit) for i in range(count)])  24.9 us
    ppermute x30, starting transfers between devices, flip(): return lax.ppermute(x, 'brick', [(i, i ^ bit) for i in range(count)])  23.8 us
    ppermute x9, starting transfers between devices, pair_views(): return lax.ppermute(x, 'view', [(i, i ^ bit) for i in range(count)])  13.2 us
    pallas_call x2, Pallas kernels, update(): pl.pallas_call(kernel, out_shape=tuple(shapes), in_specs=[pl.BlockSpec(me...  13.1 us
    pallas_call x2, Pallas kernels, read_tile(): pl.pallas_call(kernel, out_shape=tuple(shapes), in_specs=[pl.BlockSpec(me...  9.03 us
    reduce_sum x4, other arithmetic, band(): return jnp.sum(jnp.where(hit, taps, 0.0), axis=-1)  3.78 us
    unnamed x35, local copies, waits for them, and re-layouts  3.33 us
  transfers between devices with their start and end apart: 39, of which 19 were waited for; matrix products, arithmetic and copies ran while one was open for 13% of the time, Pallas kernels for 1%

profile of v7, /device:TPU:0, one launch (start us, length us, event | category | flops | bytes accessed | tf_op | source)
XLA Modules:
  0.0 152.6 jit_solution(8396660788585739444)
XLA Ops:
  6.8 3.1 %collective-permute-start.3 = (bf16[33,32,128]{2,1,0:T(8,128)(2,1)S(1)}, bf16[33,32,128]{2,1,0:T(8,128)(2,1)S(1)}, u32[]{:S(2)}, u32[]{:S(2)}) collective-permute-start(bf16[33,32,128]{2,1,0:T(8,128)(2,1)S(1)} %first_crop.1.refs_1_), channel_id=1, source_target_pairs={{0,4},{1,5},{2,6},{3,7},{4,0},{5,1},{6,2},{7,3},{8,12},{9,13},{10,... | collective-permute-start | bytes 811016 | tf_op jit(solution)/shard_map/ppermute | solution.py:336
  14.5 1.8 %collective-permute-done.3.refs_5_ = bf16[33,32,128]{2,1,0:T(8,128)(2,1)S(1)} collective-permute-done((bf16[33,32,128]{2,1,0:T(8,128)(2,1)S(1)}, bf16[33,32,128]{2,1,0:T(8,128)(2,1)S(1)}, u32[]{:S(2)}, u32[]{:S(2)}) %collective-permute-start.3) | collective-permute-done | bytes 270368 | tf_op jit(solution)/shard_map/ppermute | solution.py:336
  21.6 2.9 %collective-permute-done.5.refs_7_ = bf16[16,32,128]{2,1,0:T(8,128)(2,1)S(1)} collective-permute-done((bf16[16,32,128]{2,1,0:T(8,128)(2,1)}, bf16[16,32,128]{2,1,0:T(8,128)(2,1)S(1)}, u32[]{:S(2)}, u32[]{:S(2)}) %collective-permute-start.5) | collective-permute-done | bytes 131104 | tf_op jit(solution)/shard_map/ppermute | solution.py:336
  26.1 4.6 %read_tile.2 = (s16[4,16,32,128]{3,2,1,0:T(8,128)(2,1)S(1)}, f32[4,16,32,128]{3,2,1,0:T(8,128)S(1)}, s16[4,16,32,128]{3,2,1,0:T(8,128)(2,1)S(1)}, f32[4,16,32,12...) custom-call(s32[1]{0:T(128)} %bitcast.2.refs_0_, bf16[33,32,128]{2,1,0:T(8,128)(2,1)S(1)} %first_crop.1.refs_1_, ...), custom_call_target="tpu_custom_call" | custom-call | tf_op jit(solution)/shard_map/read_tile/pallas_call | solution.py:212
  34.2 3.6 %collective-permute-start.17 = (f32[72,128]{1,0:T(8,128)S(1)}, f32[72,128]{1,0:T(8,128)S(1)}, u32[]{:S(2)}, u32[]{:S(2)}) collective-permute-start(f32[72,128]{1,0:T(8,128)S(1)} %fusion.47), channel_id=1, source_target_pairs={{0,24},{8,16},{16,8},{24,0},{1,25},{9,17},{17,9},{25,1},{2,26},{10... | collective-permute-start | bytes 110600 | tf_op jit(solution)/shard_map/ppermute | solution.py:340
  42.8 3.6 %collective-permute-done.11 = s16[2,16,32,128]{3,2,1,0:T(8,128)(2,1)S(1)} collective-permute-done((s16[2,16,32,128]{3,2,1,0:T(8,128)(2,1)S(1)}, s16[2,16,32,128]{3,2,1,0:T(8,128)(2,1)S(1)}, u32[]{:S(2)}, u32[]{:S(2)}) %collective-permute-start.11) | collective-permute-done | bytes 262176 | tf_op jit(solution)/shard_map/ppermute | solution.py:336
  49.3 2.3 %collective-permute-done.12 = s16[1,16,32,128]{3,2,1,0:T(8,128)(2,1)S(1)} collective-permute-done((s16[1,16,32,128]{3,2,1,0:T(8,128)(2,1)S(1)}, s16[1,16,32,128]{3,2,1,0:T(8,128)(2,1)S(1)}, u32[]{:S(2)}, u32[]{:S(2)}) %collective-permute-start.12) | collective-permute-done | bytes 131104 | tf_op jit(solution)/shard_map/ppermute | solution.py:336
  55.2 3.5 %collective-permute-start.20 = (s16[32,32,128]{2,1,0:T(8,128)(2,1)}, s16[32,32,128]{2,1,0:T(8,128)(2,1)}, u32[]{:S(2)}, u32[]{:S(2)}) collective-permute-start(s16[32,32,128]{2,1,0:T(8,128)(2,1)} %pad_add_fusion.refs_1_), channel_id=1, source_target_pairs={{0,24},{8,16},{16,8},{24,0},{1,25},{9,17},{17,9},{25,1},{2,26},{10... | collective-permute-start | bytes 786440 | tf_op jit(solution)/shard_map/ppermute | solution.py:340
  62.1 2.5 %select_reduce_fusion.1 = f32[4,128]{1,0:T(4,128)} fusion(f32[4,31]{1,0:T(4,128)S(1)} %bitcast.90, pred[128,128,31]{1,0,2:T(8,128)(4,1)S(1)} %iota_compare_fusion.2), kind=kLoop, calls=%fused_computation.2 | loop fusion | flops 4062720 | bytes 510448 | tf_op jit(solution)/shard_map/vmap()/reduce_sum | solution.py:491
  64.6 2.4 %select_reduce_fusion = f32[4,256,128]{2,1,0:T(8,128)} fusion(f32[4,31]{1,0:T(4,128)S(1)} %bitcast.91, s32[4,256,128]{2,1,0:T(8,128)S(1)} %subtract_add_fusion), kind=kLoop, calls=%fused_computation | loop fusion | flops 12058624 | bytes 1049072 | tf_op jit(solution)/shard_map/vmap()/reduce_sum | solution.py:34
  67.0 2.2 %copy.31 = f32[4,256,128]{1,2,0:T(8,128)} copy(f32[4,256,128]{2,1,0:T(8,128)} %select_reduce_fusion) | data formatting | bytes 1048576 | tf_op jit(solution)/shard_map/vmap()/reduce_sum | solution.py:34
  72.8 6.4 %collective-permute-done.19.refs_3_ = s16[32,32,128]{2,1,0:T(8,128)(2,1)} collective-permute-done((s16[32,32,128]{2,1,0:T(8,128)(2,1)}, s16[32,32,128]{2,1,0:T(8,128)(2,1)}, u32[]{:S(2)}, u32[]{:S(2)}) %collective-permute-start.19) | collective-permute-done | bytes 262176 | tf_op jit(solution)/shard_map/ppermute | solution.py:340
  79.2 7.1 %update.2 = (f32[32,64,256]{2,1,0:T(8,128)S(1)}, bf16[32,32,128]{2,1,0:T(8,128)(2,1)S(1)}) custom-call(s32[3]{0:T(128)S(1)} %copy-done.11, s16[32,32,128]{2,1,0:T(8,128)(2,1)} %pad_add_fusion.refs_1_, s16[32,32,128]{2,1,0:T(8,128)(2,1)} %collective-permute-done.18.refs_2_, s16[32,32,128]{2,1,0:T(8,128)(2,1)} %collective-permute-done.19.refs_3_, ...), custom_call_target="tpu_custom_call" | custom-call | tf_op jit(solution)/shard_map/update/pallas_call | solution.py:324
  86.7 1.8 %collective-permute-start.22 = (bf16[32,32,128]{2,1,0:T(8,128)(2,1)S(1)}, bf16[32,32,128]{2,1,0:T(8,128)(2,1)S(1)}, u32[]{:S(2)}, u32[]{:S(2)}) collective-permute-start(bf16[32,32,128]{2,1,0:T(8,128)(2,1)S(1)} %get-tuple-element.40.refs_1_), channel_id=1, source_target_pairs={{0,2},{1,3},{2,0},{3,1},{4,6},{5,7},{6,4},{7,5},{8,10},{9,11},{10,... | collective-permute-start | bytes 786440 | tf_op jit(solution)/shard_map/ppermute | solution.py:336
  88.5 5.2 %collective-permute-done.24.refs_5_ = bf16[32,32,128]{2,1,0:T(8,128)(2,1)S(1)} collective-permute-done((bf16[32,32,128]{2,1,0:T(8,128)(2,1)S(1)}, bf16[32,32,128]{2,1,0:T(8,128)(2,1)S(1)}, u32[]{:S(2)}, u32[]{:S(2)}) %collective-permute-start.24) | collective-permute-done | bytes 262176 | tf_op jit(solution)/shard_map/ppermute | solution.py:336
  96.6 2.2 %collective-permute-done.27.refs_8_ = bf16[16,32,128]{2,1,0:T(8,128)(2,1)S(1)} collective-permute-done((bf16[16,32,128]{2,1,0:T(8,128)(2,1)S(1)}, bf16[16,32,128]{2,1,0:T(8,128)(2,1)S(1)}, u32[]{:S(2)}, u32[]{:S(2)}) %collective-permute-start.27) | collective-permute-done | bytes 131104 | tf_op jit(solution)/shard_map/ppermute | solution.py:336
  101.9 4.4 %read_tile.3 = (s16[4,16,32,128]{3,2,1,0:T(8,128)(2,1)S(1)}, f32[4,16,32,128]{3,2,1,0:T(8,128)S(1)}, s16[4,16,32,128]{3,2,1,0:T(8,128)(2,1)S(1)}, f32[4,16,32,128]{3,2,1,0:T(8,128)S(1)}) custom-call(s32[1]{0:T(128)} %bitcast.2.refs_0_, bf16[32,32,128]{2,1,0:T(8,128)(2,1)S(1)} %get-tuple-element.40.refs_1_, ...), custom_call_target="tpu_custom_call" | custom-call | tf_op jit(solution)/shard_map/read_tile/pallas_call | solution.py:212
  110.9 6.1 %collective-permute-done.31 = s16[2,16,32,128]{3,2,1,0:T(8,128)(2,1)S(1)} collective-permute-done((s16[2,16,32,128]{3,2,1,0:T(8,128)(2,1)S(1)}, s16[2,16,32,128]{3,2,1,0:T(8,128)(2,1)S(1)}, u32[]{:S(2)}, u32[]{:S(2)}) %collective-permute-start.31) | collective-permute-done | bytes 262176 | tf_op jit(solution)/shard_map/ppermute | solution.py:336
  119.3 2.9 %collective-permute-done.32 = s16[1,16,32,128]{3,2,1,0:T(8,128)(2,1)S(1)} collective-permute-done((s16[1,16,32,128]{3,2,1,0:T(8,128)(2,1)S(1)}, s16[1,16,32,128]{3,2,1,0:T(8,128)(2,1)S(1)}, u32[]{:S(2)}, u32[]{:S(2)}) %collective-permute-start.32) | collective-permute-done | bytes 131104 | tf_op jit(solution)/shard_map/ppermute | solution.py:336
  124.0 2.5 %collective-permute-start.38 = (s16[32,32,128]{2,1,0:T(8,128)(2,1)S(1)}, s16[32,32,128]{2,1,0:T(8,128)(2,1)S(1)}, u32[]{:S(2)}, u32[]{:S(2)}) collective-permute-start(s16[32,32,128]{2,1,0:T(8,128)(2,1)S(1)} %pad_add_fusion.1.refs_1_), channel_id=1, source_target_pairs={{0,24},{8,16},{16,8},{24,0},{1,25},{9,17},{17,9},{25,1},{2,26},{10... | collective-permute-start | bytes 786440 | tf_op jit(solution)/shard_map/ppermute | solution.py:340
  126.5 1.9 %collective-permute-start.36 = (s16[32,32,128]{2,1,0:T(8,128)(2,1)S(1)}, s16[32,32,128]{2,1,0:T(8,128)(2,1)S(1)}, u32[]{:S(2)}, u32[]{:S(2)}) collective-permute-start(s16[32,32,128]{2,1,0:T(8,128)(2,1)S(1)} %pad_add_fusion.1.refs_1_), channel_id=1, source_target_pairs={{0,8},{8,0},{16,24},{24,16},{1,9},{9,1},{17,25},{25,17},{2,10},{10... | collective-permute-start | bytes 786440 | tf_op jit(solution)/shard_map/ppermute | solution.py:340
  129.3 5.9 %collective-permute-done.38.refs_4_ = s16[32,32,128]{2,1,0:T(8,128)(2,1)S(1)} collective-permute-done((s16[32,32,128]{2,1,0:T(8,128)(2,1)S(1)}, s16[32,32,128]{2,1,0:T(8,128)(2,1)S(1)}, u32[]{:S(2)}, u32[]{:S(2)}) %collective-permute-start.38) | collective-permute-done | bytes 262176 | tf_op jit(solution)/shard_map/ppermute | solution.py:340
  135.2 11.3 %collective-permute-done.37.refs_3_ = s16[32,32,128]{2,1,0:T(8,128)(2,1)S(1)} collective-permute-done((s16[32,32,128]{2,1,0:T(8,128)(2,1)S(1)}, s16[32,32,128]{2,1,0:T(8,128)(2,1)S(1)}, u32[]{:S(2)}, u32[]{:S(2)}) %collective-permute-start.37) | collective-permute-done | bytes 262176 | tf_op jit(solution)/shard_map/ppermute | solution.py:340
  146.4 6.0 %update.3 = f32[32,64,256]{2,1,0:T(8,128)} custom-call(s32[3]{0:T(128)S(1)} %copy-done.11, s16[32,32,128]{2,1,0:T(8,128)(2,1)S(1)} %pad_add_fusion.1.refs_1_, s16[32,32,128]{2,1,0:T(8,128)(2,1)S(1)} %collective-permute-done.36.refs_2_, s16[32,32,128]{2,1,0:T(8,128)(2,1)S(1)} %collective-permute-done.37.refs_3_, ...), custom_call_target="tpu_custom_call" | custom-call | tf_op jit(solution)/shard_map/update/pallas_call | solution.py:324
  (199 shorter events, 55.6 us)
Async XLA Ops:
  6.8 9.5 %collective-permute-start.3 = (bf16[33,32,128]{2,1,0:T(8,128)(2,1)S(1)}, bf16[33,32,128]{2,1,0:T(8,128)(2,1)S(1)}, u32[]{:S(2)}, u32[]{:S(2)}) collective-permute-start(bf16[33,32,128]{2,1,0:T(8,128)(2,1)S(1)} %first_crop.1.refs_1_), channel_id=1, source_target_pairs={{0,4},{1,5},{2,6},{3,7},{4,0},{5,1},{6,2},{7,3},{8,12},{9,13},{10,... | collective-permute-start | bytes 811016 | tf_op jit(solution)/shard_map/ppermute | solution.py:336
  9.8 8.9 %collective-permute-start.1 = (bf16[33,32,128]{2,1,0:T(8,128)(2,1)S(1)}, bf16[33,32,128]{2,1,0:T(8,128)(2,1)S(1)}, u32[]{:S(2)}, u32[]{:S(2)}) collective-permute-start(bf16[33,32,128]{2,1,0:T(8,128)(2,1)S(1)} %first_crop.1.refs_1_), channel_id=1, source_target_pairs={{0,2},{1,3},{2,0},{3,1},{4,6},{5,7},{6,4},{7,5},{8,10},{9,11},{10,... | collective-permute-start | bytes 811016 | tf_op jit(solution)/shard_map/ppermute | solution.py:336
  11.3 14.7 %collective-permute-start = (bf16[33,32,128]{2,1,0:T(8,128)(2,1)S(1)}, bf16[33,32,128]{2,1,0:T(8,128)(2,1)S(1)}, u32[]{:S(2)}, u32[]{:S(2)}) collective-permute-start(bf16[33,32,128]{2,1,0:T(8,128)(2,1)S(1)} %first_crop.1.refs_1_), channel_id=1, source_target_pairs={{0,1},{1,0},{2,3},{3,2},{4,5},{5,4},{6,7},{7,6},{8,9},{9,8},{10,11... | collective-permute-start | bytes 811016 | tf_op jit(solution)/shard_map/ppermute | solution.py:336
  17.0 7.6 %collective-permute-start.6 = (bf16[17,32,128]{2,1,0:T(8,128)(2,1)}, bf16[17,32,128]{2,1,0:T(8,128)(2,1)S(1)}, u32[]{:S(2)}, u32[]{:S(2)}) collective-permute-start(bf16[17,32,128]{2,1,0:T(8,128)(2,1)} %slice.132), channel_id=1, source_target_pairs={{0,2},{1,3},{2,0},{3,1},{4,6},{5,7},{6,4},{7,5},{8,10},{9,11},{10,... | collective-permute-start | bytes 417800 | tf_op jit(solution)/shard_map/ppermute | solution.py:336
  19.4 5.2 %collective-permute-start.5 = (bf16[16,32,128]{2,1,0:T(8,128)(2,1)}, bf16[16,32,128]{2,1,0:T(8,128)(2,1)S(1)}, u32[]{:S(2)}, u32[]{:S(2)}) collective-permute-start(bf16[16,32,128]{2,1,0:T(8,128)(2,1)} %slice.131), channel_id=1, source_target_pairs={{0,4},{1,5},{2,6},{3,7},{4,0},{5,1},{6,2},{7,3},{8,12},{9,13},{10,... | collective-permute-start | bytes 393224 | tf_op jit(solution)/shard_map/ppermute | solution.py:336
  21.0 5.0 %collective-permute-start.4 = (bf16[33,32,128]{2,1,0:T(8,128)(2,1)S(1)}, bf16[33,32,128]{2,1,0:T(8,128)(2,1)S(1)}, u32[]{:S(2)}, u32[]{:S(2)}) collective-permute-start(bf16[33,32,128]{2,1,0:T(8,128)(2,1)S(1)} %collective-permute-done.3.refs_5_), channel_id=1, source_target_pairs={{0,1},{1,0},{2,3},{3,2},{4,5},{5,4},{6,7},{7,6},{8,9},{9,8},{10,11... | collective-permute-start | bytes 811016 | tf_op jit(solution)/shard_map/ppermute | solution.py:336
  34.2 7.1 %collective-permute-start.17 = (f32[72,128]{1,0:T(8,128)S(1)}, f32[72,128]{1,0:T(8,128)S(1)}, u32[]{:S(2)}, u32[]{:S(2)}) collective-permute-start(f32[72,128]{1,0:T(8,128)S(1)} %fusion.47), channel_id=1, source_target_pairs={{0,24},{8,16},{16,8},{24,0},{1,25},{9,17},{17,9},{25,1},{2,26},{10... | collective-permute-start | bytes 110600 | tf_op jit(solution)/shard_map/ppermute | solution.py:340
  38.7 7.8 %collective-permute-start.11 = (s16[2,16,32,128]{3,2,1,0:T(8,128)(2,1)S(1)}, s16[2,16,32,128]{3,2,1,0:T(8,128)(2,1)S(1)}, u32[]{:S(2)}, u32[]{:S(2)}) collective-permute-start(s16[2,16,32,128]{3,2,1,0:T(8,128)(2,1)S(1)} %get-tuple-element.32), channel_id=1, source_target_pairs={{0,2},{1,3},{2,0},{3,1},{4,6},{5,7},{6,4},{7,5},{8,10},{9,11},{10,... | collective-permute-start | bytes 786440 | tf_op jit(solution)/shard_map/ppermute | solution.py:336
  39.9 8.3 %collective-permute-start.13 = (s16[2,16,32,128]{3,2,1,0:T(8,128)(2,1)S(1)}, s16[2,16,32,128]{3,2,1,0:T(8,128)(2,1)S(1)}, u32[]{:S(2)}, u32[]{:S(2)}) collective-permute-start(s16[2,16,32,128]{3,2,1,0:T(8,128)(2,1)S(1)} %get-tuple-element.34), channel_id=1, source_target_pairs={{0,4},{1,5},{2,6},{3,7},{4,0},{5,1},{6,2},{7,3},{8,12},{9,13},{10,... | collective-permute-start | bytes 786440 | tf_op jit(solution)/shard_map/ppermute | solution.py:336
  46.6 5.0 %collective-permute-start.12 = (s16[1,16,32,128]{3,2,1,0:T(8,128)(2,1)S(1)}, s16[1,16,32,128]{3,2,1,0:T(8,128)(2,1)S(1)}, u32[]{:S(2)}, u32[]{:S(2)}) collective-permute-start(s16[1,16,32,128]{3,2,1,0:T(8,128)(2,1)S(1)} %fusion.26), channel_id=1, source_target_pairs={{0,4},{1,5},{2,6},{3,7},{4,0},{5,1},{6,2},{7,3},{8,12},{9,13},{10,... | collective-permute-start | bytes 393224 | tf_op jit(solution)/shard_map/ppermute | solution.py:336
  55.2 17.6 %collective-permute-start.20 = (s16[32,32,128]{2,1,0:T(8,128)(2,1)}, s16[32,32,128]{2,1,0:T(8,128)(2,1)}, u32[]{:S(2)}, u32[]{:S(2)}) collective-permute-start(s16[32,32,128]{2,1,0:T(8,128)(2,1)} %pad_add_fusion.refs_1_), channel_id=1, source_target_pairs={{0,24},{8,16},{16,8},{24,0},{1,25},{9,17},{17,9},{25,1},{2,26},{10... | collective-permute-start | bytes 786440 | tf_op jit(solution)/shard_map/ppermute | solution.py:340
  58.7 20.5 %collective-permute-start.19 = (s16[32,32,128]{2,1,0:T(8,128)(2,1)}, s16[32,32,128]{2,1,0:T(8,128)(2,1)}, u32[]{:S(2)}, u32[]{:S(2)}) collective-permute-start(s16[32,32,128]{2,1,0:T(8,128)(2,1)} %pad_add_fusion.refs_1_), channel_id=1, source_target_pairs={{0,16},{8,24},{16,0},{24,8},{1,17},{9,25},{17,1},{25,9},{2,18},{10... | collective-permute-start | bytes 786440 | tf_op jit(solution)/shard_map/ppermute | solution.py:340
  58.7 20.5 %collective-permute-start.18 = (s16[32,32,128]{2,1,0:T(8,128)(2,1)}, s16[32,32,128]{2,1,0:T(8,128)(2,1)}, u32[]{:S(2)}, u32[]{:S(2)}) collective-permute-start(s16[32,32,128]{2,1,0:T(8,128)(2,1)} %pad_add_fusion.refs_1_), channel_id=1, source_target_pairs={{0,8},{8,0},{16,24},{24,16},{1,9},{9,1},{17,25},{25,17},{2,10},{10... | collective-permute-start | bytes 786440 | tf_op jit(solution)/shard_map/ppermute | solution.py:340
  86.3 7.4 %collective-permute-start.24 = (bf16[32,32,128]{2,1,0:T(8,128)(2,1)S(1)}, bf16[32,32,128]{2,1,0:T(8,128)(2,1)S(1)}, u32[]{:S(2)}, u32[]{:S(2)}) collective-permute-start(bf16[32,32,128]{2,1,0:T(8,128)(2,1)S(1)} %get-tuple-element.40.refs_1_), channel_id=1, source_target_pairs={{0,4},{1,5},{2,6},{3,7},{4,0},{5,1},{6,2},{7,3},{8,12},{9,13},{10,... | collective-permute-start | bytes 786440 | tf_op jit(solution)/shard_map/ppermute | solution.py:336
  86.7 7.8 %collective-permute-start.22 = (bf16[32,32,128]{2,1,0:T(8,128)(2,1)S(1)}, bf16[32,32,128]{2,1,0:T(8,128)(2,1)S(1)}, u32[]{:S(2)}, u32[]{:S(2)}) collective-permute-start(bf16[32,32,128]{2,1,0:T(8,128)(2,1)S(1)} %get-tuple-element.40.refs_1_), channel_id=1, source_target_pairs={{0,2},{1,3},{2,0},{3,1},{4,6},{5,7},{6,4},{7,5},{8,10},{9,11},{10,... | collective-permute-start | bytes 786440 | tf_op jit(solution)/shard_map/ppermute | solution.py:336
  88.5 12.0 %collective-permute-start.21 = (bf16[32,32,128]{2,1,0:T(8,128)(2,1)S(1)}, bf16[32,32,128]{2,1,0:T(8,128)(2,1)S(1)}, u32[]{:S(2)}, u32[]{:S(2)}) collective-permute-start(bf16[32,32,128]{2,1,0:T(8,128)(2,1)S(1)} %get-tuple-element.40.refs_1_), channel_id=1, source_target_pairs={{0,1},{1,0},{2,3},{3,2},{4,5},{5,4},{6,7},{7,6},{8,9},{9,8},{10,11... | collective-permute-start | bytes 786440 | tf_op jit(solution)/shard_map/ppermute | solution.py:336
  94.5 6.1 %collective-permute-start.25 = (bf16[32,32,128]{2,1,0:T(8,128)(2,1)S(1)}, bf16[32,32,128]{2,1,0:T(8,128)(2,1)S(1)}, u32[]{:S(2)}, u32[]{:S(2)}) collective-permute-start(bf16[32,32,128]{2,1,0:T(8,128)(2,1)S(1)} %collective-permute-done.24.refs_5_), channel_id=1, source_target_pairs={{0,1},{1,0},{2,3},{3,2},{4,5},{5,4},{6,7},{7,6},{8,9},{9,8},{10,11... | collective-permute-start | bytes 786440 | tf_op jit(solution)/shard_map/ppermute | solution.py:336
  94.5 6.1 %collective-permute-start.23 = (bf16[32,32,128]{2,1,0:T(8,128)(2,1)S(1)}, bf16[32,32,128]{2,1,0:T(8,128)(2,1)S(1)}, u32[]{:S(2)}, u32[]{:S(2)}) collective-permute-start(bf16[32,32,128]{2,1,0:T(8,128)(2,1)S(1)} %collective-permute-done.22.refs_3_), channel_id=1, source_target_pairs={{0,1},{1,0},{2,3},{3,2},{4,5},{5,4},{6,7},{7,6},{8,9},{9,8},{10,11... | collective-permute-start | bytes 786440 | tf_op jit(solution)/shard_map/ppermute | solution.py:336
  95.1 5.5 %collective-permute-start.26 = (bf16[16,32,128]{2,1,0:T(8,128)(2,1)S(1)}, bf16[16,32,128]{2,1,0:T(8,128)(2,1)S(1)}, u32[]{:S(2)}, u32[]{:S(2)}) collective-permute-start(bf16[16,32,128]{2,1,0:T(8,128)(2,1)S(1)} %slice.141), channel_id=1, source_target_pairs={{0,4},{1,5},{2,6},{3,7},{4,0},{5,1},{6,2},{7,3},{8,12},{9,13},{10,... | collective-permute-start | bytes 393224 | tf_op jit(solution)/shard_map/ppermute | solution.py:336
  108.6 8.4 %collective-permute-start.31 = (s16[2,16,32,128]{3,2,1,0:T(8,128)(2,1)S(1)}, s16[2,16,32,128]{3,2,1,0:T(8,128)(2,1)S(1)}, u32[]{:S(2)}, u32[]{:S(2)}) collective-permute-start(s16[2,16,32,128]{3,2,1,0:T(8,128)(2,1)S(1)} %fusion.5), channel_id=1, source_target_pairs={{0,2},{1,3},{2,0},{3,1},{4,6},{5,7},{6,4},{7,5},{8,10},{9,11},{10,... | collective-permute-start | bytes 786440 | tf_op jit(solution)/shard_map/ppermute | solution.py:336
  110.3 8.4 %collective-permute-start.34 = (s16[2,16,32,128]{3,2,1,0:T(8,128)(2,1)S(1)}, s16[2,16,32,128]{3,2,1,0:T(8,128)(2,1)S(1)}, u32[]{:S(2)}, u32[]{:S(2)}) collective-permute-start(s16[2,16,32,128]{3,2,1,0:T(8,128)(2,1)S(1)} %fusion.3), channel_id=1, source_target_pairs={{0,4},{1,5},{2,6},{3,7},{4,0},{5,1},{6,2},{7,3},{8,12},{9,13},{10,... | collective-permute-start | bytes 786440 | tf_op jit(solution)/shard_map/ppermute | solution.py:336
  124.0 11.1 %collective-permute-start.38 = (s16[32,32,128]{2,1,0:T(8,128)(2,1)S(1)}, s16[32,32,128]{2,1,0:T(8,128)(2,1)S(1)}, u32[]{:S(2)}, u32[]{:S(2)}) collective-permute-start(s16[32,32,128]{2,1,0:T(8,128)(2,1)S(1)} %pad_add_fusion.1.refs_1_), channel_id=1, source_target_pairs={{0,24},{8,16},{16,8},{24,0},{1,25},{9,17},{17,9},{25,1},{2,26},{10... | collective-permute-start | bytes 786440 | tf_op jit(solution)/shard_map/ppermute | solution.py:340
  126.5 19.9 %collective-permute-start.37 = (s16[32,32,128]{2,1,0:T(8,128)(2,1)S(1)}, s16[32,32,128]{2,1,0:T(8,128)(2,1)S(1)}, u32[]{:S(2)}, u32[]{:S(2)}) collective-permute-start(s16[32,32,128]{2,1,0:T(8,128)(2,1)S(1)} %pad_add_fusion.1.refs_1_), channel_id=1, source_target_pairs={{0,16},{8,24},{16,0},{24,8},{1,17},{9,25},{17,1},{25,9},{2,18},{10... | collective-permute-start | bytes 786440 | tf_op jit(solution)/shard_map/ppermute | solution.py:340
  126.5 19.9 %collective-permute-start.36 = (s16[32,32,128]{2,1,0:T(8,128)(2,1)S(1)}, s16[32,32,128]{2,1,0:T(8,128)(2,1)S(1)}, u32[]{:S(2)}, u32[]{:S(2)}) collective-permute-start(s16[32,32,128]{2,1,0:T(8,128)(2,1)S(1)} %pad_add_fusion.1.refs_1_), channel_id=1, source_target_pairs={{0,8},{8,0},{16,24},{24,16},{1,9},{9,1},{17,25},{25,17},{2,10},{10... | collective-permute-start | bytes 786440 | tf_op jit(solution)/shard_map/ppermute | solution.py:340
  (32 other events, 237.8 us)
